TPU v7x, 32 devices: a whole 2x2x4 slice. The times are simulated.
32 devices in a mesh: wide: 8 (over z, y), narrow: 4 (over x, core).
Axes of the slice: x: 2, y: 2, z: 4, core: 2. Of those that a mesh axis runs over, the one named last changes fastest.
Arguments:
- layer_inputs_matrix: bfloat16 [32768, 768], P(('wide', 'narrow')), may hold values from -6 to 6
- assignment_indices: int32 [32768, 1], P(('wide', 'narrow')), may hold values from 0 to 7
- admitted_counts_matrix: int32 [8], replicated, may hold values from 24 to 48, as said below
- mixer_scaling1_factor: bfloat16 [768], P(('wide', 'narrow')), may hold values from 0.5 to 1.5
- triple_linear_matrix: bfloat16 [768, 2304], P(('wide', 'narrow')), may hold values from -0.21875 to 0.21875
- mixer_exit_matrix: bfloat16 [768, 768], P(('wide', 'narrow')), may hold values from -0.875 to 0.875
- specialist_scaling2_factor: bfloat16 [768], P(('wide', 'narrow')), may hold values from 0.5 to 1.5
- cluster_mean_columns: bfloat16 [768, 8], P(('wide', 'narrow')), may hold values from -0.21875 to 0.21875
- first_linear_matrix: bfloat16 [8, 768, 3072], P('wide', None, 'narrow'), may hold values from -0.21875 to 0.21875
- second_linear_matrix: bfloat16 [8, 768, 3072], P('wide', None, 'narrow'), may hold values from -0.109375 to 0.109375
- incoming_gradient: bfloat16 [32768, 768], P(('wide', 'narrow')), may hold values from -6 to 6
Outputs:
- mixed: bfloat16 [32768, 768], P(('wide', 'narrow'))
- tokens_grad: float32 [32768, 768], P(('wide', 'narrow'))
- norm1_gain_grad: float32 [768], P(('wide', 'narrow'))
- qkv_grad: float32 [768, 2304], P(('wide', 'narrow'))
- out_grad: float32 [768, 768], P(('wide', 'narrow'))
- norm2_gain_grad: float32 [768], P(('wide', 'narrow'))
- centroid_grad: float32 [768, 8], P(('wide', 'narrow'))
- up_grad: float32 [8, 768, 3072], P('wide', None, 'narrow')
- down_grad: float32 [8, 768, 3072], P('wide', None, 'narrow')
Inputs may be any that keep to these rules, and one draw needn't show every extreme that they name: `admitted_counts_matrix`: so a device sends at most 48 tokens to one expert.
All inputs are finite; a program needn't handle non-finite values.
Results may differ from a plain program's by a relative error of at most 0.014.
Values may be sent and summed in bfloat16 or wider, within the bound.
A program may use at most 320 MiB of HBM per device.

v0:
```python
import jax
import jax.numpy as jnp
from jax import lax
from jax.sharding import PartitionSpec as P

HD = 64
SEQ = 1024
SLOT = 48


precise = lax.Precision.HIGHEST
over_rows = (((0,), (0,)), ((), ()))
over_cols = (((1,), (1,)), ((), ()))


def layer_norm(tensor, gain_vec):
    centered = tensor - jnp.mean(tensor, -1, keepdims=True)
    spread = jnp.mean(centered * centered, -1, keepdims=True)
    return centered * lax.rsqrt(spread + 1e-05) * gain_vec


def gelu_exact(tensor):
    return jax.nn.gelu(tensor, approximate=False)


def split_heads(packed):
    seq_len = packed.shape[0]
    model_width = packed.shape[1] // 3
    head_count = model_width // HD
    queries = packed[:, :model_width].reshape(seq_len, head_count, HD)
    key_rows = packed[:, model_width : 2 * model_width].reshape(seq_len, head_count, HD)
    value_rows = packed[:, 2 * model_width :].reshape(seq_len, head_count, HD)
    raw_scores = jnp.einsum(
        "qhd,khd->hqk", queries, key_rows, preferred_element_type=jnp.float32
    ) * HD ** (-0.5)
    places = jnp.arange(seq_len)
    causal = places[:, None] >= places[None, :]
    masked = jnp.where(causal[None], raw_scores, -1e30)
    return (queries, key_rows, value_rows, masked)


def attend_forward(packed):
    queries, key_rows, value_rows, masked = split_heads(packed)
    maxima = jnp.max(masked, -1, keepdims=True)
    powers = jnp.exp(masked - maxima)
    totals = jnp.sum(powers, -1, keepdims=True)
    attn_probs = (powers / totals).astype(jnp.bfloat16)
    attended = jnp.einsum(
        "hqk,khd->qhd", attn_probs, value_rows, preferred_element_type=jnp.float32
    )
    return (attended.reshape(packed.shape[0], -1).astype(jnp.bfloat16), maxima + jnp.log(totals))


def attend_backward(member):
    packed, upstream, log_totals = member
    queries, key_rows, value_rows, masked = split_heads(packed)
    attn_probs = jnp.exp(masked - log_totals)
    probs_low = attn_probs.astype(jnp.bfloat16)
    grad_out = upstream.reshape(queries.shape)
    grad_probs = jnp.einsum(
        "qhd,khd->hqk", grad_out, value_rows, preferred_element_type=jnp.float32
    )
    grad_values = jnp.einsum(
        "hqk,qhd->khd", probs_low, grad_out, preferred_element_type=jnp.float32
    )
    grad_scores = (
        attn_probs * (grad_probs - jnp.sum(grad_probs * attn_probs, -1, keepdims=True))
    ).astype(jnp.bfloat16)
    factor = HD ** (-0.5)
    grad_queries = (
        jnp.einsum("hqk,khd->qhd", grad_scores, key_rows, preferred_element_type=jnp.float32)
        * factor
    )
    grad_keys = (
        jnp.einsum("hqk,qhd->khd", grad_scores, queries, preferred_element_type=jnp.float32)
        * factor
    )
    seq_len = packed.shape[0]
    joined = jnp.concatenate(
        [
            grad_queries.reshape(seq_len, -1),
            grad_keys.reshape(seq_len, -1),
            grad_values.reshape(seq_len, -1),
        ],
        1,
    )
    return joined.astype(jnp.bfloat16)


def expert_rows(row_block, up_mat, down_mat):
    pre_act = jnp.dot(row_block, up_mat, preferred_element_type=jnp.float32)
    hidden = gelu_exact(pre_act).astype(jnp.bfloat16)
    return lax.dot_general(hidden, down_mat, over_cols, preferred_element_type=jnp.float32)


def expert_grads(row_block, grad_block, up_mat, down_mat):
    pre_act = jnp.dot(row_block, up_mat, preferred_element_type=jnp.float32)
    hidden, gelu_back = jax.vjp(gelu_exact, pre_act)
    hidden_low = hidden.astype(jnp.bfloat16)
    down_part = lax.dot_general(
        grad_block, hidden_low, over_rows, preferred_element_type=jnp.float32
    )
    grad_hidden = jnp.dot(grad_block, down_mat, preferred_element_type=jnp.float32)
    grad_pre = gelu_back(grad_hidden)[0].astype(jnp.bfloat16)
    up_part = lax.dot_general(row_block, grad_pre, over_rows, preferred_element_type=jnp.float32)
    return (grad_pre, up_part, down_part)


def fill_slots(row_vals, target, slot_count):
    buffer = jnp.zeros((slot_count + 1, row_vals.shape[1]), row_vals.dtype).at[target].set(row_vals)
    return buffer[:slot_count]


def read_slots(buffer, target):
    padded = jnp.concatenate([buffer, jnp.zeros((1, buffer.shape[1]), buffer.dtype)], 0)
    return padded[target]


def shards(
    layer_inputs_matrix,
    assignment_indices,
    admitted_counts_matrix,
    mixer_scaling1_factor,
    triple_linear_matrix,
    mixer_exit_matrix,
    specialist_scaling2_factor,
    cluster_mean_columns,
    first_linear_matrix,
    second_linear_matrix,
    incoming_gradient,
):
    gain_one, qkv_mat, out_mat, gain_two, centers = (
        lax.all_gather(mixer_scaling1_factor, ("wide", "narrow"), axis=0, tiled=True),
        lax.all_gather(triple_linear_matrix, ("wide", "narrow"), axis=0, tiled=True),
        lax.all_gather(mixer_exit_matrix, ("wide", "narrow"), axis=0, tiled=True),
        lax.all_gather(specialist_scaling2_factor, ("wide", "narrow"), axis=0, tiled=True),
        lax.all_gather(cluster_mean_columns, ("wide", "narrow"), axis=0, tiled=True),
    )
    gain_one = gain_one.astype(jnp.float32)
    gain_two = gain_two.astype(jnp.float32)
    centers = centers.astype(jnp.float32)
    token_rows = layer_inputs_matrix.astype(jnp.float32)
    tok_count, model_width = layer_inputs_matrix.shape
    seq_count = tok_count // SEQ
    normed, norm1_back = jax.vjp(layer_norm, token_rows, gain_one)
    normed_low = normed.astype(jnp.bfloat16)
    qkv_rows = jnp.dot(normed_low, qkv_mat, preferred_element_type=jnp.float32).astype(jnp.bfloat16)
    packed_seqs = qkv_rows.reshape(seq_count, SEQ, 3 * model_width)
    attended, log_totals = lax.map(attend_forward, packed_seqs)
    attended = attended.reshape(tok_count, model_width)
    residual = token_rows + jnp.dot(attended, out_mat, preferred_element_type=jnp.float32)
    normed_two, norm2_back = jax.vjp(layer_norm, residual, gain_two)
    sent_rows = normed_two.astype(jnp.bfloat16)
    dispatched_items = assignment_indices[:, 0]
    specialist_overall_sum = admitted_counts_matrix.shape[0]
    slot_count = specialist_overall_sum * SLOT
    specialist_indicator = (
        dispatched_items[:, None] == jnp.arange(specialist_overall_sum, dtype=jnp.int32)[None, :]
    ).astype(jnp.int32)
    before = jnp.cumsum(specialist_indicator, 0) - specialist_indicator
    ranked = jnp.sum(before * specialist_indicator, 1)
    position_ceilings = jnp.sum(specialist_indicator * admitted_counts_matrix[None, :], 1)
    retained_couple_filter = ranked < position_ceilings
    target = jnp.where(retained_couple_filter, dispatched_items * SLOT + ranked, slot_count)
    kept_rows = retained_couple_filter.astype(jnp.float32)
    choose = specialist_indicator.astype(jnp.float32)
    send_buf = fill_slots(sent_rows, target, slot_count).reshape(
        specialist_overall_sum, SLOT, model_width
    )
    local_rows = lax.all_to_all(send_buf, "wide", split_axis=0, concat_axis=0, tiled=True).reshape(
        slot_count, model_width
    )
    gathered = lax.all_gather(local_rows, "narrow", axis=0, tiled=True)
    expert_local = lax.psum_scatter(
        expert_rows(gathered, first_linear_matrix[0], second_linear_matrix[0]).astype(jnp.bfloat16),
        "narrow",
        scatter_dimension=0,
        tiled=True,
    )
    returned = lax.all_to_all(
        expert_local.reshape(specialist_overall_sum, SLOT, model_width),
        "wide",
        split_axis=0,
        concat_axis=0,
        tiled=True,
    )
    expert_tok = read_slots(returned.reshape(slot_count, model_width), target).astype(jnp.float32)
    center_rows = lax.dot_general(choose, centers, over_cols, precision=precise)
    logits = jnp.sum(normed_two * center_rows, 1)
    sigma = jax.nn.sigmoid(logits)
    gating = sigma * kept_rows
    mixed = (residual + gating[:, None] * expert_tok).astype(jnp.bfloat16)
    grad_y = incoming_gradient.astype(jnp.float32)
    grad_logit = jnp.sum(grad_y * expert_tok, 1) * sigma * (1.0 - sigma) * kept_rows
    grad_normed = grad_logit[:, None] * center_rows
    centroid_part = lax.dot_general(
        normed_two, choose * grad_logit[:, None], over_rows, precision=precise
    )
    grad_expert = (grad_y * gating[:, None]).astype(jnp.bfloat16)
    grad_buf = fill_slots(grad_expert, target, slot_count).reshape(
        specialist_overall_sum, SLOT, model_width
    )
    grad_local = lax.all_to_all(grad_buf, "wide", split_axis=0, concat_axis=0, tiled=True).reshape(
        slot_count, model_width
    )
    grad_gathered = lax.all_gather(grad_local, "narrow", axis=0, tiled=True)
    grad_pre, up_part, down_part = expert_grads(
        gathered, grad_gathered, first_linear_matrix[0], second_linear_matrix[0]
    )
    input_back = lax.psum_scatter(
        lax.dot_general(
            grad_pre, first_linear_matrix[0], over_cols, preferred_element_type=jnp.float32
        ).astype(jnp.bfloat16),
        "narrow",
        scatter_dimension=0,
        tiled=True,
    )
    up_grad = up_part[None]
    down_grad = down_part[None]
    back_rows = lax.all_to_all(
        input_back.reshape(specialist_overall_sum, SLOT, model_width),
        "wide",
        split_axis=0,
        concat_axis=0,
        tiled=True,
    )
    grad_normed = grad_normed + read_slots(
        back_rows.reshape(slot_count, model_width), target
    ).astype(jnp.float32)
    grad_resid_norm, gain_two_part = norm2_back(grad_normed)
    grad_resid = grad_y + grad_resid_norm
    grad_branch = grad_resid.astype(jnp.bfloat16)
    out_part = lax.dot_general(attended, grad_branch, over_rows, preferred_element_type=jnp.float32)
    grad_attended = lax.dot_general(
        grad_branch, out_mat, over_cols, preferred_element_type=jnp.float32
    ).astype(jnp.bfloat16)
    grad_packed = lax.map(
        attend_backward,
        (packed_seqs, grad_attended.reshape(seq_count, SEQ, model_width), log_totals),
    )
    grad_packed = grad_packed.reshape(tok_count, 3 * model_width)
    qkv_part = lax.dot_general(
        normed_low, grad_packed, over_rows, preferred_element_type=jnp.float32
    )
    grad_normed_one = lax.dot_general(
        grad_packed, qkv_mat, over_cols, preferred_element_type=jnp.float32
    )
    grad_token_norm, gain_one_part = norm1_back(grad_normed_one)
    tokens_grad = grad_resid + grad_token_norm
    gain_one_grad, qkv_grad, out_grad, gain_two_grad, centroid_grad = (
        lax.psum_scatter(gain_one_part, ("wide", "narrow"), scatter_dimension=0, tiled=True),
        lax.psum_scatter(qkv_part, ("wide", "narrow"), scatter_dimension=0, tiled=True),
        lax.psum_scatter(out_part, ("wide", "narrow"), scatter_dimension=0, tiled=True),
        lax.psum_scatter(gain_two_part, ("wide", "narrow"), scatter_dimension=0, tiled=True),
        lax.psum_scatter(centroid_part, ("wide", "narrow"), scatter_dimension=0, tiled=True),
    )
    return (
        mixed,
        tokens_grad,
        gain_one_grad,
        qkv_grad,
        out_grad,
        gain_two_grad,
        centroid_grad,
        up_grad,
        down_grad,
    )


def solution(mesh):
    in_specs = (
        P(("wide", "narrow"), None),
        P(("wide", "narrow"), None),
        P(),
        P(("wide", "narrow")),
        P(("wide", "narrow"), None),
        P(("wide", "narrow"), None),
        P(("wide", "narrow")),
        P(("wide", "narrow"), None),
        P("wide", None, "narrow"),
        P("wide", None, "narrow"),
        P(("wide", "narrow"), None),
    )
    out_specs = (
        P(("wide", "narrow"), None),
        P(("wide", "narrow"), None),
        P(("wide", "narrow")),
        P(("wide", "narrow"), None),
        P(("wide", "narrow"), None),
        P(("wide", "narrow")),
        P(("wide", "narrow"), None),
        P("wide", None, "narrow"),
        P("wide", None, "narrow"),
    )
    return jax.shard_map(shards, mesh=mesh, in_specs=in_specs, out_specs=out_specs, check_vma=False)
```

profile of v0, /device:TPU:0, one launch (start us, length us, event | category | flops | bytes accessed | tf_op | source)
XLA Modules:
  0.0 762.0 jit_solution(11529941645791292390)
XLA Ops:
  10.8 42.0 %all-reduce.8 = (bf16[768]{0:T(1024)(128)(2,1)S(1)}, bf16[768]{0:T(1024)(128)(2,1)S(1)}) all-reduce(bf16[768]{0:T(1024)(128)(2,1)S(1)} %dynamic-update-slice, bf16[768]{0:T(1024)(128)(2,1)S(1)} %dynamic-update-slice.1), channel_id=1, replica_groups=mesh['wide'=8,'narrow'=4] {'wide','narrow'}, use_global_device_ids=true, to_apply=%add.2 | all-reduce | flops 1536 | bytes 6144
  56.3 40.8 %all-gather = bf16[32,24,8]{1,2,0:T(8,128)(2,1)S(1)} all-gather(bf16[1,24,8]{1,2,0:T(8,128)(2,1)} %bitcast.122), channel_id=1, replica_groups=mesh['wide'=8,'narrow'=4] {'wide','narrow'}, dimensions={0}, use_global_device_ids=true | all-gather | bytes 12672 | tf_op jit(solution)/shard_map/all_gather | solution.py:137
  103.6 6.6 convolution_convert_fusion
  115.1 2.7 copy.54
  120.4 21.5 %fusion.6 = (f32[12,1024]{1,0:T(8,128)S(1)}, f32[12,1024,1024]{1,2,0:T(8,128)}) fusion(pred[1024,1024]{0,1:T(8,128)(4,1)S(1)} %iota_compare_fusion, bf16[1024,12,64]{0,2,1:T(8,128)(2,1)} %bitcast.92, bf16[1024,12,64]{0,2,1:T(8,128)(2,1)} %bitcast.94), kind=kOutput, calls=%fused_computation.15 | convolution fusion | flops 1648349184 | bytes 54575104 | tf_op jit(solution)/shard_map/while/body/eval_jaxpr/qhd,khd->hqk/dot_general | solution.py:33
  141.9 21.0 %fusion = f32[12,1024]{1,0:T(8,128)S(1)} fusion(f32[12,1024]{1,0:T(8,128)S(1)} %get-tuple-element.86, f32[12,1024,1024]{1,2,0:T(8,128)} %get-tuple-element.87, pred[1024,1024]{0,1:T(8,128)(4,1)S(1)} %iota_compare_fusion), kind=kLoop, calls=%fused_computation.10 | loop fusion | flops 50319360 | bytes 51478528 | tf_op jit(solution)/shard_map/while/body/eval_jaxpr/reduce_sum | solution.py:46
  162.9 21.6 %fusion.36 = bf16[12,64,1024]{2,1,0:T(8,128)(2,1)} fusion(bf16[1024,12,64]{0,2,1:T(8,128)(2,1)S(1)} %bitcast.97, f32[12,1024]{1,0:T(8,128)S(1)} %fusion, f32[12,1024]{1,0:T(8,128)S(1)} %get-tuple-element.86, f32[12,1024,1024]{1,2,0:T(8,128)} %get-tuple-element.87, pred[1024,1024]{0,1:T(8,128)(4,1)S(1)} %iota_compare_fusion), kind=kOutput, calls=%fused_computation.80 | convolution fusion | flops 1674313728 | bytes 54624256 | tf_op jit(solution)/shard_map/while/body/eval_jaxpr/hqk,khd->qhd/dot_general | solution.py:48
  184.6 3.8 fusion.75
  188.8 4.8 multiply_reduce_fusion.3
  196.2 5.8 scatter_custom_fusion
  202.0 20.3 %all_to_all.20 = bf16[8,48,768]{2,1,0:T(8,128)(2,1)} all-to-all(bf16[8,48,768]{2,1,0:T(8,128)(2,1)S(1)} %bitcast.104), channel_id=1, replica_groups=mesh['wide'=8,'narrow'=4] {'wide'}, dimensions={0} | all-to-all | bytes 1179648 | tf_op jit(solution)/shard_map/all_to_all | solution.py:170
  222.4 21.7 %all-gather.10.cloned.1.call-done = bf16[1536,768]{1,0:T(8,128)(2,1)} async-done(((bf16[384,768]{1,0:T(8,128)(2,1)}), bf16[1536,768]{1,0:T(8,128)(2,1)}) %all-gather.10.cloned.1.call-update) | async-done | bytes 2359312 | tf_op jit(solution)/shard_map/all_gather | solution.py:173
  244.1 14.5 %multiply_convert_fusion.1 = (bf16[1536,768]{1,0:T(8,128)(2,1)S(1)}, f32[1536,768]{1,0:T(8,128)}, f32[1536,768]{1,0:T(8,128)}) fusion(bf16[1536,768]{1,0:T(8,128)(2,1)} %all-gather.10.cloned.1.call-done, bf16[1,768,768]{2,1,0:T(8,128)(2,1)S(1)} %copy-done), kind=kOutput, calls=%fused_computation.33 | convolution fusion | flops 1888616448 | bytes 15335424 | tf_op jit(solution)/shard_map/dot_general | solution.py:91
  260.0 4.7 convolution_convert_fusion.2
  264.7 33.2 %reduce-scatter.6.cloned.1.call-done = bf16[384,768]{1,0:T(8,128)(2,1)} async-done(((bf16[1536,768]{1,0:T(8,128)(2,1)}), bf16[384,768]{1,0:T(8,128)(2,1)}) %reduce-scatter.6.cloned.1.call-update) | async-done | bytes 589840 | tf_op jit(solution)/shard_map/reduce_scatter | solution.py:174
  297.9 5.5 all-to-all-start.1
  303.5 2.7 copy.60
  306.7 12.6 %all-to-all-done.1 = bf16[8,48,768]{2,1,0:T(8,128)(2,1)S(1)} async-done(((bf16[8,48,768]{2,1,0:T(8,128)(2,1)}), bf16[8,48,768]{2,1,0:T(8,128)(2,1)S(1)}, u32[]{:S(2)}, u32[]{:S(2)}) %all-to-all-start.1) | async-done | bytes 589856 | tf_op jit(solution)/shard_map/all_to_all | solution.py:180
  319.4 5.5 gather_fusion
  327.4 2.6 fusion.25
  334.3 5.8 scatter_custom_fusion.1
  340.1 20.2 %all_to_all.21 = bf16[8,48,768]{2,1,0:T(8,128)(2,1)} all-to-all(bf16[8,48,768]{2,1,0:T(8,128)(2,1)S(1)} %bitcast.105), channel_id=1, replica_groups=mesh['wide'=8,'narrow'=4] {'wide'}, dimensions={0} | all-to-all | bytes 1179648 | tf_op jit(solution)/shard_map/all_to_all | solution.py:203
  360.9 21.3 %all-gather.12.cloned.1.call-done = bf16[1536,768]{1,0:T(8,128)(2,1)} async-done(((bf16[384,768]{1,0:T(8,128)(2,1)}), bf16[1536,768]{1,0:T(8,128)(2,1)}) %all-gather.12.cloned.1.call-update) | async-done | bytes 2359312 | tf_op jit(solution)/shard_map/all_gather | solution.py:206
  382.1 7.9 %add_convert_fusion = bf16[1536,768]{1,0:T(8,128)(2,1)S(1)} fusion(f32[1536,768]{1,0:T(8,128)} %get-tuple-element.79, f32[1536,768]{1,0:T(8,128)} %get-tuple-element.91, bf16[1536,768]{1,0:T(8,128)(2,1)} %all-gather.12.cloned.1.call-done, bf16[1,768,768]{2,1,0:T(8,128)(2,1)} %param.20), kind=kOutput, calls=%fused_computation.32 | convolution fusion | flops 1828454400 | bytes 15335424 | tf_op jit(solution)/shard_map/dot_general | solution.py:103
  391.4 3.5 convolution_convert_fusion.1
  394.9 33.2 %reduce-scatter.8.cloned.1.call-done = bf16[384,768]{1,0:T(8,128)(2,1)} async-done(((bf16[1536,768]{1,0:T(8,128)(2,1)}), bf16[384,768]{1,0:T(8,128)(2,1)}) %reduce-scatter.8.cloned.1.call-update) | async-done | bytes 589840 | tf_op jit(solution)/shard_map/reduce_scatter | solution.py:210
  428.1 5.5 all-to-all-start.3
  433.7 15.8 %all-to-all-done.3 = bf16[8,48,768]{2,1,0:T(8,128)(2,1)S(1)} async-done(((bf16[8,48,768]{2,1,0:T(8,128)(2,1)}), bf16[8,48,768]{2,1,0:T(8,128)(2,1)S(1)}, u32[]{:S(2)}, u32[]{:S(2)}) %all-to-all-start.3) | async-done | bytes 589856 | tf_op jit(solution)/shard_map/all_to_all | solution.py:220
  449.5 5.2 gather_fusion.1
  454.8 2.6 copy.62
  457.4 5.3 multiply_reduce_fusion.1
  463.0 4.1 fusion.72
  469.8 2.9 fusion.76
  472.7 3.2 convolution_convert_fusion.3
  477.0 20.8 %fusion.33 = bf16[12,64,1024]{2,1,0:T(8,128)(2,1)} fusion(bf16[1024,12,64]{0,2,1:T(8,128)(2,1)S(1)} %bitcast.108, f32[12,1024]{1,0:T(8,128)S(1)} %log_add_fusion, f32[12,1024,1024]{1,2,0:T(8,128)} %get-tuple-element.87, pred[1024,1024]{0,1:T(8,128)(4,1)S(1)} %iota_compare_fusion), kind=kOutput, calls=%fused_computation.76 | convolution fusion | flops 1661730816 | bytes 54575104 | tf_op jit(solution)/shard_map/while/body/eval_jaxpr/hqk,qhd->khd/dot_general | solution.py:63
  497.8 34.3 %multiply_reduce_fusion = (f32[12,1024]{1,0:T(8,128)S(1)}, f32[12,1024,1024]{1,2,0:T(8,128)}) fusion(f32[12,1024]{1,0:T(8,128)S(1)} %log_add_fusion, f32[12,1024,1024]{1,2,0:T(8,128)} %get-tuple-element.87, pred[1024,1024]{0,1:T(8,128)(4,1)S(1)} %iota_compare_fusion, bf16[1024,12,64]{0,2,1:T(8,128)(2,1)} %bitcast.109, bf16[1024,12,64]{0,2,1:T(8,128)(2,1)} %bitcast.96), kind=kOutput, calls=%fused_computation.5 | convolution fusion | flops 1673515008 | bytes 104955904 | tf_op jit(solution)/shard_map/while/body/eval_jaxpr/qhd,khd->hqk/dot_general | solution.py:60
  532.2 42.1 %multiply_convert_fusion = bf16[12,1024,1024]{1,2,0:T(8,128)(2,1)} fusion(f32[12,1024,1024]{1,2,0:T(8,128)} %get-tuple-element.93, f32[12,1024]{1,0:T(8,128)S(1)} %get-tuple-element.92, f32[12,1024]{1,0:T(8,128)S(1)} %log_add_fusion, f32[12,1024,1024]{1,2,0:T(8,128)} %get-tuple-element.87, pred[1024,1024]{0,1:T(8,128)(4,1)S(1)} %iota_compare_fusion), kind=kLoop, calls=%fused_computation.4 | loop fusion | flops 75497472 | bytes 126976000 | tf_op jit(solution)/shard_map/while/body/eval_jaxpr/convert_element_type | solution.py:68
  574.3 14.4 %multiply_convert_fusion.2 = bf16[12,64,1024]{2,1,0:T(8,128)(2,1)} fusion(bf16[1024,12,64]{0,2,1:T(8,128)(2,1)} %bitcast.93, bf16[12,1024,1024]{1,2,0:T(8,128)(2,1)} %multiply_convert_fusion), kind=kOutput, calls=%fused_computation.63 | convolution fusion | flops 1612185600 | bytes 28311552 | tf_op jit(solution)/shard_map/while/body/eval_jaxpr/hqk,qhd->khd/dot_general | solution.py:75
  588.8 13.4 %multiply_convert_fusion.3 = bf16[12,64,1024]{2,1,0:T(8,128)(2,1)S(1)} fusion(bf16[1024,12,64]{0,2,1:T(8,128)(2,1)} %bitcast.95, bf16[12,1024,1024]{1,2,0:T(8,128)(2,1)} %multiply_convert_fusion), kind=kOutput, calls=%fused_computation.64 | convolution fusion | flops 1612185600 | bytes 28311552 | tf_op jit(solution)/shard_map/while/body/eval_jaxpr/hqk,khd->qhd/dot_general | solution.py:71
  603.4 6.9 fusion.31
  611.0 5.0 fusion.27
  616.1 5.3 convolution_bitcast_fusion
  621.4 3.7 convolution_bitcast_fusion.1
  627.7 6.9 fusion.24
  637.6 38.5 %all-reduce.7 = (f32[768]{0:T(1024)S(1)}, f32[768]{0:T(1024)S(1)}, f32[768,8]{0,1:T(8,128)S(1)}) all-reduce(f32[768]{0:T(1024)S(1)} %get-tuple-element.65, f32[768]{0:T(1024)S(1)} %copy-done.43, f32[768,8]{0,1:T(8,128)S(1)} %fusion.27), channel_id=4, replica_groups=mesh['wide'=8,'narrow'=4] {'wide','narrow'}, use_global_device_ids=true, to_apply=%region_22.23.clone | all-reduce | flops 7680 | bytes 61440
  677.2 6.6 add_add_fusion.2
  683.8 3.7 copy.67
  688.1 66.6 %reduce-scatter.10.cloned.1.call-done = f32[24,2304]{1,0:T(8,128)} async-done(((f32[768,2304]{1,0:T(8,128)}), f32[24,2304]{1,0:T(8,128)}) %reduce-scatter.10.cloned.1.call-update) | async-done | bytes 221200 | tf_op jit(solution)/shard_map/reduce_scatter | solution.py:252
  (166 shorter events, 48.4 us)
Async XLA Ops:
  7.2 236.9 %copy-start = (bf16[1,768,768]{2,1,0:T(8,128)(2,1)S(1)}, bf16[1,768,768]{2,1,0:T(8,128)(2,1)}, u32[]{:S(2)}) copy-start(bf16[1,768,768]{2,1,0:T(8,128)(2,1)} %param.19) | copy-start | bytes 3538948
  7.2 96.4 %all-gather.6.cloned.1.call-start = ((), (), s32[]{:S(2)}) async-start(), calls=%async_computation.8 | async-start | bytes 3649536 | tf_op jit(solution)/shard_map/all_gather | solution.py:134
  7.9 176.7 %all-gather.8.cloned.1.call-start = ((), (), s32[]{:S(2)}) async-start(), calls=%async_computation.9 | async-start | bytes 1216512 | tf_op jit(solution)/shard_map/all_gather | solution.py:135
  8.7 235.4 %all-gather.10.cloned.1.call-start = ((), (), s32[]{:S(2)}) async-start(), calls=%async_computation.10 | async-start | bytes 2949120 | tf_op jit(solution)/shard_map/all_gather | solution.py:173
  52.8 50.8 %copy-start.29 = (f32[768]{0:T(1024)}, f32[768]{0:T(1024)S(1)}, u32[]{:S(2)}) copy-start(f32[768]{0:T(1024)S(1)} %convert_element_type.89) | copy-start | bytes 9220
  52.8 136.0 %copy-start.21 = (f32[768]{0:T(1024)}, f32[768]{0:T(1024)S(1)}, u32[]{:S(2)}) copy-start(f32[768]{0:T(1024)S(1)} %convert_element_type.98) | copy-start | bytes 9220
  97.2 6.2 copy-start.25
  97.2 6.2 copy-start.46
  101.5 8.7 %copy-start.27 = (f32[1024]{0:T(1024)}, f32[1024]{0:T(1024)S(1)}, u32[]{:S(2)}) copy-start(f32[1024]{0:T(1024)S(1)} %broadcast_multiply_fusion.1) | copy-start | bytes 12292
  103.4 6.8 copy-start.33
  103.4 6.8 copy-start.31
  103.5 6.7 copy-start.38
  103.5 6.7 copy-start.40
  103.5 92.6 %copy-start.44 = (s32[1024,1]{0,1:T(1,128)}, s32[1024,1]{0,1:T(1,128)S(1)}, u32[]{:S(2)}) copy-start(s32[1024,1]{0,1:T(1,128)S(1)} %compare_select_fusion) | copy-start | bytes 12292
  141.9 21.0 %copy-start.11 = (bf16[1024,768]{0,1:T(8,128)(2,1)S(1)}, bf16[1024,768]{0,1:T(8,128)(2,1)}, u32[]{:S(2)}) copy-start(bf16[1024,768]{0,1:T(8,128)(2,1)} %copy.53) | copy-start | bytes 4718596
  188.4 5.2 copy-start.2
  188.8 4.8 copy-start.35
  188.8 4.8 copy-start.23
  222.4 75.5 %reduce-scatter.6.cloned.1.call-start = ((), (), s32[]{:S(2)}) async-start(), calls=%async_computation.11 | async-start | bytes 2949120 | tf_op jit(solution)/shard_map/reduce_scatter | solution.py:174
  264.7 41.5 %copy-start.45 = (s32[1024,1]{0,1:T(1,128)S(1)}, s32[1024,1]{0,1:T(1,128)}, u32[]{:S(2)}) copy-start(s32[1024,1]{0,1:T(1,128)} %copy-done.44) | copy-start | bytes 12292
  297.9 21.4 %all-to-all-start.1 = ((bf16[8,48,768]{2,1,0:T(8,128)(2,1)}), bf16[8,48,768]{2,1,0:T(8,128)(2,1)S(1)}, u32[]{:S(2)}, u32[]{:S(2)}) async-start(bf16[8,48,768]{2,1,0:T(8,128)(2,1)} %bitcast.111), calls=%async_computation.2 | async-start | bytes 1179648 | tf_op jit(solution)/shard_map/all_to_all | solution.py:180
  303.4 78.7 %all-gather.12.cloned.1.call-start = ((), (), s32[]{:S(2)}) async-start(), calls=%async_computation.12 | async-start | bytes 2949120 | tf_op jit(solution)/shard_map/all_gather | solution.py:206
  324.8 5.2 copy-start.37
  324.8 5.2 copy-start.39
  324.8 5.2 copy-start.41
  360.4 67.7 %reduce-scatter.8.cloned.1.call-start = ((), (), s32[]{:S(2)}) async-start(), calls=%async_computation.13 | async-start | bytes 2949120 | tf_op jit(solution)/shard_map/reduce_scatter | solution.py:210
  394.8 54.7 %copy-start.42 = (s32[1024]{0:T(1024)S(1)}, s32[1024]{0:T(1024)}, u32[]{:S(2)}) copy-start(s32[1024]{0:T(1024)} %broadcast_clamp_fusion) | copy-start | bytes 12292
  428.1 21.4 %all-to-all-start.3 = ((bf16[8,48,768]{2,1,0:T(8,128)(2,1)}), bf16[8,48,768]{2,1,0:T(8,128)(2,1)S(1)}, u32[]{:S(2)}, u32[]{:S(2)}) async-start(bf16[8,48,768]{2,1,0:T(8,128)(2,1)} %bitcast.110), calls=%async_computation.5 | async-start | bytes 1179648 | tf_op jit(solution)/shard_map/all_to_all | solution.py:220
  433.6 254.5 %reduce-scatter.12.cloned.1.call-start = ((), (), s32[]{:S(2)}) async-start(), calls=%async_computation.15 | async-start | bytes 2433024 | tf_op jit(solution)/shard_map/reduce_scatter | solution.py:253
  457.4 5.3 copy-start.36
  457.4 5.3 copy-start.3
  457.4 5.3 copy-start.7
  457.4 5.6 copy-start.9
  463.0 4.1 copy-start.6
  467.0 2.8 copy-start.47
  532.2 222.5 %reduce-scatter.10.cloned.1.call-start = ((), (), s32[]{:S(2)}) async-start(), calls=%async_computation.14 | async-start | bytes 7299072 | tf_op jit(solution)/shard_map/reduce_scatter | solution.py:252
  588.7 14.6 %copy-start.4 = (bf16[1024,768]{0,1:T(8,128)(2,1)S(1)}, bf16[1024,768]{0,1:T(8,128)(2,1)}, u32[]{:S(2)}) copy-start(bf16[1024,768]{0,1:T(8,128)(2,1)} %copy.52) | copy-start | bytes 4718596
  588.8 14.6 %copy-start.12 = (bf16[12,64,1024]{2,1,0:T(8,128)(2,1)S(1)}, bf16[12,64,1024]{2,1,0:T(8,128)(2,1)}, u32[]{:S(2)}) copy-start(bf16[12,64,1024]{2,1,0:T(8,128)(2,1)} %multiply_convert_fusion.2) | copy-start | bytes 4718596
  588.8 14.6 %copy-start.28 = (f32[1024]{0:T(1024)S(1)}, f32[1024]{0:T(1024)}, u32[]{:S(2)}) copy-start(f32[1024]{0:T(1024)} %copy-done.27) | copy-start | bytes 12292
  588.8 14.6 %copy-start.30 = (f32[768]{0:T(1024)S(1)}, f32[768]{0:T(1024)}, u32[]{:S(2)}) copy-start(f32[768]{0:T(1024)} %copy-done.29) | copy-start | bytes 9220
  588.8 14.6 %copy-start.32 = (f32[1024]{0:T(1024)S(1)}, f32[1024]{0:T(1024)}, u32[]{:S(2)}) copy-start(f32[1024]{0:T(1024)} %copy-done.31) | copy-start | bytes 12292
  588.8 14.6 %copy-start.48 = (bf16[12,64,1024]{2,1,0:T(8,128)(2,1)S(1)}, bf16[12,64,1024]{2,1,0:T(8,128)(2,1)}, u32[]{:S(2)}) copy-start(bf16[12,64,1024]{2,1,0:T(8,128)(2,1)} %fusion.33) | copy-start | bytes 4718596
  611.0 5.0 copy-start.15
  616.1 5.3 copy-start.13
  616.1 5.3 copy-start.17
  627.7 6.9 copy-start.34
  634.6 3.0 copy-start.43
  677.2 77.5 %copy-start.1 = (bf16[1,768,768]{2,1,0:T(8,128)(2,1)S(1)}, bf16[1,768,768]{2,1,0:T(8,128)(2,1)}, u32[]{:S(2)}) copy-start(bf16[1,768,768]{2,1,0:T(8,128)(2,1)} %param.19) | copy-start | bytes 3538948
  (11 other events, 18.3 us)
Sparse Core Ops, SparseCore 0:
  10.9 62.9 all-gather.5
  76.8 52.8 all-gather.7
  222.5 21.5 all-gather.9
  264.8 33.0 reduce-scatter.5
  360.5 21.5 all-gather.11
  395.0 33.0 reduce-scatter.7
  532.3 97.1 reduce-scatter.11
  636.7 117.9 reduce-scatter.9
where the time goes:
time: 773 us; the launch traced here: 762 us
  waiting for transfers between devices  206 us (27%)
  matrix products  206 us (27%)
  blocking collectives  162 us (21%)
  other arithmetic  93.3 us (12%)
  local copies, waits for them, and re-layouts  68.4 us (9%)
  between operations  15.2 us (2%)
  starting transfers between devices  11.7 us (2%)
    unnamed x2, blocking collectives  80.5 us
    reduce_scatter x1, waiting for transfers between devices, shards(): lax.psum_scatter(qkv_part, ('wide', 'narrow'), scatter_dimension=0, tiled...  66.6 us
    convert_element_type x1, other arithmetic, attend_backward(): grad_scores = (attn_probs * (grad_probs - jnp.sum(grad_probs * attn_probs...  42.1 us
    all_gather x1, blocking collectives, shards(): lax.all_gather(cluster_mean_columns, ('wide', 'narrow'), axis=0, tiled=True)  40.8 us
    dot_general x1, matrix products, attend_backward(): jnp.einsum('qhd,khd->hqk', grad_out, value_rows, preferred_element_type=j...  34.3 us
    reduce_scatter x1, waiting for transfers between devices, shards(): lax.psum_scatter(expert_rows(gathered, first_linear_matrix[0], second_lin...  33.2 us
    reduce_scatter x1, waiting for transfers between devices, shards(): lax.psum_scatter(lax.dot_general(grad_pre, first_linear_matrix[0], over_c...  33.2 us
    unnamed x110, local copies, waits for them, and re-layouts  25.2 us
  transfers between devices with their start and end apart: 10, of which 7 were waited for; matrix products, arithmetic and copies ran while one was open for 28% of the time, Pallas kernels for 0%

commit v1 on v0

--- a/solution.py
+++ b/solution.py
@@ -1,11 +1,621 @@
+import functools
+
 import jax
 import jax.numpy as jnp
 from jax import lax
+from jax.experimental import pallas as pl
+from jax.experimental.pallas import tpu as pltpu
 from jax.sharding import PartitionSpec as P
 
 HD = 64
 SEQ = 1024
 SLOT = 48
+PAIR = 2 * HD
+QB = 256
+LANES = 128
+GAIN1 = 126
+GAIN2 = 127
+NEG = -1e30
+VMEM_CAP = 62 << 20
+
+MESH = pl.DeviceIdType.MESH
+NN_ = (((1,), (0,)), ((), ()))
+NT_ = (((1,), (1,)), ((), ()))
+TN_ = (((0,), (0,)), ((), ()))
+f32 = jnp.float32
+bf16 = jnp.bfloat16
+
+
+def mm(a, b, dims=NN_):
+    return lax.dot_general(a, b, dims, preferred_element_type=f32)
+
+
+def wait_bytes(ref, sem):
+    pltpu.make_async_copy(ref, ref, sem).wait()
+
+
+def push(src, dst, send, recv, **where):
+    pltpu.make_async_remote_copy(
+        src_ref=src, dst_ref=dst, send_sem=send, recv_sem=recv,
+        device_id=where, device_id_type=MESH,
+    ).start()
+
+
+def half_mask(rows):
+    return lax.broadcasted_iota(jnp.int32, (rows, PAIR), 1) < HD
+
+
+def pick(mask, h, value):
+    zero = jnp.zeros_like(value)
+    return jnp.where(mask, value, zero) if h == 0 else jnp.where(mask, zero, value)
+
+
+def layer_stats(x):
+    centered = x - jnp.mean(x, 1, keepdims=True)
+    r = lax.rsqrt(jnp.mean(centered * centered, 1, keepdims=True) + 1e-05)
+    return centered * r, r
+
+
+def attend_rows(qkv, seq, i, put_out, put_lse):
+    length = (i + 1) * QB
+    rows = pl.ds(i * QB, QB)
+    mask = half_mask(QB)
+    causal = lax.broadcasted_iota(jnp.int32, (QB, QB), 0) <= lax.broadcasted_iota(
+        jnp.int32, (QB, QB), 1
+    )
+    q = qkv[rows, 0:PAIR] * bf16(HD**-0.5)
+    k = qkv[pl.ds(0, length), PAIR : 2 * PAIR]
+    v = qkv[pl.ds(0, length), 2 * PAIR : 3 * PAIR]
+    outs, sums = [], []
+    for h in range(2):
+        s = mm(k, pick(mask, h, q), NT_)
+        last = jnp.where(causal, s[length - QB :], NEG)
+        top = jnp.max(last, 0, keepdims=True)
+        if i:
+            top = jnp.maximum(top, jnp.max(s[: length - QB], 0, keepdims=True))
+        p = jnp.exp(last - top)
+        total = jnp.sum(p, 0, keepdims=True)
+        p = p.astype(bf16)
+        if i:
+            head = jnp.exp(s[: length - QB] - top)
+            total = total + jnp.sum(head, 0, keepdims=True)
+            p = jnp.concatenate([head.astype(bf16), p], 0)
+        put_lse(h, rows, top + jnp.log(total))
+        outs.append(mm(p, v, TN_))
+        sums.append(total)
+    inv = jnp.transpose(1.0 / jnp.concatenate(sums + [jnp.ones((6, QB), f32)], 0))
+    put_out(rows, jnp.where(mask, outs[0] * inv[:, 0:1], outs[1] * inv[:, 1:2]).astype(bf16))
+
+
+def attend_rows_back(qkv, att, datt, lse, i, first, prod, dk, dv, put_dq):
+    length = (i + 1) * QB
+    rows = pl.ds(i * QB, QB)
+    mask = half_mask(QB)
+    mask_all = half_mask(length)
+    causal = lax.broadcasted_iota(jnp.int32, (QB, QB), 0) <= lax.broadcasted_iota(
+        jnp.int32, (QB, QB), 1
+    )
+    q = qkv[rows, 0:PAIR] * bf16(HD**-0.5)
+    k = qkv[pl.ds(0, length), PAIR : 2 * PAIR]
+    v = qkv[pl.ds(0, length), 2 * PAIR : 3 * PAIR]
+    do = datt[rows, :]
+    dq = None
+    for h in range(2):
+        qh, dh = pick(mask, h, q), pick(mask, h, do)
+        s = mm(k, qh, NT_)
+        row = lse[h : h + 1, rows]
+        p = jnp.exp(jnp.where(causal, s[length - QB :], NEG) - row)
+        if i:
+            p = jnp.concatenate([jnp.exp(s[: length - QB] - row), p], 0)
+        dp = mm(v, dh, NT_)
+        ds = (p * (dp - prod[h : h + 1, rows])).astype(bf16)
+        a, b = mm(p.astype(bf16), dh), mm(ds, qh)
+        if first and h == 0:
+            dv[pl.ds(0, length), :] = a
+            dk[pl.ds(0, length), :] = b
+        else:
+            dv[pl.ds(0, length), :] += a
+            dk[pl.ds(0, length), :] += b
+        part = mm(ds, pick(mask_all, h, k), TN_)
+        dq = part if dq is None else dq + part
+    put_dq(rows, (dq * HD**-0.5).astype(bf16))
+
+
+class Sizes:
+    def __init__(self, mesh, tokens, d, slab, ff, experts):
+        self.NW, self.NN = mesh.shape["wide"], mesh.shape["narrow"]
+        self.A, self.X = self.NW // 2, self.NN // 2
+        self.T, self.D, self.slab, self.F, self.E = tokens, d, slab, ff, experts
+        self.CW = 3 * PAIR
+        self.G = d // PAIR
+        self.J = self.G + d // self.CW
+        self.R = self.NN * SLOT
+        self.S = experts * SLOT
+        self.EP = max(8, experts)
+        rows = self.NW * self.R
+        self.moe = rows * (5 * d + 3 * ff) * 2 < (24 << 20)
+        self.fits = (
+            self.moe and slab % 8 == 0 and tokens == SEQ and self.NW % 2 == 0 and self.NN % 2 == 0
+            and self.NW > 2 and self.NN > 2 and experts == self.NW
+        )
+
+
+def place(c):
+    w, n = lax.axis_index("wide"), lax.axis_index("narrow")
+    return w, n, w // 2, lax.rem(w, 2), n // 2, lax.rem(n, 2)
+
+
+def greet(c, w, n):
+    bar = pltpu.get_barrier_semaphore()
+    x, cc = n // 2, lax.rem(n, 2)
+
+    def wide(i, _):
+        pl.semaphore_signal(bar, inc=1, device_id={"wide": lax.rem(w + i, c.NW)}, device_id_type=MESH)
+        return 0
+
+    lax.fori_loop(1, c.NW, wide, 0)
+    for k in range(1, c.X):
+        pl.semaphore_signal(bar, inc=1, device_id={"narrow": lax.rem(x + k, c.X) * 2 + cc}, device_id_type=MESH)
+    pl.semaphore_signal(bar, inc=1, device_id={"narrow": x * 2 + 1 - cc}, device_id_type=MESH)
+    return lambda: pl.semaphore_wait(bar, c.NW - 1 + c.X)
+
+
+def forward_kernel(c, *refs):
+    (v_hbm, dy_hbm, idx_ref, cap_ref, wq_hbm, wo_hbm, misc_hbm, up_hbm, down_hbm) = refs[:9]
+    (wall, mall, qkv_out, lse_out, att_out, resid_out, sent_out, meta_out, mrow_out) = refs[9:18]
+    (ret_out, outp_out, ug_out, dg_out, cent_out) = refs[18:23]
+    scratch = refs[23:]
+    (v, dy, nrm, normed, oh, wbuf, wmat, misc, mrow, qkv, lse, att, sent, sendx, senddy,
+     lsem, in_sem, out_sem, ld_sem, s1s, s1r, s2s, s2r, s3s, s3r, s4s, s4r) = scratch[:27]
+    A, X, NW, NN, T, D, CW, G, J = c.A, c.X, c.NW, c.NN, c.T, c.D, c.CW, c.G, c.J
+    w, n, a, b, x, cc = place(c)
+    own = (a, b, x, cc)
+
+    def cols(j):
+        dst = wall.at[(j, *own)]
+        if j < G:
+            return [(wq_hbm.at[:, pl.ds(p * D + j * PAIR, PAIR)], dst.at[:, pl.ds(p * PAIR, PAIR)]) for p in range(3)]
+        return [(wo_hbm.at[:, pl.ds((j - G) * CW, CW)], dst)]
+
+    pltpu.make_async_copy(misc_hbm, mall.at[own], lsem.at[J]).start()
+    for j in range(J):
+        for s, d in cols(j):
+            pltpu.make_async_copy(s, d, lsem.at[j]).start()
+    loads = [(dy_hbm, dy), (v_hbm, v)]
+    if c.moe:
+        (up, down, xin, dyin, hid, dpre, dexp, outp, part, lc, lx, stage, cent,
+         ds_, dr, xs_, xr, cs_, cr, fs, fr, gs, gr, ks, kr, rs_, rr, ws_, wr) = scratch[27:]
+        loads += [(up_hbm.at[0], up), (down_hbm.at[0], down)]
+    for i, (s, d) in enumerate(loads):
+        pltpu.make_async_copy(s, d, in_sem.at[i]).start()
+
+    def load_wait(i):
+        wait_bytes(loads[i][1], in_sem.at[i])
+
+    met = greet(c, w, n)
+
+    one = lax.broadcasted_iota(jnp.int32, (c.EP, T), 0) == idx_ref[...]
+    hot = one.astype(f32)
+    lane = lax.broadcasted_iota(jnp.int32, (c.EP, T), 1)
+    count = hot
+    shift = 1
+    while shift < T:
+        count = count + jnp.where(lane >= shift, pltpu.roll(count, shift, 1), 0.0)
+        shift *= 2
+    rank = jnp.sum((count - hot) * hot, 0, keepdims=True)
+    ceiling = jnp.sum(hot * cap_ref[:, 0:1].astype(f32), 0, keepdims=True)
+    kept = rank < ceiling
+    slot = jnp.where(kept, idx_ref[...].astype(f32) * SLOT + rank, -1.0)
+    meta_out_rows = [slot]
+
+    met()
+
+    def buf(j):
+        return mall if j is J else wall.at[j]
+
+    def s1(j):
+        wait_bytes(buf(j).at[own], lsem.at[j])
+        for k in range(1, A):
+            push(buf(j).at[own], buf(j).at[own], s1s.at[j], s1r.at[j], wide=lax.rem(a + k, A) * 2 + b)
+
+    def s2(j):
+        wait_bytes(buf(j).at[pl.ds(0, A - 1), b, x, cc], s1r.at[j])
+        for k in range(1, X):
+            part_ = buf(j).at[:, b, x, cc]
+            push(part_, part_, s2s.at[j], s2r.at[j], narrow=lax.rem(x + k, X) * 2 + cc)
+
+    def s3(j):
+        wait_bytes(buf(j).at[:, b, pl.ds(0, X - 1), cc], s2r.at[j])
+        part_ = buf(j).at[:, b, :, cc]
+        push(part_, part_, s3s.at[j], s3r.at[j], wide=a * 2 + 1 - b)
+
+    def s4(j):
+        wait_bytes(buf(j).at[:, b, :, cc], s3r.at[j])
+        part_ = buf(j).at[:, :, :, cc]
+        push(part_, part_, s4s.at[j], s4r.at[j], narrow=x * 2 + 1 - cc)
+
+    def ld(j):
+        wait_bytes(buf(j).at[:, :, :, cc], s4r.at[j])
+        if j is J:
+            pltpu.make_async_copy(mall, misc, ld_sem.at[J]).start()
+        else:
+            pltpu.make_async_copy(wall.at[j], wbuf.at[lax.rem(j, 2)], ld_sem.at[j]).start()
+
+    def loaded(j, at):
+        slot_ = lax.rem(j, 2)
+        wait_bytes(wbuf.at[slot_], ld_sem.at[j])
+        wmat[at] = wbuf[slot_].reshape(D, CW)
+
+    s1(J)
+    for j in range(J):
+        s1(j)
+
+    ohv = (lax.broadcasted_iota(jnp.int32, (c.S, T), 0).astype(f32) == slot).astype(bf16)
+    oh[...] = ohv
+    load_wait(0)
+    senddy[...] = mm(oh[...], dy[...]).astype(bf16)
+    s2(J)
+    s2(0)
+
+    if c.moe:
+        for k in range(1, NW):
+            to = lax.rem(w + k, NW)
+            push(senddy.at[pl.ds(to * SLOT, SLOT)], dyin.at[w, x, cc], ds_, dr, wide=to)
+        dyin[w, x, cc] = senddy[pl.ds(w * SLOT, SLOT), :]
+    else:
+        pltpu.make_async_copy(senddy, senddy_out, out_sem.at[7]).start()
+    s3(J)
+    s3(0)
+    s2(1)
+
+    load_wait(1)
+
+    def norm1(i, _):
+        rows = pl.ds(i * 128, 128)
+        nrm[rows, :] = layer_stats(v[rows, :].astype(f32))[0]
+        return 0
+
+    lax.fori_loop(0, T // 128, norm1, 0)
+    s4(J)
+    s4(0)
+    s3(1)
+    s2(2)
+    ld(J)
+    wait_bytes(misc, ld_sem.at[J])
+    mrow[...] = jnp.transpose(misc[...].reshape(D, LANES).astype(f32))
+    gain1 = mrow[GAIN1 : GAIN1 + 1, :]
+    gain2 = mrow[GAIN2 : GAIN2 + 1, :]
+    pltpu.make_async_copy(mrow, mrow_out, out_sem.at[0]).start()
+
+    def norm1b(i, _):
+        rows = pl.ds(i * 128, 128)
+        normed[rows, :] = (nrm[rows, :] * gain1).astype(bf16)
+        return 0
+
+    lax.fori_loop(0, T // 128, norm1b, 0)
+    ld(0)
+
+    def pair(g, _):
+        loaded(g, 0)
+
+        def project(i, _):
+            rows = pl.ds(i * QB, QB)
+            qkv[g, rows, :] = mm(normed[rows, :], wmat[0]).astype(bf16)
+            return 0
+
+        lax.fori_loop(0, T // QB, project, 0)
+        pltpu.make_async_copy(qkv.at[g], qkv_out.at[g], out_sem.at[1]).start()
+        s3(g + 2)
+
+        @pl.when(g + 3 < J)
+        def _():
+            s2(g + 3)
+
+        def put_out(rows, val):
+            att[rows, pl.ds(pl.multiple_of(g * PAIR, PAIR), PAIR)] = val
+
+        def put_lse(h, rows, val):
+            lse[g, h : h + 1, rows] = val
+
+        for i in range(T // QB):
+            if i == T // QB - 1:
+                s4(g + 1)
+                if c.moe:
+                    @pl.when(g == 4)
+                    def _():
+                        wait_bytes(dyin.at[pl.ds(0, NW - 1), x, cc], dr)
+                        for k in range(1, X):
+                            push(dyin.at[:, x, cc], dyin.at[:, x, cc], xs_, xr, narrow=lax.rem(x + k, X) * 2 + cc)
+            attend_rows(qkv.at[g], T, i, put_out, put_lse)
+        ld(g + 1)
+        return 0
+
+    lax.fori_loop(0, G, pair, 0)
+    pltpu.make_async_copy(lse, lse_out, out_sem.at[2]).start()
+    pltpu.make_async_copy(att, att_out, out_sem.at[3]).start()
+    for j in range(G + 1, J):
+        s4(j)
+        ld(j)
+    if c.moe:
+        wait_bytes(dyin.at[:, pl.ds(0, X - 1), cc], xr)
+        push(dyin.at[:, :, cc], dyin.at[:, :, cc], cs_, cr, narrow=x * 2 + 1 - cc)
+    for j in range(G, J):
+        loaded(j, 1 + j - G)
+
+    def tail(i, _):
+        rows = pl.ds(i * QB, QB)
+        left = att[rows, :]
+        prod = jnp.concatenate([mm(left, wmat[1 + j - G]) for j in range(G, J)], 1)
+        resid = v[rows, :].astype(f32) + prod
+        nrm[rows, :] = resid
+        sent[rows, :] = (layer_stats(resid)[0] * gain2).astype(bf16)
+        return 0
+
+    lax.fori_loop(0, T // QB, tail, 0)
+    pltpu.make_async_copy(nrm, resid_out, out_sem.at[4]).start()
+    sendx[...] = mm(oh[...], sent[...]).astype(bf16)
+    if c.moe:
+        for k in range(1, NW):
+            to = lax.rem(w + k, NW)
+            push(sendx.at[pl.ds(to * SLOT, SLOT)], xin.at[w, x, cc], fs.at[k], fr.at[k], wide=to)
+        xin[w, x, cc] = sendx[pl.ds(w * SLOT, SLOT), :]
+    else:
+        pltpu.make_async_copy(sendx, sendx_out, out_sem.at[8]).start()
+    pltpu.make_async_copy(sent, sent_out, out_sem.at[5]).start()
+    logits = mm(mrow[0 : c.EP, :].astype(bf16), sent[...], NT_)
+    logit = jnp.sum(logits * hot, 0, keepdims=True)
+    gate = jax.nn.sigmoid(logit) * kept.astype(f32)
+    meta_out[...] = jnp.concatenate([slot, gate, jnp.zeros((6, T), f32)], 0)
+
+    if c.moe:
+        load_wait(2)
+        load_wait(3)
+        wait_bytes(dyin.at[:, :, cc], cr)
+        cent[...] = jnp.zeros_like(cent)
+        crow = mrow[pl.ds(w, 1), :]
+
+        def source(i):
+            return lax.rem(w - i + NW, NW)
+
+        def fwd_x(i):
+            src = source(i)
+
+            @pl.when(i > 0)
+            def _():
+                wait_bytes(xin.at[src, x, cc], fr.at[i])
+
+            for k in range(1, X):
+                push(xin.at[src, x, cc], xin.at[src, x, cc], gs.at[i], gr.at[i], narrow=lax.rem(x + k, X) * 2 + cc)
+
+        def fwd_c(i):
+            src = source(i)
+            wait_bytes(xin.at[src, pl.ds(0, X - 1), cc], gr.at[i])
+            push(xin.at[src, :, cc], xin.at[src, :, cc], ks.at[i], kr.at[i], narrow=x * 2 + 1 - cc)
+
+        def expert(i):
+            src = source(i)
+            wait_bytes(xin.at[src, :, cc], kr.at[i])
+            xb = xin[src].reshape(c.R, D)
+            db = dyin[src].reshape(c.R, D)
+            xf, df = xb.astype(f32), db.astype(f32)
+            s = jax.nn.sigmoid(jnp.sum(xf * crow, 1, keepdims=True))
+            de = (df * s).astype(bf16)
+            pre = mm(xb, up[...])
+            cdf = 0.5 * (1.0 + lax.erf(pre * 0.7071067811865476))
+            hb = (pre * cdf).astype(bf16)
+            slope = cdf + pre * (jnp.exp(-0.5 * pre * pre) * 0.3989422804014327)
+            dpb = (mm(de, down[...]) * slope).astype(bf16)
+            out = mm(hb, down[...], NT_)
+            dl = jnp.sum(df * out, 1, keepdims=True) * (s * (1.0 - s))
+            dn = mm(dpb, up[...], NT_) + dl * crow
+            part[src] = dn.astype(bf16).reshape(X, 2, SLOT, D)
+            outp[src] = out.astype(bf16).reshape(X, 2, SLOT, D)
+            cent[...] += jnp.broadcast_to(jnp.sum(dl * xf, 0, keepdims=True), cent.shape)
+            rows = pl.ds(pl.multiple_of(src * c.R, SLOT), c.R)
+            hid[rows, :] = hb
+            dpre[rows, :] = dpb
+            dexp[rows, :] = de
+
+        def ret_c(i):
+            src = source(i)
+            push(part.at[src, :, 1 - cc], lc.at[src], rs_.at[0, i], rr.at[0, i], narrow=x * 2 + 1 - cc)
+
+        def ret_x(i):
+            src = source(i)
+            wait_bytes(lc.at[src], rr.at[0, i])
+            part[src, :, cc] = (part[src, :, cc].astype(f32) + lc[src].astype(f32)).astype(bf16)
+            for k in range(1, X):
+                x2 = lax.rem(x + k, X)
+                push(part.at[src, x2, cc], lx.at[src, x], rs_.at[1, i], rr.at[1, i], narrow=x2 * 2 + cc)
+
+        def ret_w(i):
+            src = source(i)
+            wait_bytes(lx.at[src, pl.ds(0, X - 1)], rr.at[1, i])
+            total = part[src, x, cc].astype(f32)
+            for k in range(1, X):
+                total = total + lx[src, lax.rem(x + k, X)].astype(f32)
+            part[src, x, cc] = total.astype(bf16)
+
+            @pl.when(i > 0)
+            def _():
+                push(part.at[src, x, cc], ret_out.at[w], ws_.at[i], wr.at[i], wide=src)
+
+            @pl.when(i == 0)
+            def _():
+                pltpu.make_async_copy(part.at[src, x, cc], ret_out.at[w], ws_.at[0]).start()
+
+        fwd_x(0)
+        fwd_c(0)
+        fwd_x(1)
+
+        def block(i, _):
+            @pl.when(i + 1 < NW)
+            def _():
+                fwd_c(i + 1)
+
+            @pl.when(i + 2 < NW)
+            def _():
+                fwd_x(i + 2)
+
+            expert(i)
+            ret_c(i)
+
+            @pl.when(i >= 1)
+            def _():
+                ret_x(i - 1)
+
+            @pl.when(i >= 2)
+            def _():
+                ret_w(i - 2)
+
+            return 0
+
+        lax.fori_loop(0, NW, block, 0)
+        ret_x(NW - 1)
+        ret_w(NW - 2)
+        pltpu.make_async_copy(outp, outp_out, out_sem.at[6]).start()
+        cent_out[...] = cent[...]
+
+        def grads(lhs, rhs, out, base, flush):
+            def one_block(i, _):
+                at = pl.ds(pl.multiple_of(i * QB, QB), QB)
+                lhs_block = lhs(at)
+                stage[base + i] = mm(lhs_block, rhs[...], TN_)
+                pltpu.make_async_copy(stage.at[base + i], out.at[0, at], in_sem.at[4 + base + i]).start()
+                return 0
+
+            lax.fori_loop(0, D // QB, one_block, 0)
+
+        grads(lambda at: dexp[:, at], hid, dg_out, 0, None)
+        ret_w(NW - 1)
+        grads(lambda at: xin[:, :, :, :, at].reshape(NW * c.R, QB), dpre, ug_out, D // QB, None)
+
+    for q, (s, ref) in enumerate([(mrow, None), (qkv, None), (lse, None), (att, None), (nrm, None), (sent, None)]):
+        wait_bytes(s, out_sem.at[q])
+    for j in [J] + list(range(J)):
+        wait_bytes(buf(j).at[pl.ds(0, A - 1), b, x, cc], s1s.at[j])
+        wait_bytes(buf(j).at[:, b, pl.ds(0, X - 1), cc], s2s.at[j])
+        wait_bytes(buf(j).at[:, b, :, cc], s3s.at[j])
+        wait_bytes(buf(j).at[:, :, :, cc], s4s.at[j])
+    if c.moe:
+        wait_bytes(dyin.at[pl.ds(0, NW - 1), x, cc], ds_)
+        wait_bytes(dyin.at[:, pl.ds(0, X - 1), cc], xs_)
+        wait_bytes(dyin.at[:, :, cc], cs_)
+        wait_bytes(outp, out_sem.at[6])
+
+        def drain(i, _):
+            src = source(i)
+            wait_bytes(xin.at[src, pl.ds(0, X - 1), cc], gs.at[i])
+            wait_bytes(xin.at[src, :, cc], ks.at[i])
+            wait_bytes(lc.at[src], rs_.at[0, i])
+            wait_bytes(lx.at[src, pl.ds(0, X - 1)], rs_.at[1, i])
+            wait_bytes(xin.at[src, x, cc], ws_.at[i])
+
+            @pl.when(i > 0)
+            def _():
+                wait_bytes(xin.at[src, x, cc], fs.at[i])
+                wait_bytes(xin.at[src, x, cc], wr.at[i])
+
+            return 0
+
+        lax.fori_loop(0, NW, drain, 0)
+        for i in range(2 * (D // QB)):
+            wait_bytes(stage.at[i], in_sem.at[4 + i])
+    else:
+        wait_bytes(senddy, out_sem.at[7])
+        wait_bytes(sendx, out_sem.at[8])
+
+
+def forward_call(c, v, dy, idx, cap, wq, wo, misc, up, down):
+    T, D, CW, G, J, NW, NN, A, X = c.T, c.D, c.CW, c.G, c.J, c.NW, c.NN, c.A, c.X
+    any_ = pl.BlockSpec(memory_space=pl.ANY)
+    vm = pl.BlockSpec(memory_space=pltpu.VMEM)
+    sds = jax.ShapeDtypeStruct
+    F = c.F
+    outs = [
+        (sds((J, A, 2, X, 2, c.slab, CW), bf16), any_),
+        (sds((A, 2, X, 2, c.slab, LANES), bf16), any_),
+        (sds((G, T, CW), bf16), any_),
+        (sds((G, 8, T), f32), any_),
+        (sds((T, D), bf16), any_),
+        (sds((T, D), f32), any_),
+        (sds((T, D), bf16), any_),
+        (sds((8, T), f32), vm),
+        (sds((LANES, D), f32), any_),
+    ]
+    dma, V = pltpu.SemaphoreType.DMA, pltpu.VMEM
+    scratch = [
+        V((T, D), bf16), V((T, D), bf16), V((T, D), f32), V((T, D), bf16), V((c.S, T), bf16),
+        V((2, A, 2, X, 2, c.slab, CW), bf16), V((1 + J - G, D, CW), bf16),
+        V((A, 2, X, 2, c.slab, LANES), bf16), V((LANES, D), f32), V((G, T, CW), bf16), V((G, 8, T), f32),
+        V((T, D), bf16), V((T, D), bf16), V((c.S, D), bf16), V((c.S, D), bf16),
+        dma((J + 1,)), dma((4 + 2 * (D // QB),)), dma((9,)), dma((J + 1,)),
+    ] + [dma((J + 1,))] * 8
+    if c.moe:
+        outs += [
+            (sds((NW, SLOT, D), bf16), any_),
+            (sds((NW, X, 2, SLOT, D), bf16), any_),
+            (sds((1, D, F), f32), any_),
+            (sds((1, D, F), f32), any_),
+            (sds((8, D), f32), vm),
+        ]
+        rows = NW * c.R
+        scratch += [
+            V((D, F), bf16), V((D, F), bf16), V((NW, X, 2, SLOT, D), bf16), V((NW, X, 2, SLOT, D), bf16),
+            V((rows, F), bf16), V((rows, F), bf16), V((rows, D), bf16), V((NW, X, 2, SLOT, D), bf16),
+            V((NW, X, 2, SLOT, D), bf16), V((NW, X, SLOT, D), bf16), V((NW, X, SLOT, D), bf16),
+            V((2 * (D // QB), QB, F), f32), V((8, D), f32),
+            dma(()), dma(()), dma(()), dma(()), dma(()), dma(()),
+            dma((NW,)), dma((NW,)), dma((NW,)), dma((NW,)), dma((NW,)), dma((NW,)),
+            dma((2, NW)), dma((2, NW)), dma((NW,)), dma((NW,)),
+        ]
+    else:
+        outs += [(sds((c.S, D), bf16), any_), (sds((c.S, D), bf16), any_)]
+    return pl.pallas_call(
+        functools.partial(forward_kernel, c),
+        out_shape=tuple(o[0] for o in outs),
+        in_specs=[any_, any_, vm, vm, any_, any_, any_, any_, any_],
+        out_specs=tuple(o[1] for o in outs),
+        scratch_shapes=scratch,
+        compiler_params=pltpu.CompilerParams(
+            collective_id=0, has_side_effects=True, vmem_limit_bytes=VMEM_CAP
+        ),
+        name="forward",
+    )(v, dy, idx, cap, wq, wo, misc, up, down)
+
+
+def attend_back_kernel(c, qkv, att, datt, lse, dqkv, dk, dv, prod):
+    full = jnp.transpose(datt[...].astype(f32) * att[...].astype(f32))
+    prod[0:1, :] = jnp.sum(full[0:HD], 0, keepdims=True)
+    prod[1:2, :] = jnp.sum(full[HD:], 0, keepdims=True)
+
+    def put_dq(rows, val):
+        dqkv[0, rows, 0:PAIR] = val
+
+    blocks = c.T // QB
+    for i in reversed(range(blocks)):
+        attend_rows_back(qkv.at[0], att, datt, lse.at[0], i, i == blocks - 1, prod, dk, dv, put_dq)
+    dqkv[0, :, PAIR : 2 * PAIR] = dk[...].astype(bf16)
+    dqkv[0, :, 2 * PAIR :] = dv[...].astype(bf16)
+
+
+def attend_back_call(c, qkv, att, datt, lse):
+    T = c.T
+    return pl.pallas_call(
+        functools.partial(attend_back_kernel, c),
+        grid=(c.G,),
+        out_shape=jax.ShapeDtypeStruct((c.G, T, c.CW), bf16),
+        in_specs=[
+            pl.BlockSpec((1, T, c.CW), lambda g: (g, 0, 0)),
+            pl.BlockSpec((T, PAIR), lambda g: (0, g)),
+            pl.BlockSpec((T, PAIR), lambda g: (0, g)),
+            pl.BlockSpec((1, 8, T), lambda g: (g, 0, 0)),
+        ],
+        out_specs=pl.BlockSpec((1, T, c.CW), lambda g: (g, 0, 0)),
+        scratch_shapes=[pltpu.VMEM((T, PAIR), f32), pltpu.VMEM((T, PAIR), f32), pltpu.VMEM((8, T), f32)],
+        compiler_params=pltpu.CompilerParams(vmem_limit_bytes=VMEM_CAP),
+        name="attend_back",
+    )(qkv, att, datt, lse)
 
 
 precise = lax.Precision.HIGHEST
@@ -116,7 +726,7 @@
     return padded[target]
 
 
-def shards(
+def plain_shards(
     layer_inputs_matrix,
     assignment_indices,
     admitted_counts_matrix,
@@ -267,29 +877,77 @@
     )
 
 
+def shards(mesh, v, idx, caps, g1, wq, wo, g2, centers, up, down, dy):
+    T, D = v.shape
+    E = caps.shape[0]
+    c = Sizes(mesh, T, D, wq.shape[0], up.shape[2], E)
+    if not c.fits:
+        return plain_shards(v, idx, caps, g1, wq, wo, g2, centers, up, down, dy)
+    w = lax.axis_index("wide")
+    misc = jnp.concatenate(
+        [centers, jnp.zeros((c.slab, GAIN1 - E), bf16), g1[:, None], g2[:, None]], 1
+    )
+    cap = jnp.broadcast_to(jnp.pad(caps, (0, c.EP - E))[:, None], (c.EP, LANES))
+    res = forward_call(c, v, dy, idx.reshape(1, T), cap, wq, wo, misc, up, down)
+    wall, mall, qkv, lse, att, resid, sent, meta, mrow = res[:9]
+    ret, outp, ug, dg, cent = res[9:]
+    cent = cent[0:1]
+    outs = lax.psum_scatter(
+        outp.reshape(c.NW, c.NN, SLOT, D).transpose(1, 0, 2, 3).reshape(c.NN * c.S, D),
+        "narrow", scatter_dimension=0, tiled=True,
+    )
+    outs = lax.all_to_all(outs.reshape(c.NW, SLOT, D), "wide", split_axis=0, concat_axis=0, tiled=True)
+    slot, gate = meta[0:1], meta[1:2]
+    onehot = (jnp.arange(c.S, dtype=f32)[:, None] == slot).astype(bf16)
+    expert_tok = mm(onehot, outs.reshape(c.S, D), TN_)
+    mixed = (resid + gate.reshape(T, 1) * expert_tok).astype(bf16)
+    dn2 = mm(onehot, ret.reshape(c.S, D), TN_)
+    gain1, gain2 = mrow[GAIN1 : GAIN1 + 1], mrow[GAIN2 : GAIN2 + 1]
+    n2, r2 = layer_stats(resid)
+    gain2_part = jnp.sum(dn2 * n2, 0)
+    dn = dn2 * gain2
+    dres = dy.astype(f32) + r2 * (dn - jnp.mean(dn, 1, keepdims=True) - n2 * jnp.mean(dn * n2, 1, keepdims=True))
+    dbr = dres.astype(bf16)
+    out_part = mm(att, dbr, TN_)
+    wmat = wall.reshape(c.J, D, c.CW)
+    womat = jnp.concatenate([wmat[j] for j in range(c.G, c.J)], 1)
+    datt = mm(dbr, womat, NT_).astype(bf16)
+    dqkv = attend_back_call(c, qkv, att, datt, lse)
+    n1, r1 = layer_stats(v.astype(f32))
+    normed = (n1 * gain1).astype(bf16)
+
+    def flat(t):
+        return t.reshape(c.G, T, 3, PAIR).transpose(1, 2, 0, 3).reshape(T, 3 * D)
+
+    dq = flat(dqkv)
+    wqm = wmat[: c.G].reshape(c.G, D, 3, PAIR).transpose(1, 2, 0, 3).reshape(D, 3 * D)
+    qkv_part = mm(normed, dq, TN_)
+    dnm = mm(dq, wqm, NT_)
+    gain1_part = jnp.sum(dnm * n1, 0)
+    dm = dnm * gain1
+    tokens_grad = dres + r1 * (dm - jnp.mean(dm, 1, keepdims=True) - n1 * jnp.mean(dm * n1, 1, keepdims=True))
+    cent_part = jnp.where(jnp.arange(E)[None, :] == w, cent.reshape(D, 1), 0.0)
+    axes = ("wide", "narrow")
+    joined = jnp.concatenate([qkv_part, out_part], 1).astype(bf16)
+    joined = lax.psum_scatter(joined, axes, scatter_dimension=0, tiled=True).astype(f32)
+    small = jnp.concatenate([gain1_part[:, None], gain2_part[:, None], cent_part], 1)
+    small = lax.psum_scatter(small, axes, scatter_dimension=0, tiled=True)
+    return (
+        mixed, tokens_grad, small[:, 0], joined[:, : 3 * D], joined[:, 3 * D :],
+        small[:, 1], small[:, 2:], ug, dg,
+    )
+
+
 def solution(mesh):
+    both = ("wide", "narrow")
     in_specs = (
-        P(("wide", "narrow"), None),
-        P(("wide", "narrow"), None),
-        P(),
-        P(("wide", "narrow")),
-        P(("wide", "narrow"), None),
-        P(("wide", "narrow"), None),
-        P(("wide", "narrow")),
-        P(("wide", "narrow"), None),
-        P("wide", None, "narrow"),
-        P("wide", None, "narrow"),
-        P(("wide", "narrow"), None),
+        P(both, None), P(both, None), P(), P(both), P(both, None), P(both, None), P(both), P(both, None),
+        P("wide", None, "narrow"), P("wide", None, "narrow"), P(both, None),
     )
     out_specs = (
-        P(("wide", "narrow"), None),
-        P(("wide", "narrow"), None),
-        P(("wide", "narrow")),
-        P(("wide", "narrow"), None),
-        P(("wide", "narrow"), None),
-        P(("wide", "narrow")),
-        P(("wide", "narrow"), None),
-        P("wide", None, "narrow"),
-        P("wide", None, "narrow"),
-    )
-    return jax.shard_map(shards, mesh=mesh, in_specs=in_specs, out_specs=out_specs, check_vma=False)
+        P(both, None), P(both, None), P(both), P(both, None), P(both, None), P(both), P(both, None),
+        P("wide", None, "narrow"), P("wide", None, "narrow"),
+    )
+    return jax.shard_map(
+        functools.partial(shards, mesh), mesh=mesh, in_specs=in_specs, out_specs=out_specs, check_vma=False
+    )

time: 773 us -> 322 us (0.42); the launches traced: 762 us -> 320 us
  matrix products: 206 us -> 24.1 us
  waiting for transfers between devices: 206 us -> 29.4 us
  Pallas kernels: 0 us -> 147 us
  blocking collectives: 162 us -> 42.4 us
  other arithmetic: 93.3 us -> 11.9 us
  local copies, waits for them, and re-layouts: 68.4 us -> 45.2 us
    dot_general x20 -> x6, matrix products: 206 us -> 24.1 us  [mm(): return lax.dot_general(a, b, dims, preferred_element_type=f32)]
    pallas_call x0 -> x2, Pallas kernels: none -> 147 us  [the longest x1 122 us: forward_call(): pl.pallas_call(functools.partial(forward_kernel, c), out_shape=tuple((o[0...]
    reduce_scatter x4 -> x2, waiting for transfers between devices: 133 us -> 14 us  [the longest x1 14 us: shards(): lax.psum_scatter(joined, axes, scatter_dimension=0, tiled=True).astype(f32)]
    convert_element_type x6 -> x0, other arithmetic: 44.9 us -> none  [the longest x1 42.1 us: attend_backward(): grad_scores = (attn_probs * (grad_probs - jnp.sum(grad_probs * attn_probs...]
    all_gather x4 -> x0, waiting for transfers between devices: 42.9 us -> none  [the longest x1 21.7 us: shards(): gathered = lax.all_gather(local_rows, 'narrow', axis=0, tiled=True)]
    all_gather x1 -> x0, blocking collectives: 40.8 us -> none  [shards(): lax.all_gather(cluster_mean_columns, ('wide', 'narrow'), axis=0, tiled=True)]
    all_to_all x2 -> x0, blocking collectives: 40.6 us -> none  [the longest x1 20.3 us: shards(): lax.all_to_all(send_buf, 'wide', split_axis=0, concat_axis=0, tiled=True)]
    unnamed x2 -> x1, blocking collectives: 80.5 us -> 42.4 us
  transfers between devices with their start and end apart: 10 -> 3, of which waited for: 7 -> 2; matrix products, arithmetic and copies ran while one was open for 28% -> 20% of each run, Pallas kernels for 0% -> 8%
where the time goes in v1:
time: 322 us; the launch traced here: 320 us
  Pallas kernels  147 us (46%)
  local copies, waits for them, and re-layouts  45.2 us (14%)
  blocking collectives  42.4 us (13%)
  waiting for transfers between devices  29.4 us (9%)
  matrix products  24.1 us (7%)
  between operations  14.3 us (4%)
  other arithmetic  11.9 us (4%)
  starting transfers between devices  5.69 us (2%)
    pallas_call x1, Pallas kernels, forward_call(): pl.pallas_call(functools.partial(forward_kernel, c), out_shape=tuple((o[0...  122 us
    unnamed x1, blocking collectives  42.4 us
    pallas_call x1, Pallas kernels, attend_back_call(): pl.pallas_call(functools.partial(attend_back_kernel, c), grid=(c.G,), out...  25.6 us
    dot_general x6, matrix products, mm(): return lax.dot_general(a, b, dims, preferred_element_type=f32)  24.1 us
    all_to_all x1, waiting for transfers between devices, shards(): lax.all_to_all(outs.reshape(c.NW, SLOT, D), 'wide', split_axis=0, concat_...  15.3 us
    reduce_scatter x1, waiting for transfers between devices, shards(): lax.psum_scatter(joined, axes, scatter_dimension=0, tiled=True).astype(f32)  14 us
    reshape x1, local copies, waits for them, and re-layouts, shards(): wmat[:c.G].reshape(c.G, D, 3, PAIR).transpose(1, 2, 0, 3).reshape(D, 3 * D)  10.1 us
    unnamed x21, local copies, waits for them, and re-layouts  6.67 us
  transfers between devices with their start and end apart: 3, of which 2 were waited for; matrix products, arithmetic and copies ran while one was open for 20% of the time, Pallas kernels for 8%

profile of v1, /device:TPU:0, one launch (start us, length us, event | category | flops | bytes accessed | tf_op | source)
XLA Modules:
  0.0 320.1 jit_solution(5380464623604714498)
XLA Ops:
  7.2 0.0 reduce-scatter.4.cloned.1.call-start
  7.2 0.7 copy.44
  8.0 0.7 copy.45
  8.7 0.8 copy.43
  9.5 0.1 pad.8.clone
  9.6 0.7 pad_maximum_fusion.2.refs_6_
  10.2 1.3 broadcast_in_dim.53.refs_3_
  11.6 121.5 %forward.1 = (bf16[8,4,2,2,2,24,384]{6,5,4,3,2,1,0:T(8,128)(2,1)}, bf16[4,2,2,2,24,128]{5,4,3,2,1,0:T(8,128)(2,1)}, bf16[6,1024,384]{2,1,0:T(8,128)(2,1)}, f32[6...) custom-call(bf16[1024,768]{1,0:T(8,128)(2,1)} %refs_0_.1, ...), custom_call_target="tpu_custom_call" | custom-call | tf_op jit(solution)/shard_map/forward/pallas_call | solution.py:574
  133.1 3.4 %copy.46 = bf16[8,4,48,768]{3,2,0,1:T(8,128)(2,1)} copy(bf16[8,4,48,768]{3,2,1,0:T(8,128)(2,1)} %bitcast.50) | data formatting | bytes 4718592 | tf_op jit(solution)/shard_map/reshape | solution.py:896
  136.5 0.0 reduce-scatter.4.cloned.1.call-update
  136.6 0.2 reduce-scatter.6.cloned.1.call-start
  136.8 0.2 reduce_sum.90
  137.0 0.5 multiply_reduce_fusion.2
  137.5 0.8 slice_reduce_fusion.1
  138.4 0.8 fusion.32
  139.2 1.8 multiply_reduce_fusion
  141.1 1.5 fusion.31
  142.6 0.3 copy-done.5
  142.8 1.3 multiply_add_fusion
  144.1 2.6 convolution_convert_fusion.1.datt
  146.7 25.6 %attend_back.1 = bf16[6,1024,384]{2,1,0:T(8,128)(2,1)} custom-call(bf16[6,1024,384]{2,1,0:T(8,128)(2,1)} %get-tuple-element.26.qkv, bf16[1024,768]{1,0:T(8,128)(2,1)} %get-tuple-element.27.att, bf16[1024,768]{1,0:T(8,128)(2,1)} %convolution_convert_fusion.1.datt, f32[6,8,1024]{2,1,0:T(8,128)} %get-tuple-element.29.lse), custom_call_target="tpu_custom_call" | custom-call | tf_op jit(solution)/shard_map/attend_back/pallas_call | solution.py:604
  172.4 6.6 %copy.48 = bf16[6,1024,384]{1,2,0:T(8,128)(2,1)} copy(bf16[6,1024,384]{2,1,0:T(8,128)(2,1)} %attend_back.1) | data formatting | bytes 9437184 | tf_op jit(solution)/shard_map/attend_back/pallas_call | solution.py:604
  179.0 3.2 copy.57
  182.2 0.0 copy-start.4
  182.2 0.3 convert_reduce_fusion
  182.5 0.6 fusion.15
  183.1 1.0 copy-done.4
  184.1 1.5 convolution_convert_fusion.2
  185.6 4.8 %convolution_convert_fusion = bf16[768,2304]{1,0:T(8,128)(2,1)S(1)} fusion(bf16[1024,2304]{0,1:T(8,128)(2,1)S(1)} %bitcast.49, bf16[1024,768]{1,0:T(8,128)(2,1)S(1)} %copy-done.2, f32[768]{0:T(1024)S(1)} %get-tuple-element.39, f32[1024]{0:T(1024)S(1)} %add_rsqrt_fusion, f32[1024]{0:T(1024)S(1)} %broadcast_multiply_fusion.2), kind=kOutput, calls=%fused_computation | convolution fusion | flops 3629580288 | bytes 9841664 | tf_op jit(solution)/shard_map/dot_general | solution.py:30
  190.4 2.8 pad_maximum_fusion
  193.2 0.0 reduce-scatter.6.cloned.1.call-update
  193.3 4.2 %slice.47 = bf16[6,4,2,2,2,24,384]{6,5,4,3,2,1,0:T(8,128)(2,1)} slice(bf16[8,4,2,2,2,24,384]{6,5,4,3,2,1,0:T(8,128)(2,1)} %get-tuple-element.28), slice={[0:6], [0:4], [0:2], [0:2], [0:2], [0:24], [0:384]} | slice | bytes 7077888 | tf_op jit(solution)/shard_map/slice | solution.py:923
  197.5 10.1 %reshape.110 = bf16[6,768,3,128]{3,2,1,0:T(4,128)(2,1)} reshape(bf16[6,4,2,2,2,24,384]{6,5,4,3,2,1,0:T(8,128)(2,1)} %slice.47) | data formatting | bytes 7077888 | tf_op jit(solution)/shard_map/reshape | solution.py:923
  207.5 10.1 %fusion.13 = (f32[768]{0:T(1024)S(1)}, f32[1024]{0:T(1024)S(1)}, f32[1024]{0:T(1024)S(1)}, f32[1024,768,1,1]{1,0,3,2:T(8,128)}) fusion(bf16[1024,768]{1,0:T(8,128)(2,1)S(1)} %copy-done.2, f32[1024]{0:T(1024)S(1)} %add_rsqrt_fusion, f32[1024]{0:T(1024)S(1)} %broadcast_multiply_fusion.2, f32[768]{0:T(1024)S(1)} %get-tuple-element.39, ...), kind=kOutput, calls=%fused_computation.17 | convolution fusion | flops 3630953728 | bytes 12998656 | tf_op jit(solution)/shard_map/dot_general | solution.py:30
  217.7 0.8 slice_reduce_fusion
  218.4 0.1 broadcast_select_fusion
  218.5 42.4 %all-reduce = f32[768,10]{0,1:T(8,128)S(1)} all-reduce(f32[768,10]{0,1:T(8,128)S(1)} %pad_maximum_fusion.1), channel_id=3, replica_groups=mesh['wide'=8,'narrow'=4] {'wide','narrow'}, use_global_device_ids=true, to_apply=%region_11.12.clone | all-reduce | flops 7680 | bytes 61440
  260.9 0.7 dynamic-slice.3
  261.6 5.4 %all-to-all-start = ((bf16[8,48,768]{2,1,0:T(8,128)(2,1)}), bf16[8,48,768]{2,1,0:T(8,128)(2,1)}, u32[]{:S(2)}, u32[]{:S(2)}) async-start(bf16[8,48,768]{2,1,0:T(8,128)(2,1)} %bitcast.51), calls=%async_computation.1 | async-start | bytes 1179648 | tf_op jit(solution)/shard_map/all_to_all | solution.py:899
  267.0 0.6 dynamic-slice_bitcast_fusion
  267.6 5.4 %fusion.12 = f32[1024,768]{1,0:T(8,128)} fusion(f32[1024,768]{1,0:T(8,128)} %copy-done.3, bf16[1024,768]{1,0:T(8,128)(2,1)} %refs_0_.1, f32[1024,768,1,1]{1,0,3,2:T(8,128)} %get-tuple-element.48, f32[1024]{0:T(1024)S(1)} %broadcast_multiply_fusion, f32[1024]{0:T(1024)S(1)} %broadcast_multiply_fusion.1, f32[768]{0:T(1024)S(1)} %get-tuple-element.39, ...), kind=kLoop, calls=%fused_computation.16 | loop fusion | flops 7077888 | bytes 11029504 | tf_op jit(solution)/shard_map/add | solution.py:928
  273.1 15.3 %all-to-all-done = bf16[8,48,768]{2,1,0:T(8,128)(2,1)} async-done(((bf16[8,48,768]{2,1,0:T(8,128)(2,1)}), bf16[8,48,768]{2,1,0:T(8,128)(2,1)}, u32[]{:S(2)}, u32[]{:S(2)}) %all-to-all-start) | async-done | bytes 589856 | tf_op jit(solution)/shard_map/all_to_all | solution.py:899
  288.4 3.3 %add_convert_fusion = bf16[1024,768]{1,0:T(8,128)(2,1)} fusion(f32[1024,768]{1,0:T(8,128)S(1)} %copy-done.1, bf16[384,768]{1,0:T(8,128)(2,1)} %bitcast.9, f32[1024]{0:T(1024)S(1)} %bitcast.56, f32[1024]{0:T(1024)S(1)} %bitcast.55), kind=kOutput, calls=%fused_computation.25 | convolution fusion | flops 606732288 | bytes 5316608 | tf_op jit(solution)/shard_map/dot_general | solution.py:30
  291.7 14.0 %reduce-scatter.6.cloned.1.call-done = bf16[24,3072]{1,0:T(8,128)(2,1)} async-done(((bf16[768,3072]{1,0:T(8,128)(2,1)}), bf16[24,3072]{1,0:T(8,128)(2,1)}) %reduce-scatter.6.cloned.1.call-update) | async-done | bytes 147472 | tf_op jit(solution)/shard_map/reduce_scatter | solution.py:932
  305.6 1.4 slice.56
  307.1 1.6 slice.55
  308.6 3.2 %copy.77 = f32[1,768,768]{2,1,0:T(8,128)} copy(f32[1,768,768]{2,1,0:T(8,128)} %get-tuple-element.67) | data formatting | bytes 4718592
  311.9 1.4 copy.78
  (28 shorter events, 0.1 us)
Async XLA Ops:
  7.2 254.4 %reduce-scatter.4.cloned.1.call-start = ((), (), s32[]{:S(2)}) async-start(), calls=%async_computation.3 | async-start | bytes 2949120 | tf_op jit(solution)/shard_map/reduce_scatter | solution.py:895
  133.1 3.7 %copy-start = (f32[1024,768]{1,0:T(8,128)S(1)}, f32[1024,768]{1,0:T(8,128)}, u32[]{:S(2)}) copy-start(f32[1024,768]{1,0:T(8,128)} %get-tuple-element.21) | copy-start | bytes 9437188
  136.6 169.1 %reduce-scatter.6.cloned.1.call-start = ((), (), s32[]{:S(2)}) async-start(), calls=%async_computation.4 | async-start | bytes 4866048 | tf_op jit(solution)/shard_map/reduce_scatter | solution.py:932
  137.0 2.2 copy-start.8
  141.1 1.8 copy-start.5
  144.1 2.6 copy-start.3
  179.0 3.2 copy-start.2
  179.0 4.1 %copy-start.7 = (bf16[1024,768]{1,0:T(8,128)(2,1)S(1)}, bf16[1024,768]{1,0:T(8,128)(2,1)}, u32[]{:S(2)}) copy-start(bf16[1024,768]{1,0:T(8,128)(2,1)} %get-tuple-element.27.att) | copy-start | bytes 4718596
  182.2 1.9 copy-start.4
  261.6 26.8 %all-to-all-start = ((bf16[8,48,768]{2,1,0:T(8,128)(2,1)}), bf16[8,48,768]{2,1,0:T(8,128)(2,1)}, u32[]{:S(2)}, u32[]{:S(2)}) async-start(bf16[8,48,768]{2,1,0:T(8,128)(2,1)} %bitcast.51), calls=%async_computation.1 | async-start | bytes 1179648 | tf_op jit(solution)/shard_map/all_to_all | solution.py:899
  267.6 20.8 %copy-start.1 = (f32[1024,768]{1,0:T(8,128)S(1)}, f32[1024,768]{1,0:T(8,128)}, u32[]{:S(2)}) copy-start(f32[1024,768]{1,0:T(8,128)} %get-tuple-element.21) | copy-start | bytes 9437188
  291.6 20.2 %copy-start.6 = (f32[1,768,768]{2,1,0:T(8,128)S(1)}, f32[1,768,768]{2,1,0:T(8,128)}, u32[]{:S(2)}) copy-start(f32[1,768,768]{2,1,0:T(8,128)} %get-tuple-element.68) | copy-start | bytes 7077892
Sparse Core Ops, SparseCore 0:
  136.7 34.1 reduce-scatter.3
  193.4 112.2 reduce-scatter.5

commit v2 on v1

--- a/solution.py
+++ b/solution.py
@@ -584,38 +584,366 @@
     )(v, dy, idx, cap, wq, wo, misc, up, down)
 
 
-def attend_back_kernel(c, qkv, att, datt, lse, dqkv, dk, dv, prod):
-    full = jnp.transpose(datt[...].astype(f32) * att[...].astype(f32))
-    prod[0:1, :] = jnp.sum(full[0:HD], 0, keepdims=True)
-    prod[1:2, :] = jnp.sum(full[HD:], 0, keepdims=True)
-
-    def put_dq(rows, val):
-        dqkv[0, rows, 0:PAIR] = val
-
-    blocks = c.T // QB
-    for i in reversed(range(blocks)):
-        attend_rows_back(qkv.at[0], att, datt, lse.at[0], i, i == blocks - 1, prod, dk, dv, put_dq)
-    dqkv[0, :, PAIR : 2 * PAIR] = dk[...].astype(bf16)
-    dqkv[0, :, 2 * PAIR :] = dv[...].astype(bf16)
-
-
-def attend_back_call(c, qkv, att, datt, lse):
-    T = c.T
+def backward_kernel(c, *refs):
+    (v_hbm, dy_hbm, qkv_hbm, lse_hbm, att_hbm, resid_hbm, wall, ret_hbm, outp_hbm, mrow, meta, cent) = refs[:12]
+    (mixed_out, tok_out, qg_out, og_out, small_out) = refs[12:17]
+    (v, dy, qkv, lse, att, resid, wbuf, wmat, ret, oh, normt, dbr, datt, dnm, dqkv, dk, dv, prod, rowbuf,
+     part, lc, lx, got, mixed,
+     gb, la, lb, lxx, lz, sgb, sla, slb, slx, slz,
+     in_sem, q_sem, out_sem, os_, orv, ows, owr, rs_, rr, tokacc) = refs[17:]
+    A, X, NW, NN, T, D, CW, G, J = c.A, c.X, c.NW, c.NN, c.T, c.D, c.CW, c.G, c.J
+    H = J - G
+    w, n, a, b, x, cc = place(c)
+    blocks = T // QB
+
+    loads = [
+        (ret_hbm, ret), (resid_hbm, resid), (dy_hbm, dy), (att_hbm, att), (v_hbm, v), (lse_hbm, lse),
+    ]
+    for i, (s, d) in enumerate(loads):
+        pltpu.make_async_copy(s, d, in_sem.at[i]).start()
+    own_part = pltpu.make_async_copy(outp_hbm.at[:, :, cc], part, in_sem.at[6])
+    own_part.start()
+
+    def load_wait(i):
+        wait_bytes(loads[i][1], in_sem.at[i])
+
+    def fetch_w(j, slot_):
+        pltpu.make_async_copy(wall.at[j], wbuf.at[slot_], q_sem.at[0, slot_]).start()
+
+    def take_w(slot_, at):
+        wait_bytes(wbuf.at[slot_], q_sem.at[0, slot_])
+        wmat[at] = wbuf[slot_].reshape(D, CW)
+
+    def fetch_qkv(g, slot_):
+        pltpu.make_async_copy(qkv_hbm.at[g], qkv.at[slot_], q_sem.at[1, slot_]).start()
+
+    for h in range(H):
+        fetch_w(G + h, h)
+    fetch_qkv(0, 0)
+    met = greet(c, w, n)
+
+    slot, gate = meta[0:1, :], meta[1:2, :]
+    hits = lax.broadcasted_iota(jnp.int32, (c.S, T), 0).astype(f32) == slot
+    oh[...] = hits.astype(bf16)
+    gain1, gain2 = mrow[GAIN1 : GAIN1 + 1, :], mrow[GAIN2 : GAIN2 + 1, :]
+    load_wait(0)
+    dnm[...] = mm(oh[...], ret[...].reshape(c.S, D), TN_)
+    oh[...] = jnp.where(hits, gate, 0.0).astype(bf16)
+    met()
+    push(outp_hbm.at[:, :, 1 - cc], lc, os_.at[0], orv.at[0], narrow=x * 2 + 1 - cc)
+    load_wait(1)
+    load_wait(2)
+    rowbuf[...] = jnp.zeros_like(rowbuf)
+    rowbuf[pl.ds(w, 1), :] = cent[0:1, :]
+
+    def norm2_back(i, acc):
+        rows = pl.ds(i * QB, QB)
+        n2, r2 = layer_stats(resid[rows, :])
+        dn2 = dnm[rows, :]
+        dn = dn2 * gain2
+        step = r2 * (dn - jnp.mean(dn, 1, keepdims=True) - n2 * jnp.mean(dn * n2, 1, keepdims=True))
+        dres = dy[rows, :].astype(f32) + step
+        dnm[rows, :] = dres
+        dbr[rows, :] = dres.astype(bf16)
+        return acc + jnp.sum(dn2 * n2, 0, keepdims=True)
+
+    rowbuf[GAIN2 : GAIN2 + 1, :] = lax.fori_loop(0, blocks, norm2_back, jnp.zeros((1, D), f32))
+    load_wait(3)
+
+    big = (gb, la, lb, lxx, lz, 0)
+    tiny = (sgb, sla, slb, slx, slz, J)
+
+    def add(p, q):
+        return (p.astype(f32) + q.astype(f32)).astype(bf16)
+
+    def ra(t, j):
+        push(t[0].at[j, :, :, :, 1 - cc], t[1].at[j], rs_.at[0, t[5] + j], rr.at[0, t[5] + j], narrow=x * 2 + 1 - cc)
+
+    def rb(t, j):
+        wait_bytes(t[1].at[j], rr.at[0, t[5] + j])
+        t[0][j, :, :, :, cc] = add(t[0][j, :, :, :, cc], t[1][j])
+        push(t[0].at[j, :, 1 - b, :, cc], t[2].at[j], rs_.at[1, t[5] + j], rr.at[1, t[5] + j], wide=a * 2 + 1 - b)
+
+    def rc(t, j):
+        wait_bytes(t[2].at[j], rr.at[1, t[5] + j])
+        t[0][j, :, b, :, cc] = add(t[0][j, :, b, :, cc], t[2][j])
+        for k in range(1, X):
+            x2 = lax.rem(x + k, X)
+            push(t[0].at[j, :, b, x2, cc], t[3].at[j, x], rs_.at[2, t[5] + j], rr.at[2, t[5] + j], narrow=x2 * 2 + cc)
+
+    def rd(t, j):
+        wait_bytes(t[3].at[j, pl.ds(0, X - 1)], rr.at[2, t[5] + j])
+        total = t[0][j, :, b, x, cc].astype(f32)
+        for k in range(1, X):
+            total = total + t[3][j, lax.rem(x + k, X)].astype(f32)
+        t[0][j, :, b, x, cc] = total.astype(bf16)
+        for k in range(1, A):
+            a2 = lax.rem(a + k, A)
+            push(t[0].at[j, a2, b, x, cc], t[4].at[j, a], rs_.at[3, t[5] + j], rr.at[3, t[5] + j], wide=a2 * 2 + b)
+
+    def rf(t, j):
+        wait_bytes(t[4].at[j, pl.ds(0, A - 1)], rr.at[3, t[5] + j])
+        total = t[0][j, a, b, x, cc].astype(f32)
+        for k in range(1, A):
+            total = total + t[4][j, lax.rem(a + k, A)].astype(f32)
+        return total
+
+    def rf_w(j):
+        og_out[:, j * CW : (j + 1) * CW] = rf(big, j)
+
+    def rf_q(g):
+        total = rf(big, H + g)
+        for p in range(3):
+            qg_out[:, pl.ds(pl.multiple_of(p * D + g * PAIR, PAIR), PAIR)] = total[:, p * PAIR : (p + 1) * PAIR]
+
+    for h in range(H):
+        gb[h] = mm(att[...], dbr[:, h * CW : (h + 1) * CW], TN_).astype(bf16).reshape(A, 2, X, 2, c.slab, CW)
+        ra(big, h)
+
+    for h in range(H):
+        take_w(h, h)
+
+    def out_back(i, _):
+        rows = pl.ds(i * QB, QB)
+        total = mm(dbr[rows, 0:CW], wmat[0], NT_)
+        for h in range(1, H):
+            total = total + mm(dbr[rows, h * CW : (h + 1) * CW], wmat[h], NT_)
+        datt[rows, :] = total.astype(bf16)
+        return 0
+
+    lax.fori_loop(0, blocks, out_back, 0)
+    fetch_w(0, 0)
+    load_wait(4)
+
+    def norm1(i, _):
+        rows = pl.ds(i * QB, QB)
+        val = (layer_stats(v[rows, :].astype(f32))[0] * gain1).astype(bf16)
+        normt[:, pl.ds(pl.multiple_of(i * QB, QB), QB)] = jnp.transpose(val)
+        return 0
+
+    lax.fori_loop(0, blocks, norm1, 0)
+    for h in range(H):
+        rb(big, h)
+    load_wait(5)
+    own_part.wait()
+
+    def o_x(i):
+        for k in range(1, X):
+            x2 = lax.rem(x + k, X)
+            push(part.at[i, x2], lx.at[i, x], os_.at[1 + i], orv.at[1 + i], narrow=x2 * 2 + cc)
+
+    def o_w(i):
+        wait_bytes(lx.at[i, pl.ds(0, X - 1)], orv.at[1 + i])
+        total = part[i, x].astype(f32)
+        for k in range(1, X):
+            total = total + lx[i, lax.rem(x + k, X)].astype(f32)
+        part[i, x] = total.astype(bf16)
+
+        @pl.when(i != w)
+        def _():
+            push(part.at[i, x], got.at[w], ows.at[i], owr.at[lax.rem(w - i + NW, NW)], wide=i)
+
+        @pl.when(i == w)
+        def _():
+            got[w] = part[w, x]
+
+    wait_bytes(lc, orv.at[0])
+
+    def merge(i, _):
+        part[i] = add(part[i], lc[i])
+        return 0
+
+    lax.fori_loop(0, NW, merge, 0)
+    per = -(-NW // 4)
+
+    def spread(fn, step):
+        for k in range(per):
+            i = lax.rem(w + step * per + k, NW)
+
+            @pl.when(step * per + k < NW)
+            def _():
+                fn(i)
+
+    def pair(g, _):
+        s_ = lax.rem(g, 2)
+
+        @pl.when(g + 1 < G)
+        def _():
+            fetch_w(g + 1, 1 - s_)
+            fetch_qkv(g + 1, 1 - s_)
+
+        wait_bytes(qkv.at[s_], q_sem.at[1, s_])
+        lanes = pl.ds(pl.multiple_of(g * PAIR, PAIR), PAIR)
+        att_g, datt_g = att.at[:, lanes], datt.at[:, lanes]
+        full = jnp.transpose(datt_g[...].astype(f32) * att_g[...].astype(f32))
+        prod[0:1, :] = jnp.sum(full[0:HD], 0, keepdims=True)
+        prod[1:2, :] = jnp.sum(full[HD:], 0, keepdims=True)
+
+        def put_dq(rows, val):
+            dqkv[rows, 0:PAIR] = val
+
+        for i in reversed(range(blocks)):
+            attend_rows_back(qkv.at[s_], att_g, datt_g, lse.at[g], i, i == blocks - 1, prod, dk, dv, put_dq)
+            if i == blocks - 1:
+                @pl.when(g >= 1)
+                def _():
+                    rb(big, g + H - 1)
+
+                rc(big, g + H - 2)
+
+                @pl.when(g + H >= 3)
+                def _():
+                    rd(big, g + H - 3)
+
+                @pl.when(g < 4)
+                def _():
+                    spread(o_x, g)
+
+                @pl.when(g >= 2)
+                def _():
+                    spread(o_w, g - 2)
+
+        dqkv[:, PAIR : 2 * PAIR] = dk[...].astype(bf16)
+        dqkv[:, 2 * PAIR :] = dv[...].astype(bf16)
+        gb[H + g] = mm(normt[...], dqkv[...]).astype(bf16).reshape(A, 2, X, 2, c.slab, CW)
+        ra(big, H + g)
+        take_w(s_, 0)
+
+        def back(i, _):
+            rows = pl.ds(i * QB, QB)
+            val = mm(dqkv[rows, :], wmat[0], NT_)
+
+            @pl.when(g == 0)
+            def _():
+                tokacc[rows, :] = val
+
+            @pl.when(g > 0)
+            def _():
+                tokacc[rows, :] += val
+
+            return 0
+
+        lax.fori_loop(0, blocks, back, 0)
+        return 0
+
+    lax.fori_loop(0, G, pair, 0)
+
+    rb(big, J - 1)
+    def norm1_back(i, acc):
+        rows = pl.ds(i * QB, QB)
+        n1, r1 = layer_stats(v[rows, :].astype(f32))
+        dm0 = tokacc[rows, :]
+        dm = dm0 * gain1
+        step = r1 * (dm - jnp.mean(dm, 1, keepdims=True) - n1 * jnp.mean(dm * n1, 1, keepdims=True))
+        dnm[rows, :] = dnm[rows, :] + step
+        return acc + jnp.sum(dm0 * n1, 0, keepdims=True)
+
+    rowbuf[GAIN1 : GAIN1 + 1, :] = lax.fori_loop(0, blocks, norm1_back, jnp.zeros((1, D), f32))
+    tok_copy = pltpu.make_async_copy(dnm, tok_out, out_sem.at[0])
+    tok_copy.start()
+    sgb[0] = jnp.transpose(rowbuf[...]).astype(bf16).reshape(A, 2, X, 2, c.slab, LANES)
+    ra(tiny, 0)
+    rc(big, J - 2)
+    rd(big, J - 3)
+    rb(tiny, 0)
+    rc(big, J - 1)
+
+    def o_wait(k, _):
+        wait_bytes(got.at[0], owr.at[k])
+        return 0
+
+    lax.fori_loop(1, NW, o_wait, 0)
+    rd(big, J - 2)
+    rc(tiny, 0)
+
+    def mix(i, _):
+        cols = pl.ds(pl.multiple_of(i * QB, QB), QB)
+        rows = pl.ds(i * QB, QB)
+        mixed[rows, :] = (resid[rows, :] + mm(oh[:, cols], got[...].reshape(c.S, D), TN_)).astype(bf16)
+        return 0
+
+    lax.fori_loop(0, blocks, mix, 0)
+    mix_copy = pltpu.make_async_copy(mixed, mixed_out, out_sem.at[1])
+    mix_copy.start()
+    rd(big, J - 1)
+    rd(tiny, 0)
+    for h in range(H):
+        rf_w(h)
+
+    def fin(g, _):
+        rf_q(g)
+        return 0
+
+    lax.fori_loop(0, G, fin, 0)
+    small_out[...] = rf(tiny, 0)
+
+    wait_bytes(lc, os_.at[0])
+
+    def drain(i, _):
+        wait_bytes(lx.at[i, pl.ds(0, X - 1)], os_.at[1 + i])
+
+        @pl.when(i != w)
+        def _():
+            wait_bytes(got.at[0], ows.at[i])
+
+        return 0
+
+    lax.fori_loop(0, NW, drain, 0)
+
+    def drain_sums(t, j):
+        for q in range(2):
+            wait_bytes(t[1 + q].at[j], rs_.at[q, t[5] + j])
+        wait_bytes(t[3].at[j, pl.ds(0, X - 1)], rs_.at[2, t[5] + j])
+        wait_bytes(t[4].at[j, pl.ds(0, A - 1)], rs_.at[3, t[5] + j])
+
+    def drain_big(j, _):
+        drain_sums(big, j)
+        return 0
+
+    lax.fori_loop(0, J, drain_big, 0)
+    drain_sums(tiny, 0)
+    tok_copy.wait()
+    mix_copy.wait()
+
+
+def backward_call(c, v, dy, qkv, lse, att, resid, wall, ret, outp, mrow, meta, cent):
+    T, D, CW, G, J, NW, NN, A, X, L = c.T, c.D, c.CW, c.G, c.J, c.NW, c.NN, c.A, c.X, c.slab
+    any_ = pl.BlockSpec(memory_space=pl.ANY)
+    vm = pl.BlockSpec(memory_space=pltpu.VMEM)
+    sds = jax.ShapeDtypeStruct
+    dma, V = pltpu.SemaphoreType.DMA, pltpu.VMEM
+
+    def sums(k, width):
+        return [
+            V((k, A, 2, X, 2, L, width), bf16), V((k, A, 2, X, L, width), bf16), V((k, A, X, L, width), bf16),
+            V((k, X, A, L, width), bf16), V((k, A, L, width), bf16),
+        ]
+
+    scratch = [
+        V((T, D), bf16), V((T, D), bf16), V((2, T, CW), bf16), V((G, 8, T), f32), V((T, D), bf16), V((T, D), f32),
+        V((2, A, 2, X, 2, L, CW), bf16), V((J - G, D, CW), bf16), V((NW, SLOT, D), bf16), V((c.S, T), bf16),
+        V((D, T), bf16), V((T, D), bf16), V((T, D), bf16), V((T, D), f32), V((T, CW), bf16),
+        V((T, PAIR), f32), V((T, PAIR), f32), V((8, T), f32), V((LANES, D), f32),
+        V((NW, X, SLOT, D), bf16), V((NW, X, SLOT, D), bf16), V((NW, X, SLOT, D), bf16), V((NW, SLOT, D), bf16),
+        V((T, D), bf16),
+    ] + sums(J, CW) + sums(1, LANES) + [
+        dma((7,)), dma((2, 2)), dma((2,)), dma((NW + 1,)), dma((NW + 1,)), dma((NW,)), dma((NW,)),
+        dma((4, J + 1)), dma((4, J + 1)),
+        V((T, D), f32),
+    ]
     return pl.pallas_call(
-        functools.partial(attend_back_kernel, c),
-        grid=(c.G,),
-        out_shape=jax.ShapeDtypeStruct((c.G, T, c.CW), bf16),
-        in_specs=[
-            pl.BlockSpec((1, T, c.CW), lambda g: (g, 0, 0)),
-            pl.BlockSpec((T, PAIR), lambda g: (0, g)),
-            pl.BlockSpec((T, PAIR), lambda g: (0, g)),
-            pl.BlockSpec((1, 8, T), lambda g: (g, 0, 0)),
-        ],
-        out_specs=pl.BlockSpec((1, T, c.CW), lambda g: (g, 0, 0)),
-        scratch_shapes=[pltpu.VMEM((T, PAIR), f32), pltpu.VMEM((T, PAIR), f32), pltpu.VMEM((8, T), f32)],
-        compiler_params=pltpu.CompilerParams(vmem_limit_bytes=VMEM_CAP),
-        name="attend_back",
-    )(qkv, att, datt, lse)
+        functools.partial(backward_kernel, c),
+        out_shape=(
+            sds((T, D), bf16), sds((T, D), f32), sds((L, 3 * D), f32), sds((L, D), f32), sds((L, LANES), f32),
+        ),
+        in_specs=[any_] * 9 + [vm] * 3,
+        out_specs=(any_, any_, vm, vm, vm),
+        scratch_shapes=scratch,
+        compiler_params=pltpu.CompilerParams(
+            collective_id=1, has_side_effects=True, vmem_limit_bytes=VMEM_CAP
+        ),
+        name="backward",
+    )(v, dy, qkv, lse, att, resid, wall, ret, outp, mrow, meta, cent)
 
 
 precise = lax.Precision.HIGHEST
@@ -891,50 +1219,11 @@
     res = forward_call(c, v, dy, idx.reshape(1, T), cap, wq, wo, misc, up, down)
     wall, mall, qkv, lse, att, resid, sent, meta, mrow = res[:9]
     ret, outp, ug, dg, cent = res[9:]
-    cent = cent[0:1]
-    outs = lax.psum_scatter(
-        outp.reshape(c.NW, c.NN, SLOT, D).transpose(1, 0, 2, 3).reshape(c.NN * c.S, D),
-        "narrow", scatter_dimension=0, tiled=True,
-    )
-    outs = lax.all_to_all(outs.reshape(c.NW, SLOT, D), "wide", split_axis=0, concat_axis=0, tiled=True)
-    slot, gate = meta[0:1], meta[1:2]
-    onehot = (jnp.arange(c.S, dtype=f32)[:, None] == slot).astype(bf16)
-    expert_tok = mm(onehot, outs.reshape(c.S, D), TN_)
-    mixed = (resid + gate.reshape(T, 1) * expert_tok).astype(bf16)
-    dn2 = mm(onehot, ret.reshape(c.S, D), TN_)
-    gain1, gain2 = mrow[GAIN1 : GAIN1 + 1], mrow[GAIN2 : GAIN2 + 1]
-    n2, r2 = layer_stats(resid)
-    gain2_part = jnp.sum(dn2 * n2, 0)
-    dn = dn2 * gain2
-    dres = dy.astype(f32) + r2 * (dn - jnp.mean(dn, 1, keepdims=True) - n2 * jnp.mean(dn * n2, 1, keepdims=True))
-    dbr = dres.astype(bf16)
-    out_part = mm(att, dbr, TN_)
-    wmat = wall.reshape(c.J, D, c.CW)
-    womat = jnp.concatenate([wmat[j] for j in range(c.G, c.J)], 1)
-    datt = mm(dbr, womat, NT_).astype(bf16)
-    dqkv = attend_back_call(c, qkv, att, datt, lse)
-    n1, r1 = layer_stats(v.astype(f32))
-    normed = (n1 * gain1).astype(bf16)
-
-    def flat(t):
-        return t.reshape(c.G, T, 3, PAIR).transpose(1, 2, 0, 3).reshape(T, 3 * D)
-
-    dq = flat(dqkv)
-    wqm = wmat[: c.G].reshape(c.G, D, 3, PAIR).transpose(1, 2, 0, 3).reshape(D, 3 * D)
-    qkv_part = mm(normed, dq, TN_)
-    dnm = mm(dq, wqm, NT_)
-    gain1_part = jnp.sum(dnm * n1, 0)
-    dm = dnm * gain1
-    tokens_grad = dres + r1 * (dm - jnp.mean(dm, 1, keepdims=True) - n1 * jnp.mean(dm * n1, 1, keepdims=True))
-    cent_part = jnp.where(jnp.arange(E)[None, :] == w, cent.reshape(D, 1), 0.0)
-    axes = ("wide", "narrow")
-    joined = jnp.concatenate([qkv_part, out_part], 1).astype(bf16)
-    joined = lax.psum_scatter(joined, axes, scatter_dimension=0, tiled=True).astype(f32)
-    small = jnp.concatenate([gain1_part[:, None], gain2_part[:, None], cent_part], 1)
-    small = lax.psum_scatter(small, axes, scatter_dimension=0, tiled=True)
+    mixed, tokens_grad, qg, og, small = backward_call(
+        c, v, dy, qkv, lse, att, resid, wall, ret, outp, mrow, meta, cent
+    )
     return (
-        mixed, tokens_grad, small[:, 0], joined[:, : 3 * D], joined[:, 3 * D :],
-        small[:, 1], small[:, 2:], ug, dg,
+        mixed, tokens_grad, small[:, GAIN1], qg, og, small[:, GAIN2], small[:, :E], ug, dg,
     )
 
 

time: 322 us -> 216 us (0.67)
  Pallas kernels: 147 us -> 198 us
  blocking collectives: 42.4 us -> 0 us
  waiting for transfers between devices: 29.4 us -> 0 us
  local copies, waits for them, and re-layouts: 45.2 us -> 16.2 us
  matrix products: 24.1 us -> 0 us
  between operations: 14.3 us -> 0.69 us
  other arithmetic: 11.9 us -> 0.67 us
  starting transfers between devices: 5.69 us -> 0 us
    pallas_call x1, Pallas kernels: 25.6 us -> 76 us  [backward_call(): pl.pallas_call(functools.partial(backward_kernel, c), out_shape=(sds((T,...]
    unnamed x1 -> x0, blocking collectives: 42.4 us -> none
    dot_general x6 -> x0, matrix products: 24.1 us -> none  [mm(): return lax.dot_general(a, b, dims, preferred_element_type=f32)]
    all_to_all x1 -> x0, waiting for transfers between devices: 15.3 us -> none  [shards(): lax.all_to_all(outs.reshape(c.NW, SLOT, D), 'wide', split_axis=0, concat_...]
    reduce_scatter x2 -> x0, waiting for transfers between devices: 14 us -> none  [the longest x1 14 us: shards(): lax.psum_scatter(joined, axes, scatter_dimension=0, tiled=True).astype(f32)]
    reshape x2 -> x0, local copies, waits for them, and re-layouts: 13.5 us -> none  [the longest x1 10.1 us: shards(): wmat[:c.G].reshape(c.G, D, 3, PAIR).transpose(1, 2, 0, 3).reshape(D, 3 * D)]
    slice x8 -> x1, local copies, waits for them, and re-layouts: 11.8 us -> 1.58 us  [shards(): small[:, GAIN2]]
    add x2 -> x0, other arithmetic: 6.72 us -> none  [the longest x1 5.44 us: shards(): dres + r1 * (dm - jnp.mean(dm, 1, keepdims=True) - n1 * jnp.mean(dm * n1,...]
  transfers between devices with their start and end apart: 3 -> 0, of which waited for: 2 -> 0; matrix products, arithmetic and copies ran while one was open for 20% -> 0% of each run, Pallas kernels for 8% -> 0%
where the time goes in v2:
time: 216 us; the launch traced here: 215 us
  Pallas kernels  198 us (92%)
  local copies, waits for them, and re-layouts  16.2 us (8%)
    pallas_call x1, Pallas kernels, forward_call(): pl.pallas_call(functools.partial(forward_kernel, c), out_shape=tuple((o[0...  122 us
    pallas_call x1, Pallas kernels, backward_call(): pl.pallas_call(functools.partial(backward_kernel, c), out_shape=(sds((T,...  76 us
    unnamed x18, local copies, waits for them, and re-layouts  11.7 us

profile of v2, /device:TPU:0, one launch (start us, length us, event | category | flops | bytes accessed | tf_op | source)
XLA Modules:
  0.0 215.1 jit_solution(14372583272045292166)
XLA Ops:
  0.7 0.1 pad.1.clone
  0.7 1.3 broadcast_in_dim.15.refs_3_
  2.0 0.7 copy.25
  2.8 0.7 copy.26
  3.5 0.8 copy.24
  4.3 0.7 pad_maximum_fusion.refs_6_
  5.0 121.5 %forward.1 = (bf16[8,4,2,2,2,24,384]{6,5,4,3,2,1,0:T(8,128)(2,1)}, bf16[4,2,2,2,24,128]{5,4,3,2,1,0:T(8,128)(2,1)}, bf16[6,1024,384]{2,1,0:T(8,128)(2,1)}, f32[6...) custom-call(bf16[1024,768]{1,0:T(8,128)(2,1)} %refs_0_.3, ...), custom_call_target="tpu_custom_call" | custom-call | tf_op jit(solution)/shard_map/forward/pallas_call | solution.py:574
  126.5 76.0 %backward.1 = (bf16[1024,768]{1,0:T(8,128)(2,1)}, f32[1024,768]{1,0:T(8,128)}, f32[24,2304]{1,0:T(8,128)}, f32[24,768]{1,0:T(8,128)}, f32[24,128]{1,0:T(8,128)}) custom-call(bf16[1024,768]{1,0:T(8,128)(2,1)} %refs_0_.3, bf16[1024,768]{1,0:T(8,128)(2,1)} %refs_1_.3, bf16[6,1024,384]{2,1,0:T(8,128)(2,1)} %get-tuple-element.26.refs_2_, ...), custom_call_target="tpu_custom_call" | custom-call | tf_op jit(solution)/shard_map/backward/pallas_call | solution.py:934
  202.6 0.0 copy-start
  202.6 1.6 slice_reduce_fusion
  204.2 1.4 copy.27
  205.5 2.7 %copy.34 = bf16[1024,768]{1,0:T(8,128)(2,1)} copy(bf16[1024,768]{1,0:T(8,128)(2,1)} %get-tuple-element.72) | data formatting | bytes 3145728
  208.2 0.0 copy-done
  208.2 0.0 copy-start.3
  208.2 0.0 copy-start.4
  208.2 0.0 copy-start.2
  208.2 1.7 copy.35
  209.9 0.0 copy-done.3
  209.9 0.7 copy.36
  210.5 0.0 copy-done.4
  210.5 0.6 copy.37
  211.2 0.0 copy-done.2
  211.2 0.0 copy-start.1
  211.2 1.4 copy.38
  212.6 1.1 copy-done.1
  213.7 1.4 copy.39
  (1 shorter events, 0.0 us)
Async XLA Ops:
  202.6 5.6 %copy-start = (f32[1024,768]{1,0:T(8,128)S(1)}, f32[1024,768]{1,0:T(8,128)}, u32[]{:S(2)}) copy-start(f32[1024,768]{1,0:T(8,128)} %get-tuple-element.73) | copy-start | bytes 9437188
  208.2 1.7 copy-start.3
  208.2 2.4 %copy-start.4 = (f32[24,768]{1,0:T(8,128)S(1)}, f32[24,768]{1,0:T(8,128)}, u32[]{:S(2)}) copy-start(f32[24,768]{1,0:T(8,128)} %get-tuple-element.76) | copy-start | bytes 221188
  208.2 3.0 %copy-start.2 = (f32[1,768,768]{2,1,0:T(8,128)S(1)}, f32[1,768,768]{2,1,0:T(8,128)}, u32[]{:S(2)}) copy-start(f32[1,768,768]{2,1,0:T(8,128)} %get-tuple-element.79) | copy-start | bytes 7077892
  211.2 2.5 %copy-start.1 = (f32[1,768,768]{2,1,0:T(8,128)S(1)}, f32[1,768,768]{2,1,0:T(8,128)}, u32[]{:S(2)}) copy-start(f32[1,768,768]{2,1,0:T(8,128)} %get-tuple-element.80) | copy-start | bytes 7077892

commit v3 on v2

--- a/solution.py
+++ b/solution.py
@@ -17,6 +17,11 @@
 GAIN2 = 127
 NEG = -1e30
 VMEM_CAP = 62 << 20
+CID0 = 0
+CID1 = 1
+AHEAD_W = 4
+AHEAD_X = 2
+BEHIND_W = 2
 
 MESH = pl.DeviceIdType.MESH
 NN_ = (((1,), (0,)), ((), ()))
@@ -32,6 +37,9 @@
 
 def wait_bytes(ref, sem):
     pltpu.make_async_copy(ref, ref, sem).wait()
+
+
+arrive = wait_bytes
 
 
 def push(src, dst, send, recv, **where):
@@ -155,37 +163,37 @@
 
     lax.fori_loop(1, c.NW, wide, 0)
     for k in range(1, c.X):
-        pl.semaphore_signal(bar, inc=1, device_id={"narrow": lax.rem(x + k, c.X) * 2 + cc}, device_id_type=MESH)
+        to = lax.rem(x + k, c.X) * 2 + cc
+        pl.semaphore_signal(bar, inc=1, device_id={"narrow": to}, device_id_type=MESH)
+        other = w + 1 - 2 * lax.rem(w, 2)
+        pl.semaphore_signal(bar, inc=1, device_id={"wide": other, "narrow": to}, device_id_type=MESH)
     pl.semaphore_signal(bar, inc=1, device_id={"narrow": x * 2 + 1 - cc}, device_id_type=MESH)
-    return lambda: pl.semaphore_wait(bar, c.NW - 1 + c.X)
+    return lambda: pl.semaphore_wait(bar, c.NW - 1 + 2 * c.X - 1)
 
 
 def forward_kernel(c, *refs):
-    (v_hbm, dy_hbm, idx_ref, cap_ref, wq_hbm, wo_hbm, misc_hbm, up_hbm, down_hbm) = refs[:9]
-    (wall, mall, qkv_out, lse_out, att_out, resid_out, sent_out, meta_out, mrow_out) = refs[9:18]
-    (ret_out, outp_out, ug_out, dg_out, cent_out) = refs[18:23]
-    scratch = refs[23:]
-    (v, dy, nrm, normed, oh, wbuf, wmat, misc, mrow, qkv, lse, att, sent, sendx, senddy,
-     lsem, in_sem, out_sem, ld_sem, s1s, s1r, s2s, s2r, s3s, s3r, s4s, s4r) = scratch[:27]
+    (v_hbm, dy_hbm, idx_ref, cap_ref, wq_hbm, wo_hbm, cen_ref, g1_ref, g2_ref, up_hbm, down_hbm) = refs[:11]
+    (w_out, normt_out, qkv_out, lse_out, att_out, resid_out, meta_out, mrow_out) = refs[11:19]
+    (ret_out, outp_out, ug_out, dg_out, cent_out) = refs[19:24]
+    (v, nrm, normed, normt, oh, wbuf, wmat, wtr, misc, mrow, qkv, lse, att, sent, sendx, senddy,
+     up, down, xin, dyin, hid, dpre, dexp, outp, part, lc, lx, stage, cent,
+     lsem, in_sem, out_sem, w_sem, q_sem, st_sem, s1s, s1r, s2s, s2r, s4s, s4r,
+     ds_, dr, xs_, xr, cs_, cr, fs, fr, gs, gr, ks, kr, rs_, rr, ws_, wr) = refs[24:]
     A, X, NW, NN, T, D, CW, G, J = c.A, c.X, c.NW, c.NN, c.T, c.D, c.CW, c.G, c.J
     w, n, a, b, x, cc = place(c)
     own = (a, b, x, cc)
-
-    def cols(j):
-        dst = wall.at[(j, *own)]
+    dy = sent
+
+    for j in range(J):
+        dst = wbuf.at[(j, *own)]
         if j < G:
-            return [(wq_hbm.at[:, pl.ds(p * D + j * PAIR, PAIR)], dst.at[:, pl.ds(p * PAIR, PAIR)]) for p in range(3)]
-        return [(wo_hbm.at[:, pl.ds((j - G) * CW, CW)], dst)]
-
-    pltpu.make_async_copy(misc_hbm, mall.at[own], lsem.at[J]).start()
-    for j in range(J):
-        for s, d in cols(j):
-            pltpu.make_async_copy(s, d, lsem.at[j]).start()
-    loads = [(dy_hbm, dy), (v_hbm, v)]
-    if c.moe:
-        (up, down, xin, dyin, hid, dpre, dexp, outp, part, lc, lx, stage, cent,
-         ds_, dr, xs_, xr, cs_, cr, fs, fr, gs, gr, ks, kr, rs_, rr, ws_, wr) = scratch[27:]
-        loads += [(up_hbm.at[0], up), (down_hbm.at[0], down)]
+            for p in range(3):
+                pltpu.make_async_copy(
+                    wq_hbm.at[:, pl.ds(p * D + j * PAIR, PAIR)], dst.at[:, pl.ds(p * PAIR, PAIR)], lsem.at[j]
+                ).start()
+        else:
+            pltpu.make_async_copy(wo_hbm.at[:, pl.ds((j - G) * CW, CW)], dst, lsem.at[j]).start()
+    loads = [(dy_hbm, dy), (v_hbm, v), (up_hbm.at[0], up), (down_hbm.at[0], down)]
     for i, (s, d) in enumerate(loads):
         pltpu.make_async_copy(s, d, in_sem.at[i]).start()
 
@@ -194,8 +202,14 @@
 
     met = greet(c, w, n)
 
-    one = lax.broadcasted_iota(jnp.int32, (c.EP, T), 0) == idx_ref[...]
-    hot = one.astype(f32)
+    pad = LANES - c.slab
+    small = jnp.concatenate(
+        [cen_ref[...].astype(f32), jnp.zeros((GAIN1 - c.E, c.slab), f32), g1_ref[...].astype(f32), g2_ref[...].astype(f32)], 0
+    )
+    small = jnp.concatenate([small, jnp.zeros((LANES, pad), f32)], 1)
+    misc[own] = jnp.transpose(small)[0 : c.slab].astype(bf16)
+
+    hot = (lax.broadcasted_iota(jnp.int32, (c.EP, T), 0) == idx_ref[...]).astype(f32)
     lane = lax.broadcasted_iota(jnp.int32, (c.EP, T), 1)
     count = hot
     shift = 1
@@ -203,71 +217,77 @@
         count = count + jnp.where(lane >= shift, pltpu.roll(count, shift, 1), 0.0)
         shift *= 2
     rank = jnp.sum((count - hot) * hot, 0, keepdims=True)
-    ceiling = jnp.sum(hot * cap_ref[:, 0:1].astype(f32), 0, keepdims=True)
+    ceiling = jnp.zeros((1, T), f32)
+    for e in range(c.E):
+        ceiling = ceiling + hot[e : e + 1, :] * cap_ref[e].astype(f32)
     kept = rank < ceiling
     slot = jnp.where(kept, idx_ref[...].astype(f32) * SLOT + rank, -1.0)
-    meta_out_rows = [slot]
 
     met()
 
     def buf(j):
-        return mall if j is J else wall.at[j]
+        return misc if isinstance(j, int) and j == J else wbuf.at[j]
 
     def s1(j):
-        wait_bytes(buf(j).at[own], lsem.at[j])
+        if not (isinstance(j, int) and j == J):
+            wait_bytes(buf(j).at[own], lsem.at[j])
         for k in range(1, A):
             push(buf(j).at[own], buf(j).at[own], s1s.at[j], s1r.at[j], wide=lax.rem(a + k, A) * 2 + b)
 
+    plane = [(p, q) for p in range(2) for q in range(X) if p or q]
+
     def s2(j):
-        wait_bytes(buf(j).at[pl.ds(0, A - 1), b, x, cc], s1r.at[j])
-        for k in range(1, X):
-            part_ = buf(j).at[:, b, x, cc]
-            push(part_, part_, s2s.at[j], s2r.at[j], narrow=lax.rem(x + k, X) * 2 + cc)
-
-    def s3(j):
-        wait_bytes(buf(j).at[:, b, pl.ds(0, X - 1), cc], s2r.at[j])
-        part_ = buf(j).at[:, b, :, cc]
-        push(part_, part_, s3s.at[j], s3r.at[j], wide=a * 2 + 1 - b)
+        arrive(buf(j).at[pl.ds(0, A - 1), b, x, cc], s1r.at[j])
+        mine = buf(j).at[:, b, x, cc]
+        for i, (p, q) in enumerate(plane):
+            push(
+                mine, mine, s2s.at[j, i], s2r.at[j, i],
+                wide=a * 2 + lax.rem(b + p, 2), narrow=lax.rem(x + q, X) * 2 + cc,
+            )
+
+    def plane_bytes(j, sem):
+        for i in range(len(plane)):
+            arrive(buf(j).at[:, b, x, cc], sem.at[j, i])
 
     def s4(j):
-        wait_bytes(buf(j).at[:, b, :, cc], s3r.at[j])
-        part_ = buf(j).at[:, :, :, cc]
-        push(part_, part_, s4s.at[j], s4r.at[j], narrow=x * 2 + 1 - cc)
-
-    def ld(j):
-        wait_bytes(buf(j).at[:, :, :, cc], s4r.at[j])
-        if j is J:
-            pltpu.make_async_copy(mall, misc, ld_sem.at[J]).start()
-        else:
-            pltpu.make_async_copy(wall.at[j], wbuf.at[lax.rem(j, 2)], ld_sem.at[j]).start()
-
-    def loaded(j, at):
-        slot_ = lax.rem(j, 2)
-        wait_bytes(wbuf.at[slot_], ld_sem.at[j])
-        wmat[at] = wbuf[slot_].reshape(D, CW)
+        plane_bytes(j, s2r)
+        mine = buf(j).at[:, :, :, cc]
+        push(mine, mine, s4s.at[j], s4r.at[j], narrow=x * 2 + 1 - cc)
+
+    def take(j):
+        arrive(buf(j).at[:, :, :, cc], s4r.at[j])
+        val = wbuf[j].reshape(D, CW)
+        wmat[j] = val
+        wtr[j] = jnp.transpose(val)
+        pltpu.make_async_copy(wtr.at[j], w_out.at[j], w_sem.at[j]).start()
 
     s1(J)
-    for j in range(J):
-        s1(j)
-
-    ohv = (lax.broadcasted_iota(jnp.int32, (c.S, T), 0).astype(f32) == slot).astype(bf16)
-    oh[...] = ohv
+    s1(0)
+    oh[...] = (lax.broadcasted_iota(jnp.int32, (c.S, T), 0).astype(f32) == slot).astype(bf16)
+    s1(1)
+    s2(J)
+    s2(0)
+    s1(2)
     load_wait(0)
     senddy[...] = mm(oh[...], dy[...]).astype(bf16)
-    s2(J)
-    s2(0)
-
-    if c.moe:
-        for k in range(1, NW):
-            to = lax.rem(w + k, NW)
-            push(senddy.at[pl.ds(to * SLOT, SLOT)], dyin.at[w, x, cc], ds_, dr, wide=to)
-        dyin[w, x, cc] = senddy[pl.ds(w * SLOT, SLOT), :]
-    else:
-        pltpu.make_async_copy(senddy, senddy_out, out_sem.at[7]).start()
-    s3(J)
-    s3(0)
     s2(1)
-
+    s1(3)
+
+    def dy_w(k):
+        to = lax.rem(w + k, NW)
+        push(senddy.at[pl.ds(pl.multiple_of(to * SLOT, SLOT), SLOT)], dyin.at[w, x, cc], ds_.at[k], dr.at[k], wide=to)
+
+    def dy_x(k):
+        src = lax.rem(w - k + NW, NW)
+
+        @pl.when(k > 0)
+        def _():
+            arrive(dyin.at[src, x, cc], dr.at[k])
+
+        for q in range(1, X):
+            push(dyin.at[src, x, cc], dyin.at[src, x, cc], xs_.at[k], xr.at[k], narrow=lax.rem(x + q, X) * 2 + cc)
+
+    dyin[w, x, cc] = senddy[pl.ds(pl.multiple_of(w * SLOT, SLOT), SLOT), :]
     load_wait(1)
 
     def norm1(i, _):
@@ -278,10 +298,9 @@
     lax.fori_loop(0, T // 128, norm1, 0)
     s4(J)
     s4(0)
-    s3(1)
     s2(2)
-    ld(J)
-    wait_bytes(misc, ld_sem.at[J])
+    s1(4)
+    arrive(misc.at[:, :, :, cc], s4r.at[J])
     mrow[...] = jnp.transpose(misc[...].reshape(D, LANES).astype(f32))
     gain1 = mrow[GAIN1 : GAIN1 + 1, :]
     gain2 = mrow[GAIN2 : GAIN2 + 1, :]
@@ -293,23 +312,27 @@
         return 0
 
     lax.fori_loop(0, T // 128, norm1b, 0)
-    ld(0)
+    per = -(-NW // 4)
 
     def pair(g, _):
-        loaded(g, 0)
-
-        def project(i, _):
-            rows = pl.ds(i * QB, QB)
-            qkv[g, rows, :] = mm(normed[rows, :], wmat[0]).astype(bf16)
-            return 0
-
-        lax.fori_loop(0, T // QB, project, 0)
-        pltpu.make_async_copy(qkv.at[g], qkv_out.at[g], out_sem.at[1]).start()
-        s3(g + 2)
+        slot_ = lax.rem(g, 2)
+        take(g)
+
+        @pl.when(g >= 2)
+        def _():
+            wait_bytes(qkv.at[slot_], q_sem.at[slot_])
+
+        qkv[slot_] = mm(normed[...], wmat[g]).astype(bf16)
+        pltpu.make_async_copy(qkv.at[slot_], qkv_out.at[g], q_sem.at[slot_]).start()
+        s4(g + 1)
 
         @pl.when(g + 3 < J)
         def _():
             s2(g + 3)
+
+        @pl.when(g + 5 < J)
+        def _():
+            s1(g + 5)
 
         def put_out(rows, val):
             att[rows, pl.ds(pl.multiple_of(g * PAIR, PAIR), PAIR)] = val
@@ -319,306 +342,305 @@
 
         for i in range(T // QB):
             if i == T // QB - 1:
-                s4(g + 1)
-                if c.moe:
-                    @pl.when(g == 4)
+                for q in range(per):
+                    k = g * per + q
+
+                    @pl.when((k >= 1) & (k < NW))
                     def _():
-                        wait_bytes(dyin.at[pl.ds(0, NW - 1), x, cc], dr)
-                        for k in range(1, X):
-                            push(dyin.at[:, x, cc], dyin.at[:, x, cc], xs_, xr, narrow=lax.rem(x + k, X) * 2 + cc)
-            attend_rows(qkv.at[g], T, i, put_out, put_lse)
-        ld(g + 1)
+                        dy_w(k)
+
+                    @pl.when((g >= 2) & (k - 2 * per < NW))
+                    def _():
+                        dy_x(k - 2 * per)
+
+            attend_rows(qkv.at[slot_], T, i, put_out, put_lse)
         return 0
 
     lax.fori_loop(0, G, pair, 0)
-    pltpu.make_async_copy(lse, lse_out, out_sem.at[2]).start()
-    pltpu.make_async_copy(att, att_out, out_sem.at[3]).start()
+    pltpu.make_async_copy(lse, lse_out, out_sem.at[1]).start()
+    pltpu.make_async_copy(att, att_out, out_sem.at[2]).start()
     for j in range(G + 1, J):
         s4(j)
-        ld(j)
-    if c.moe:
-        wait_bytes(dyin.at[:, pl.ds(0, X - 1), cc], xr)
-        push(dyin.at[:, :, cc], dyin.at[:, :, cc], cs_, cr, narrow=x * 2 + 1 - cc)
     for j in range(G, J):
-        loaded(j, 1 + j - G)
+        take(j)
+
+    for j in range(G, J):
+        at = slice((j - G) * CW, (j - G + 1) * CW)
+        nrm[:, at] = v[:, at].astype(f32) + mm(att[...], wmat[j])
 
     def tail(i, _):
         rows = pl.ds(i * QB, QB)
-        left = att[rows, :]
-        prod = jnp.concatenate([mm(left, wmat[1 + j - G]) for j in range(G, J)], 1)
-        resid = v[rows, :].astype(f32) + prod
-        nrm[rows, :] = resid
-        sent[rows, :] = (layer_stats(resid)[0] * gain2).astype(bf16)
+        sent[rows, :] = (layer_stats(nrm[rows, :])[0] * gain2).astype(bf16)
         return 0
 
     lax.fori_loop(0, T // QB, tail, 0)
-    pltpu.make_async_copy(nrm, resid_out, out_sem.at[4]).start()
+    pltpu.make_async_copy(nrm, resid_out, out_sem.at[3]).start()
     sendx[...] = mm(oh[...], sent[...]).astype(bf16)
-    if c.moe:
-        for k in range(1, NW):
-            to = lax.rem(w + k, NW)
-            push(sendx.at[pl.ds(to * SLOT, SLOT)], xin.at[w, x, cc], fs.at[k], fr.at[k], wide=to)
-        xin[w, x, cc] = sendx[pl.ds(w * SLOT, SLOT), :]
-    else:
-        pltpu.make_async_copy(sendx, sendx_out, out_sem.at[8]).start()
-    pltpu.make_async_copy(sent, sent_out, out_sem.at[5]).start()
+
+    def x_w(k):
+        to = lax.rem(w + k, NW)
+        push(sendx.at[pl.ds(pl.multiple_of(to * SLOT, SLOT), SLOT)], xin.at[w, x, cc], fs.at[k], fr.at[k], wide=to)
+
+    for k in range(1, AHEAD_W):
+        x_w(k)
+    xin[w, x, cc] = sendx[pl.ds(pl.multiple_of(w * SLOT, SLOT), SLOT), :]
+
+    crow = mrow[pl.ds(w, 1), :]
+
+    def source(i):
+        return lax.rem(w - i + NW, NW)
+
+    def fwd_x(i):
+        src = source(i)
+
+        @pl.when(i > 0)
+        def _():
+            arrive(xin.at[src, x, cc], fr.at[i])
+
+        for k in range(1, X):
+            push(xin.at[src, x, cc], xin.at[src, x, cc], gs.at[i], gr.at[i], narrow=lax.rem(x + k, X) * 2 + cc)
+
+    def fwd_c(i):
+        src = source(i)
+        arrive(xin.at[src, pl.ds(0, X - 1), cc], gr.at[i])
+        push(xin.at[src, :, cc], xin.at[src, :, cc], ks.at[i], kr.at[i], narrow=x * 2 + 1 - cc)
+
+    def expert(i):
+        src = source(i)
+        arrive(xin.at[src, :, cc], kr.at[i])
+        xb = xin[src].reshape(c.R, D)
+        db = dyin[src].reshape(c.R, D)
+        xf, df = xb.astype(f32), db.astype(f32)
+        s = jax.nn.sigmoid(jnp.sum(xf * crow, 1, keepdims=True))
+        de = (df * s).astype(bf16)
+        pre = mm(xb, up[...])
+        cdf = 0.5 * (1.0 + lax.erf(pre * 0.7071067811865476))
+        hb = (pre * cdf).astype(bf16)
+        slope = cdf + pre * (jnp.exp(-0.5 * pre * pre) * 0.3989422804014327)
+        dpb = (mm(de, down[...]) * slope).astype(bf16)
+        out = mm(hb, down[...], NT_)
+        dl = jnp.sum(df * out, 1, keepdims=True) * (s * (1.0 - s))
+        dn = mm(dpb, up[...], NT_) + dl * crow
+        part[src] = dn.astype(bf16).reshape(X, 2, SLOT, D)
+        outp[src] = out.astype(bf16).reshape(X, 2, SLOT, D)
+        cent[...] += jnp.broadcast_to(jnp.sum(dl * xf, 0, keepdims=True), cent.shape)
+        rows = pl.ds(pl.multiple_of(src * c.R, SLOT), c.R)
+        hid[rows, :] = hb
+        dpre[rows, :] = dpb
+        dexp[rows, :] = de
+
+    def ret_c(i):
+        src = source(i)
+        push(part.at[src, :, 1 - cc], lc.at[src], rs_.at[0, i], rr.at[0, i], narrow=x * 2 + 1 - cc)
+
+    def ret_x(i):
+        src = source(i)
+        arrive(lc.at[src], rr.at[0, i])
+        part[src, :, cc] = (part[src, :, cc].astype(f32) + lc[src].astype(f32)).astype(bf16)
+        for k in range(1, X):
+            x2 = lax.rem(x + k, X)
+            push(part.at[src, x2, cc], lx.at[src, x], rs_.at[1, i], rr.at[1, i], narrow=x2 * 2 + cc)
+
+    def ret_w(i):
+        src = source(i)
+        arrive(lx.at[src, pl.ds(0, X - 1)], rr.at[1, i])
+        total = part[src, x, cc].astype(f32)
+        for k in range(1, X):
+            total = total + lx[src, lax.rem(x + k, X)].astype(f32)
+        part[src, x, cc] = total.astype(bf16)
+
+        @pl.when(i > 0)
+        def _():
+            push(part.at[src, x, cc], ret_out.at[w], ws_.at[i], wr.at[i], wide=src)
+
+        @pl.when(i == 0)
+        def _():
+            pltpu.make_async_copy(part.at[src, x, cc], ret_out.at[w], ws_.at[0]).start()
+
+    fwd_x(0)
+    normt[...] = jnp.transpose(normed[...])
+    pltpu.make_async_copy(normt, normt_out, out_sem.at[5]).start()
+    for k in range(per * (G - 2), NW):
+        dy_x(k)
+
     logits = mm(mrow[0 : c.EP, :].astype(bf16), sent[...], NT_)
-    logit = jnp.sum(logits * hot, 0, keepdims=True)
-    gate = jax.nn.sigmoid(logit) * kept.astype(f32)
+    gate = jax.nn.sigmoid(jnp.sum(logits * hot, 0, keepdims=True)) * kept.astype(f32)
     meta_out[...] = jnp.concatenate([slot, gate, jnp.zeros((6, T), f32)], 0)
-
-    if c.moe:
-        load_wait(2)
-        load_wait(3)
-        wait_bytes(dyin.at[:, :, cc], cr)
-        cent[...] = jnp.zeros_like(cent)
-        crow = mrow[pl.ds(w, 1), :]
-
-        def source(i):
-            return lax.rem(w - i + NW, NW)
-
-        def fwd_x(i):
-            src = source(i)
-
-            @pl.when(i > 0)
-            def _():
-                wait_bytes(xin.at[src, x, cc], fr.at[i])
-
-            for k in range(1, X):
-                push(xin.at[src, x, cc], xin.at[src, x, cc], gs.at[i], gr.at[i], narrow=lax.rem(x + k, X) * 2 + cc)
-
-        def fwd_c(i):
-            src = source(i)
-            wait_bytes(xin.at[src, pl.ds(0, X - 1), cc], gr.at[i])
-            push(xin.at[src, :, cc], xin.at[src, :, cc], ks.at[i], kr.at[i], narrow=x * 2 + 1 - cc)
-
-        def expert(i):
-            src = source(i)
-            wait_bytes(xin.at[src, :, cc], kr.at[i])
-            xb = xin[src].reshape(c.R, D)
-            db = dyin[src].reshape(c.R, D)
-            xf, df = xb.astype(f32), db.astype(f32)
-            s = jax.nn.sigmoid(jnp.sum(xf * crow, 1, keepdims=True))
-            de = (df * s).astype(bf16)
-            pre = mm(xb, up[...])
-            cdf = 0.5 * (1.0 + lax.erf(pre * 0.7071067811865476))
-            hb = (pre * cdf).astype(bf16)
-            slope = cdf + pre * (jnp.exp(-0.5 * pre * pre) * 0.3989422804014327)
-            dpb = (mm(de, down[...]) * slope).astype(bf16)
-            out = mm(hb, down[...], NT_)
-            dl = jnp.sum(df * out, 1, keepdims=True) * (s * (1.0 - s))
-            dn = mm(dpb, up[...], NT_) + dl * crow
-            part[src] = dn.astype(bf16).reshape(X, 2, SLOT, D)
-            outp[src] = out.astype(bf16).reshape(X, 2, SLOT, D)
-            cent[...] += jnp.broadcast_to(jnp.sum(dl * xf, 0, keepdims=True), cent.shape)
-            rows = pl.ds(pl.multiple_of(src * c.R, SLOT), c.R)
-            hid[rows, :] = hb
-            dpre[rows, :] = dpb
-            dexp[rows, :] = de
-
-        def ret_c(i):
-            src = source(i)
-            push(part.at[src, :, 1 - cc], lc.at[src], rs_.at[0, i], rr.at[0, i], narrow=x * 2 + 1 - cc)
-
-        def ret_x(i):
-            src = source(i)
-            wait_bytes(lc.at[src], rr.at[0, i])
-            part[src, :, cc] = (part[src, :, cc].astype(f32) + lc[src].astype(f32)).astype(bf16)
-            for k in range(1, X):
-                x2 = lax.rem(x + k, X)
-                push(part.at[src, x2, cc], lx.at[src, x], rs_.at[1, i], rr.at[1, i], narrow=x2 * 2 + cc)
-
-        def ret_w(i):
-            src = source(i)
-            wait_bytes(lx.at[src, pl.ds(0, X - 1)], rr.at[1, i])
-            total = part[src, x, cc].astype(f32)
-            for k in range(1, X):
-                total = total + lx[src, lax.rem(x + k, X)].astype(f32)
-            part[src, x, cc] = total.astype(bf16)
-
-            @pl.when(i > 0)
-            def _():
-                push(part.at[src, x, cc], ret_out.at[w], ws_.at[i], wr.at[i], wide=src)
-
-            @pl.when(i == 0)
-            def _():
-                pltpu.make_async_copy(part.at[src, x, cc], ret_out.at[w], ws_.at[0]).start()
-
-        fwd_x(0)
-        fwd_c(0)
-        fwd_x(1)
-
-        def block(i, _):
-            @pl.when(i + 1 < NW)
-            def _():
-                fwd_c(i + 1)
-
-            @pl.when(i + 2 < NW)
-            def _():
-                fwd_x(i + 2)
-
-            expert(i)
-            ret_c(i)
-
-            @pl.when(i >= 1)
-            def _():
-                ret_x(i - 1)
-
-            @pl.when(i >= 2)
-            def _():
-                ret_w(i - 2)
-
+    cent[...] = jnp.zeros_like(cent)
+
+    def dy_all(k, _):
+        arrive(dyin.at[w, x, cc], xr.at[k])
+        return 0
+
+    for q in range(X - 1):
+        lax.fori_loop(0, NW, dy_all, 0)
+    push(dyin.at[:, :, cc], dyin.at[:, :, cc], cs_, cr, narrow=x * 2 + 1 - cc)
+    fwd_c(0)
+    for k in range(1, AHEAD_X):
+        fwd_x(k)
+    load_wait(2)
+    load_wait(3)
+    arrive(dyin.at[:, :, cc], cr)
+
+    def block(i, _):
+        @pl.when(i + AHEAD_W < NW)
+        def _():
+            x_w(i + AHEAD_W)
+
+        @pl.when(i + 1 < NW)
+        def _():
+            fwd_c(i + 1)
+
+        @pl.when(i + AHEAD_X < NW)
+        def _():
+            fwd_x(i + AHEAD_X)
+
+        expert(i)
+        ret_c(i)
+
+        @pl.when(i >= 1)
+        def _():
+            ret_x(i - 1)
+
+        @pl.when(i >= BEHIND_W)
+        def _():
+            ret_w(i - BEHIND_W)
+
+        return 0
+
+    lax.fori_loop(0, NW, block, 0)
+    ret_x(NW - 1)
+    for i in range(NW - BEHIND_W, NW - 1):
+        ret_w(i)
+    pltpu.make_async_copy(outp, outp_out, out_sem.at[4]).start()
+    cent_out[...] = cent[...]
+    parts = D // QB
+
+    def grads(lhs, rhs, out, second):
+        def one_block(i, _):
+            at = pl.ds(pl.multiple_of(i * QB, QB), QB)
+            if second:
+                wait_bytes(stage.at[i], st_sem.at[i])
+            stage[i] = mm(lhs(at), rhs[...], TN_)
+            pltpu.make_async_copy(stage.at[i], out.at[0, at], st_sem.at[i]).start()
             return 0
 
-        lax.fori_loop(0, NW, block, 0)
-        ret_x(NW - 1)
-        ret_w(NW - 2)
-        pltpu.make_async_copy(outp, outp_out, out_sem.at[6]).start()
-        cent_out[...] = cent[...]
-
-        def grads(lhs, rhs, out, base, flush):
-            def one_block(i, _):
-                at = pl.ds(pl.multiple_of(i * QB, QB), QB)
-                lhs_block = lhs(at)
-                stage[base + i] = mm(lhs_block, rhs[...], TN_)
-                pltpu.make_async_copy(stage.at[base + i], out.at[0, at], in_sem.at[4 + base + i]).start()
-                return 0
-
-            lax.fori_loop(0, D // QB, one_block, 0)
-
-        grads(lambda at: dexp[:, at], hid, dg_out, 0, None)
-        ret_w(NW - 1)
-        grads(lambda at: xin[:, :, :, :, at].reshape(NW * c.R, QB), dpre, ug_out, D // QB, None)
-
-    for q, (s, ref) in enumerate([(mrow, None), (qkv, None), (lse, None), (att, None), (nrm, None), (sent, None)]):
-        wait_bytes(s, out_sem.at[q])
+        lax.fori_loop(0, parts, one_block, 0)
+
+    grads(lambda at: dexp[:, at], hid, dg_out, False)
+    ret_w(NW - 1)
+    grads(lambda at: xin[:, :, :, :, at].reshape(NW * c.R, QB), dpre, ug_out, True)
+
+    for q, ref in enumerate([mrow, lse, att, nrm, outp, normt]):
+        wait_bytes(ref, out_sem.at[q])
+    for q in range(2):
+        wait_bytes(qkv.at[q], q_sem.at[q])
     for j in [J] + list(range(J)):
-        wait_bytes(buf(j).at[pl.ds(0, A - 1), b, x, cc], s1s.at[j])
-        wait_bytes(buf(j).at[:, b, pl.ds(0, X - 1), cc], s2s.at[j])
-        wait_bytes(buf(j).at[:, b, :, cc], s3s.at[j])
-        wait_bytes(buf(j).at[:, :, :, cc], s4s.at[j])
-    if c.moe:
-        wait_bytes(dyin.at[pl.ds(0, NW - 1), x, cc], ds_)
-        wait_bytes(dyin.at[:, pl.ds(0, X - 1), cc], xs_)
-        wait_bytes(dyin.at[:, :, cc], cs_)
-        wait_bytes(outp, out_sem.at[6])
-
-        def drain(i, _):
-            src = source(i)
-            wait_bytes(xin.at[src, pl.ds(0, X - 1), cc], gs.at[i])
-            wait_bytes(xin.at[src, :, cc], ks.at[i])
-            wait_bytes(lc.at[src], rs_.at[0, i])
-            wait_bytes(lx.at[src, pl.ds(0, X - 1)], rs_.at[1, i])
-            wait_bytes(xin.at[src, x, cc], ws_.at[i])
-
-            @pl.when(i > 0)
-            def _():
-                wait_bytes(xin.at[src, x, cc], fs.at[i])
-                wait_bytes(xin.at[src, x, cc], wr.at[i])
-
-            return 0
-
-        lax.fori_loop(0, NW, drain, 0)
-        for i in range(2 * (D // QB)):
-            wait_bytes(stage.at[i], in_sem.at[4 + i])
-    else:
-        wait_bytes(senddy, out_sem.at[7])
-        wait_bytes(sendx, out_sem.at[8])
-
-
-def forward_call(c, v, dy, idx, cap, wq, wo, misc, up, down):
-    T, D, CW, G, J, NW, NN, A, X = c.T, c.D, c.CW, c.G, c.J, c.NW, c.NN, c.A, c.X
+        if not (isinstance(j, int) and j == J):
+            wait_bytes(wtr.at[j], w_sem.at[j])
+        arrive(buf(j).at[pl.ds(0, A - 1), b, x, cc], s1s.at[j])
+        plane_bytes(j, s2s)
+        arrive(buf(j).at[:, :, :, cc], s4s.at[j])
+    arrive(dyin.at[:, :, cc], cs_)
+
+    def drain(i, _):
+        src = source(i)
+        arrive(xin.at[src, pl.ds(0, X - 1), cc], xs_.at[i])
+        arrive(xin.at[src, pl.ds(0, X - 1), cc], gs.at[i])
+        arrive(xin.at[src, :, cc], ks.at[i])
+        arrive(lc.at[src], rs_.at[0, i])
+        arrive(lx.at[src, pl.ds(0, X - 1)], rs_.at[1, i])
+
+        @pl.when(i > 0)
+        def _():
+            arrive(xin.at[src, x, cc], ds_.at[i])
+            arrive(xin.at[src, x, cc], fs.at[i])
+            arrive(xin.at[src, x, cc], ws_.at[i])
+            arrive(xin.at[src, x, cc], wr.at[i])
+
+        return 0
+
+    lax.fori_loop(0, NW, drain, 0)
+    wait_bytes(part.at[0, 0, 0], ws_.at[0])
+    for i in range(parts):
+        wait_bytes(stage.at[i], st_sem.at[i])
+
+
+def forward_call(c, v, dy, idx, cap, wq, wo, cen, g1, g2, up, down):
+    T, D, CW, G, J, NW, NN, A, X, L, F = c.T, c.D, c.CW, c.G, c.J, c.NW, c.NN, c.A, c.X, c.slab, c.F
     any_ = pl.BlockSpec(memory_space=pl.ANY)
     vm = pl.BlockSpec(memory_space=pltpu.VMEM)
+    sm = pl.BlockSpec(memory_space=pltpu.SMEM)
     sds = jax.ShapeDtypeStruct
-    F = c.F
+    rows_ = (NW, X, 2, SLOT, D)
     outs = [
-        (sds((J, A, 2, X, 2, c.slab, CW), bf16), any_),
-        (sds((A, 2, X, 2, c.slab, LANES), bf16), any_),
+        (sds((J, CW, D), bf16), any_),
+        (sds((D, T), bf16), any_),
         (sds((G, T, CW), bf16), any_),
         (sds((G, 8, T), f32), any_),
         (sds((T, D), bf16), any_),
         (sds((T, D), f32), any_),
-        (sds((T, D), bf16), any_),
         (sds((8, T), f32), vm),
         (sds((LANES, D), f32), any_),
+        (sds((NW, SLOT, D), bf16), any_),
+        (sds(rows_, bf16), any_),
+        (sds((1, D, F), f32), any_),
+        (sds((1, D, F), f32), any_),
+        (sds((8, D), f32), vm),
     ]
     dma, V = pltpu.SemaphoreType.DMA, pltpu.VMEM
+    rows = NW * c.R
     scratch = [
-        V((T, D), bf16), V((T, D), bf16), V((T, D), f32), V((T, D), bf16), V((c.S, T), bf16),
-        V((2, A, 2, X, 2, c.slab, CW), bf16), V((1 + J - G, D, CW), bf16),
-        V((A, 2, X, 2, c.slab, LANES), bf16), V((LANES, D), f32), V((G, T, CW), bf16), V((G, 8, T), f32),
-        V((T, D), bf16), V((T, D), bf16), V((c.S, D), bf16), V((c.S, D), bf16),
-        dma((J + 1,)), dma((4 + 2 * (D // QB),)), dma((9,)), dma((J + 1,)),
-    ] + [dma((J + 1,))] * 8
-    if c.moe:
-        outs += [
-            (sds((NW, SLOT, D), bf16), any_),
-            (sds((NW, X, 2, SLOT, D), bf16), any_),
-            (sds((1, D, F), f32), any_),
-            (sds((1, D, F), f32), any_),
-            (sds((8, D), f32), vm),
-        ]
-        rows = NW * c.R
-        scratch += [
-            V((D, F), bf16), V((D, F), bf16), V((NW, X, 2, SLOT, D), bf16), V((NW, X, 2, SLOT, D), bf16),
-            V((rows, F), bf16), V((rows, F), bf16), V((rows, D), bf16), V((NW, X, 2, SLOT, D), bf16),
-            V((NW, X, 2, SLOT, D), bf16), V((NW, X, SLOT, D), bf16), V((NW, X, SLOT, D), bf16),
-            V((2 * (D // QB), QB, F), f32), V((8, D), f32),
-            dma(()), dma(()), dma(()), dma(()), dma(()), dma(()),
-            dma((NW,)), dma((NW,)), dma((NW,)), dma((NW,)), dma((NW,)), dma((NW,)),
-            dma((2, NW)), dma((2, NW)), dma((NW,)), dma((NW,)),
-        ]
-    else:
-        outs += [(sds((c.S, D), bf16), any_), (sds((c.S, D), bf16), any_)]
+        V((T, D), bf16), V((T, D), f32), V((T, D), bf16), V((D, T), bf16), V((c.S, T), bf16),
+        V((J, A, 2, X, 2, L, CW), bf16), V((J, D, CW), bf16), V((J, CW, D), bf16), V((A, 2, X, 2, L, LANES), bf16), V((LANES, D), f32),
+        V((2, T, CW), bf16), V((G, 8, T), f32), V((T, D), bf16), V((T, D), bf16), V((c.S, D), bf16), V((c.S, D), bf16),
+        V((D, F), bf16), V((D, F), bf16), V(rows_, bf16), V(rows_, bf16),
+        V((rows, F), bf16), V((rows, F), bf16), V((rows, D), bf16), V(rows_, bf16), V(rows_, bf16),
+        V((NW, X, SLOT, D), bf16), V((NW, X, SLOT, D), bf16), V((D // QB, QB, F), f32), V((8, D), f32),
+        dma((J,)), dma((4,)), dma((6,)), dma((J,)), dma((2,)), dma((D // QB,)),
+    ] + [dma((J + 1,))] * 2 + [dma((J + 1, 2 * X - 1))] * 2 + [dma((J + 1,))] * 2 + [dma((NW,))] * 4 + [dma(()), dma(())] + [dma((NW,))] * 6 + [
+        dma((2, NW)), dma((2, NW)), dma((NW,)), dma((NW,)),
+    ]
     return pl.pallas_call(
         functools.partial(forward_kernel, c),
         out_shape=tuple(o[0] for o in outs),
-        in_specs=[any_, any_, vm, vm, any_, any_, any_, any_, any_],
+        in_specs=[any_, any_, vm, sm, any_, any_, vm, vm, vm, any_, any_],
         out_specs=tuple(o[1] for o in outs),
         scratch_shapes=scratch,
         compiler_params=pltpu.CompilerParams(
-            collective_id=0, has_side_effects=True, vmem_limit_bytes=VMEM_CAP
+            collective_id=CID0, has_side_effects=True, vmem_limit_bytes=VMEM_CAP
         ),
         name="forward",
-    )(v, dy, idx, cap, wq, wo, misc, up, down)
+    )(v, dy, idx, cap, wq, wo, cen, g1, g2, up, down)
 
 
 def backward_kernel(c, *refs):
-    (v_hbm, dy_hbm, qkv_hbm, lse_hbm, att_hbm, resid_hbm, wall, ret_hbm, outp_hbm, mrow, meta, cent) = refs[:12]
-    (mixed_out, tok_out, qg_out, og_out, small_out) = refs[12:17]
-    (v, dy, qkv, lse, att, resid, wbuf, wmat, ret, oh, normt, dbr, datt, dnm, dqkv, dk, dv, prod, rowbuf,
+    (v_hbm, dy_hbm, qkv_hbm, lse_hbm, att_hbm, resid_hbm, wt_hbm, nt_hbm, ret_hbm, outp_hbm, mrow, meta, cent) = refs[:13]
+    (mixed_out, tok_out, qg_out, og_out, small_out) = refs[13:18]
+    (v, dy, qkv, lse, att, resid, wt, ret, oh, normt, dbr, datt, dnm, dqkv, dk, dv, prod, rowbuf,
      part, lc, lx, got, mixed,
-     gb, la, lb, lxx, lz, sgb, sla, slb, slx, slz,
-     in_sem, q_sem, out_sem, os_, orv, ows, owr, rs_, rr, tokacc) = refs[17:]
+     gb, la, lb, lz, sgb, sla, slb, slz,
+     in_sem, q_sem, out_sem, os_, orv, ows, owr, rs_, rr, ps_, pr, tokacc) = refs[18:]
     A, X, NW, NN, T, D, CW, G, J = c.A, c.X, c.NW, c.NN, c.T, c.D, c.CW, c.G, c.J
     H = J - G
     w, n, a, b, x, cc = place(c)
     blocks = T // QB
 
     loads = [
-        (ret_hbm, ret), (resid_hbm, resid), (dy_hbm, dy), (att_hbm, att), (v_hbm, v), (lse_hbm, lse),
+        (ret_hbm, ret), (resid_hbm, resid), (dy_hbm, dy), (att_hbm, att), (v_hbm, v), (lse_hbm, lse), (nt_hbm, normt),
+        (wt_hbm.at[pl.ds(G, H)], wt.at[pl.ds(G, H)]), (wt_hbm.at[pl.ds(0, G)], wt.at[pl.ds(0, G)]),
     ]
     for i, (s, d) in enumerate(loads):
         pltpu.make_async_copy(s, d, in_sem.at[i]).start()
-    own_part = pltpu.make_async_copy(outp_hbm.at[:, :, cc], part, in_sem.at[6])
+    own_part = pltpu.make_async_copy(outp_hbm.at[:, :, cc], part, in_sem.at[9])
     own_part.start()
 
     def load_wait(i):
         wait_bytes(loads[i][1], in_sem.at[i])
 
-    def fetch_w(j, slot_):
-        pltpu.make_async_copy(wall.at[j], wbuf.at[slot_], q_sem.at[0, slot_]).start()
-
-    def take_w(slot_, at):
-        wait_bytes(wbuf.at[slot_], q_sem.at[0, slot_])
-        wmat[at] = wbuf[slot_].reshape(D, CW)
-
     def fetch_qkv(g, slot_):
         pltpu.make_async_copy(qkv_hbm.at[g], qkv.at[slot_], q_sem.at[1, slot_]).start()
 
-    for h in range(H):
-        fetch_w(G + h, h)
     fetch_qkv(0, 0)
     met = greet(c, w, n)
 
@@ -650,42 +672,46 @@
     rowbuf[GAIN2 : GAIN2 + 1, :] = lax.fori_loop(0, blocks, norm2_back, jnp.zeros((1, D), f32))
     load_wait(3)
 
-    big = (gb, la, lb, lxx, lz, 0)
-    tiny = (sgb, sla, slb, slx, slz, J)
+    big = (gb, la, lb, lz, 0)
+    tiny = (sgb, sla, slb, slz, J)
 
     def add(p, q):
         return (p.astype(f32) + q.astype(f32)).astype(bf16)
 
     def ra(t, j):
-        push(t[0].at[j, :, :, :, 1 - cc], t[1].at[j], rs_.at[0, t[5] + j], rr.at[0, t[5] + j], narrow=x * 2 + 1 - cc)
+        push(t[0].at[j, :, :, :, 1 - cc], t[1].at[j], rs_.at[0, t[4] + j], rr.at[0, t[4] + j], narrow=x * 2 + 1 - cc)
+
+    plane = [(p, q) for p in range(2) for q in range(X) if p or q]
 
     def rb(t, j):
-        wait_bytes(t[1].at[j], rr.at[0, t[5] + j])
+        arrive(t[1].at[j], rr.at[0, t[4] + j])
         t[0][j, :, :, :, cc] = add(t[0][j, :, :, :, cc], t[1][j])
-        push(t[0].at[j, :, 1 - b, :, cc], t[2].at[j], rs_.at[1, t[5] + j], rr.at[1, t[5] + j], wide=a * 2 + 1 - b)
+        for i, (p, q) in enumerate(plane):
+            b2, x2 = lax.rem(b + p, 2), lax.rem(x + q, X)
+            push(
+                t[0].at[j, :, b2, x2, cc], t[2].at[j, b, x], ps_.at[t[4] + j, i], pr.at[t[4] + j, i],
+                wide=a * 2 + b2, narrow=x2 * 2 + cc,
+            )
+
+    def plane_bytes(t, j, sem):
+        for i in range(len(plane)):
+            arrive(t[2].at[j, 0, 0], sem.at[t[4] + j, i])
 
     def rc(t, j):
-        wait_bytes(t[2].at[j], rr.at[1, t[5] + j])
-        t[0][j, :, b, :, cc] = add(t[0][j, :, b, :, cc], t[2][j])
-        for k in range(1, X):
-            x2 = lax.rem(x + k, X)
-            push(t[0].at[j, :, b, x2, cc], t[3].at[j, x], rs_.at[2, t[5] + j], rr.at[2, t[5] + j], narrow=x2 * 2 + cc)
-
-    def rd(t, j):
-        wait_bytes(t[3].at[j, pl.ds(0, X - 1)], rr.at[2, t[5] + j])
+        plane_bytes(t, j, pr)
         total = t[0][j, :, b, x, cc].astype(f32)
-        for k in range(1, X):
-            total = total + t[3][j, lax.rem(x + k, X)].astype(f32)
+        for p, q in plane:
+            total = total + t[2][j, lax.rem(b + p, 2), lax.rem(x + q, X)].astype(f32)
         t[0][j, :, b, x, cc] = total.astype(bf16)
         for k in range(1, A):
             a2 = lax.rem(a + k, A)
-            push(t[0].at[j, a2, b, x, cc], t[4].at[j, a], rs_.at[3, t[5] + j], rr.at[3, t[5] + j], wide=a2 * 2 + b)
+            push(t[0].at[j, a2, b, x, cc], t[3].at[j, a], rs_.at[1, t[4] + j], rr.at[1, t[4] + j], wide=a2 * 2 + b)
 
     def rf(t, j):
-        wait_bytes(t[4].at[j, pl.ds(0, A - 1)], rr.at[3, t[5] + j])
+        arrive(t[3].at[j, pl.ds(0, A - 1)], rr.at[1, t[4] + j])
         total = t[0][j, a, b, x, cc].astype(f32)
         for k in range(1, A):
-            total = total + t[4][j, lax.rem(a + k, A)].astype(f32)
+            total = total + t[3][j, lax.rem(a + k, A)].astype(f32)
         return total
 
     def rf_w(j):
@@ -700,28 +726,16 @@
         gb[h] = mm(att[...], dbr[:, h * CW : (h + 1) * CW], TN_).astype(bf16).reshape(A, 2, X, 2, c.slab, CW)
         ra(big, h)
 
-    for h in range(H):
-        take_w(h, h)
+    load_wait(7)
 
     def out_back(i, _):
-        rows = pl.ds(i * QB, QB)
-        total = mm(dbr[rows, 0:CW], wmat[0], NT_)
-        for h in range(1, H):
-            total = total + mm(dbr[rows, h * CW : (h + 1) * CW], wmat[h], NT_)
-        datt[rows, :] = total.astype(bf16)
-        return 0
-
-    lax.fori_loop(0, blocks, out_back, 0)
-    fetch_w(0, 0)
+        at = pl.ds(pl.multiple_of(i * QB, QB), QB)
+        datt[:, at] = mm(dbr[...], wt[pl.ds(G, H), :, at].reshape(D, QB)).astype(bf16)
+        return 0
+
+    lax.fori_loop(0, D // QB, out_back, 0)
     load_wait(4)
-
-    def norm1(i, _):
-        rows = pl.ds(i * QB, QB)
-        val = (layer_stats(v[rows, :].astype(f32))[0] * gain1).astype(bf16)
-        normt[:, pl.ds(pl.multiple_of(i * QB, QB), QB)] = jnp.transpose(val)
-        return 0
-
-    lax.fori_loop(0, blocks, norm1, 0)
+    load_wait(6)
     for h in range(H):
         rb(big, h)
     load_wait(5)
@@ -733,7 +747,7 @@
             push(part.at[i, x2], lx.at[i, x], os_.at[1 + i], orv.at[1 + i], narrow=x2 * 2 + cc)
 
     def o_w(i):
-        wait_bytes(lx.at[i, pl.ds(0, X - 1)], orv.at[1 + i])
+        arrive(lx.at[i, pl.ds(0, X - 1)], orv.at[1 + i])
         total = part[i, x].astype(f32)
         for k in range(1, X):
             total = total + lx[i, lax.rem(x + k, X)].astype(f32)
@@ -747,7 +761,7 @@
         def _():
             got[w] = part[w, x]
 
-    wait_bytes(lc, orv.at[0])
+    arrive(lc, orv.at[0])
 
     def merge(i, _):
         part[i] = add(part[i], lc[i])
@@ -769,7 +783,6 @@
 
         @pl.when(g + 1 < G)
         def _():
-            fetch_w(g + 1, 1 - s_)
             fetch_qkv(g + 1, 1 - s_)
 
         wait_bytes(qkv.at[s_], q_sem.at[1, s_])
@@ -780,21 +793,17 @@
         prod[1:2, :] = jnp.sum(full[HD:], 0, keepdims=True)
 
         def put_dq(rows, val):
-            dqkv[rows, 0:PAIR] = val
+            dqkv[g, rows, 0:PAIR] = val
 
         for i in reversed(range(blocks)):
+            if i == 0:
+                rc(big, g + H - 2)
             attend_rows_back(qkv.at[s_], att_g, datt_g, lse.at[g], i, i == blocks - 1, prod, dk, dv, put_dq)
             if i == blocks - 1:
                 @pl.when(g >= 1)
                 def _():
                     rb(big, g + H - 1)
 
-                rc(big, g + H - 2)
-
-                @pl.when(g + H >= 3)
-                def _():
-                    rd(big, g + H - 3)
-
                 @pl.when(g < 4)
                 def _():
                     spread(o_x, g)
@@ -803,32 +812,27 @@
                 def _():
                     spread(o_w, g - 2)
 
-        dqkv[:, PAIR : 2 * PAIR] = dk[...].astype(bf16)
-        dqkv[:, 2 * PAIR :] = dv[...].astype(bf16)
-        gb[H + g] = mm(normt[...], dqkv[...]).astype(bf16).reshape(A, 2, X, 2, c.slab, CW)
+        dqkv[g, :, PAIR : 2 * PAIR] = dk[...].astype(bf16)
+        dqkv[g, :, 2 * PAIR :] = dv[...].astype(bf16)
+        gb[H + g] = mm(normt[...], dqkv[g]).astype(bf16).reshape(A, 2, X, 2, c.slab, CW)
         ra(big, H + g)
-        take_w(s_, 0)
-
-        def back(i, _):
-            rows = pl.ds(i * QB, QB)
-            val = mm(dqkv[rows, :], wmat[0], NT_)
-
-            @pl.when(g == 0)
-            def _():
-                tokacc[rows, :] = val
-
-            @pl.when(g > 0)
-            def _():
-                tokacc[rows, :] += val
-
-            return 0
-
-        lax.fori_loop(0, blocks, back, 0)
         return 0
 
     lax.fori_loop(0, G, pair, 0)
-
+    load_wait(8)
+
+    def back(i):
+        at = slice(i * QB, (i + 1) * QB)
+        total = mm(dqkv[0], wt[0, :, at])
+        for g in range(1, G):
+            total = total + mm(dqkv[g], wt[g, :, at])
+        tokacc[:, at] = total
+
+    back(0)
     rb(big, J - 1)
+    rc(big, J - 2)
+    for i in range(1, D // QB):
+        back(i)
     def norm1_back(i, acc):
         rows = pl.ds(i * QB, QB)
         n1, r1 = layer_stats(v[rows, :].astype(f32))
@@ -843,18 +847,14 @@
     tok_copy.start()
     sgb[0] = jnp.transpose(rowbuf[...]).astype(bf16).reshape(A, 2, X, 2, c.slab, LANES)
     ra(tiny, 0)
-    rc(big, J - 2)
-    rd(big, J - 3)
+    rc(big, J - 1)
     rb(tiny, 0)
-    rc(big, J - 1)
 
     def o_wait(k, _):
-        wait_bytes(got.at[0], owr.at[k])
+        arrive(got.at[0], owr.at[k])
         return 0
 
     lax.fori_loop(1, NW, o_wait, 0)
-    rd(big, J - 2)
-    rc(tiny, 0)
 
     def mix(i, _):
         cols = pl.ds(pl.multiple_of(i * QB, QB), QB)
@@ -865,8 +865,7 @@
     lax.fori_loop(0, blocks, mix, 0)
     mix_copy = pltpu.make_async_copy(mixed, mixed_out, out_sem.at[1])
     mix_copy.start()
-    rd(big, J - 1)
-    rd(tiny, 0)
+    rc(tiny, 0)
     for h in range(H):
         rf_w(h)
 
@@ -877,24 +876,23 @@
     lax.fori_loop(0, G, fin, 0)
     small_out[...] = rf(tiny, 0)
 
-    wait_bytes(lc, os_.at[0])
+    arrive(lc, os_.at[0])
 
     def drain(i, _):
-        wait_bytes(lx.at[i, pl.ds(0, X - 1)], os_.at[1 + i])
+        arrive(lx.at[i, pl.ds(0, X - 1)], os_.at[1 + i])
 
         @pl.when(i != w)
         def _():
-            wait_bytes(got.at[0], ows.at[i])
+            arrive(got.at[0], ows.at[i])
 
         return 0
 
     lax.fori_loop(0, NW, drain, 0)
 
     def drain_sums(t, j):
-        for q in range(2):
-            wait_bytes(t[1 + q].at[j], rs_.at[q, t[5] + j])
-        wait_bytes(t[3].at[j, pl.ds(0, X - 1)], rs_.at[2, t[5] + j])
-        wait_bytes(t[4].at[j, pl.ds(0, A - 1)], rs_.at[3, t[5] + j])
+        arrive(t[1].at[j], rs_.at[0, t[4] + j])
+        plane_bytes(t, j, ps_)
+        arrive(t[3].at[j, pl.ds(0, A - 1)], rs_.at[1, t[4] + j])
 
     def drain_big(j, _):
         drain_sums(big, j)
@@ -906,7 +904,7 @@
     mix_copy.wait()
 
 
-def backward_call(c, v, dy, qkv, lse, att, resid, wall, ret, outp, mrow, meta, cent):
+def backward_call(c, v, dy, qkv, lse, att, resid, wt, nt, ret, outp, mrow, meta, cent):
     T, D, CW, G, J, NW, NN, A, X, L = c.T, c.D, c.CW, c.G, c.J, c.NW, c.NN, c.A, c.X, c.slab
     any_ = pl.BlockSpec(memory_space=pl.ANY)
     vm = pl.BlockSpec(memory_space=pltpu.VMEM)
@@ -915,20 +913,20 @@
 
     def sums(k, width):
         return [
-            V((k, A, 2, X, 2, L, width), bf16), V((k, A, 2, X, L, width), bf16), V((k, A, X, L, width), bf16),
-            V((k, X, A, L, width), bf16), V((k, A, L, width), bf16),
+            V((k, A, 2, X, 2, L, width), bf16), V((k, A, 2, X, L, width), bf16),
+            V((k, 2, X, A, L, width), bf16), V((k, A, L, width), bf16),
         ]
 
     scratch = [
         V((T, D), bf16), V((T, D), bf16), V((2, T, CW), bf16), V((G, 8, T), f32), V((T, D), bf16), V((T, D), f32),
-        V((2, A, 2, X, 2, L, CW), bf16), V((J - G, D, CW), bf16), V((NW, SLOT, D), bf16), V((c.S, T), bf16),
-        V((D, T), bf16), V((T, D), bf16), V((T, D), bf16), V((T, D), f32), V((T, CW), bf16),
+        V((J, CW, D), bf16), V((NW, SLOT, D), bf16), V((c.S, T), bf16),
+        V((D, T), bf16), V((T, D), bf16), V((T, D), bf16), V((T, D), f32), V((G, T, CW), bf16),
         V((T, PAIR), f32), V((T, PAIR), f32), V((8, T), f32), V((LANES, D), f32),
         V((NW, X, SLOT, D), bf16), V((NW, X, SLOT, D), bf16), V((NW, X, SLOT, D), bf16), V((NW, SLOT, D), bf16),
         V((T, D), bf16),
     ] + sums(J, CW) + sums(1, LANES) + [
-        dma((7,)), dma((2, 2)), dma((2,)), dma((NW + 1,)), dma((NW + 1,)), dma((NW,)), dma((NW,)),
-        dma((4, J + 1)), dma((4, J + 1)),
+        dma((10,)), dma((2, 2)), dma((2,)), dma((NW + 1,)), dma((NW + 1,)), dma((NW,)), dma((NW,)),
+        dma((2, J + 1)), dma((2, J + 1)), dma((J + 1, 2 * X - 1)), dma((J + 1, 2 * X - 1)),
         V((T, D), f32),
     ]
     return pl.pallas_call(
@@ -936,14 +934,14 @@
         out_shape=(
             sds((T, D), bf16), sds((T, D), f32), sds((L, 3 * D), f32), sds((L, D), f32), sds((L, LANES), f32),
         ),
-        in_specs=[any_] * 9 + [vm] * 3,
+        in_specs=[any_] * 10 + [vm] * 3,
         out_specs=(any_, any_, vm, vm, vm),
         scratch_shapes=scratch,
         compiler_params=pltpu.CompilerParams(
-            collective_id=1, has_side_effects=True, vmem_limit_bytes=VMEM_CAP
+            collective_id=CID1, has_side_effects=True, vmem_limit_bytes=VMEM_CAP
         ),
         name="backward",
-    )(v, dy, qkv, lse, att, resid, wall, ret, outp, mrow, meta, cent)
+    )(v, dy, qkv, lse, att, resid, wt, nt, ret, outp, mrow, meta, cent)
 
 
 precise = lax.Precision.HIGHEST
@@ -1211,16 +1209,12 @@
     c = Sizes(mesh, T, D, wq.shape[0], up.shape[2], E)
     if not c.fits:
         return plain_shards(v, idx, caps, g1, wq, wo, g2, centers, up, down, dy)
-    w = lax.axis_index("wide")
-    misc = jnp.concatenate(
-        [centers, jnp.zeros((c.slab, GAIN1 - E), bf16), g1[:, None], g2[:, None]], 1
-    )
-    cap = jnp.broadcast_to(jnp.pad(caps, (0, c.EP - E))[:, None], (c.EP, LANES))
-    res = forward_call(c, v, dy, idx.reshape(1, T), cap, wq, wo, misc, up, down)
-    wall, mall, qkv, lse, att, resid, sent, meta, mrow = res[:9]
-    ret, outp, ug, dg, cent = res[9:]
+    res = forward_call(
+        c, v, dy, idx.reshape(1, T), caps, wq, wo, centers.T, g1.reshape(1, -1), g2.reshape(1, -1), up, down
+    )
+    wt, nt, qkv, lse, att, resid, meta, mrow, ret, outp, ug, dg, cent = res
     mixed, tokens_grad, qg, og, small = backward_call(
-        c, v, dy, qkv, lse, att, resid, wall, ret, outp, mrow, meta, cent
+        c, v, dy, qkv, lse, att, resid, wt, nt, ret, outp, mrow, meta, cent
     )
     return (
         mixed, tokens_grad, small[:, GAIN1], qg, og, small[:, GAIN2], small[:, :E], ug, dg,

time: 216 us -> 181 us (0.84)
  Pallas kernels: 198 us -> 168 us
  local copies, waits for them, and re-layouts: 16.2 us -> 12.6 us
    pallas_call x1, Pallas kernels: 122 us -> 102 us  [forward_call(): pl.pallas_call(functools.partial(forward_kernel, c), out_shape=tuple((o[0...]
    pallas_call x1, Pallas kernels: 76 us -> 65.4 us  [backward_call(): pl.pallas_call(functools.partial(backward_kernel, c), out_shape=(sds((T,...]
    broadcast_in_dim x4 -> x0, local copies, waits for them, and re-layouts: 2.81 us -> none  [the longest x1 1.32 us: shards(): cap = jnp.broadcast_to(jnp.pad(caps, (0, c.EP - E))[:, None], (c.EP, LANES))]
    unnamed x18 -> x17, local copies, waits for them, and re-layouts: 11.7 us -> 11 us
where the time goes in v3:
time: 181 us
  Pallas kernels  168 us (93%)
  local copies, waits for them, and re-layouts  12.6 us (7%)
    pallas_call x1, Pallas kernels, forward_call(): pl.pallas_call(functools.partial(forward_kernel, c), out_shape=tuple((o[0...  102 us
    pallas_call x1, Pallas kernels, backward_call(): pl.pallas_call(functools.partial(backward_kernel, c), out_shape=(sds((T,...  65.4 us
    unnamed x17, local copies, waits for them, and re-layouts  11 us

profile of v3, /device:TPU:0, one launch (start us, length us, event | category | flops | bytes accessed | tf_op | source)
XLA Modules:
  0.0 180.8 jit_solution(6248156379884557995)
XLA Ops:
  0.6 102.1 %forward.1 = (bf16[8,384,768]{2,1,0:T(8,128)(2,1)}, bf16[768,1024]{1,0:T(8,128)(2,1)}, bf16[6,1024,384]{2,1,0:T(8,128)(2,1)}, f32[6,8,1024]{2,1,0:T(8,128)}, bf1...) custom-call(bf16[1024,768]{1,0:T(8,128)(2,1)} %refs_0_.3, ...), custom_call_target="tpu_custom_call" | custom-call | tf_op jit(solution)/shard_map/forward/pallas_call | solution.py:604
  102.8 65.4 %backward.1 = (bf16[1024,768]{1,0:T(8,128)(2,1)}, f32[1024,768]{1,0:T(8,128)}, f32[24,2304]{1,0:T(8,128)}, f32[24,768]{1,0:T(8,128)}, f32[24,128]{1,0:T(8,128)}) custom-call(bf16[1024,768]{1,0:T(8,128)(2,1)} %refs_0_.3, bf16[1024,768]{1,0:T(8,128)(2,1)} %refs_1_.3, bf16[6,1024,384]{2,1,0:T(8,128)(2,1)} %get-tuple-element.27.refs_2_, ...), custom_call_target="tpu_custom_call" | custom-call | tf_op jit(solution)/shard_map/backward/pallas_call | solution.py:932
  168.2 0.0 copy-start
  168.2 1.6 slice_reduce_fusion
  169.8 1.4 copy.21
  171.2 2.7 %copy.28 = bf16[1024,768]{1,0:T(8,128)(2,1)} copy(bf16[1024,768]{1,0:T(8,128)(2,1)} %get-tuple-element.74) | data formatting | bytes 3145728
  173.8 0.0 copy-done
  173.8 0.0 copy-start.3
  173.8 0.0 copy-start.4
  173.8 0.0 copy-start.2
  173.8 1.7 copy.29
  175.5 0.0 copy-done.3
  175.5 0.7 copy.30
  176.2 0.0 copy-done.4
  176.2 0.6 copy.31
  176.8 0.0 copy-done.2
  176.9 0.0 copy-start.1
  176.9 1.4 copy.32
  178.3 1.1 copy-done.1
  179.4 1.4 copy.33
Async XLA Ops:
  168.2 5.6 %copy-start = (f32[1024,768]{1,0:T(8,128)S(1)}, f32[1024,768]{1,0:T(8,128)}, u32[]{:S(2)}) copy-start(f32[1024,768]{1,0:T(8,128)} %get-tuple-element.75) | copy-start | bytes 9437188
  173.8 1.7 copy-start.3
  173.8 2.4 %copy-start.4 = (f32[24,768]{1,0:T(8,128)S(1)}, f32[24,768]{1,0:T(8,128)}, u32[]{:S(2)}) copy-start(f32[24,768]{1,0:T(8,128)} %get-tuple-element.78) | copy-start | bytes 221188
  173.8 3.0 %copy-start.2 = (f32[1,768,768]{2,1,0:T(8,128)S(1)}, f32[1,768,768]{2,1,0:T(8,128)}, u32[]{:S(2)}) copy-start(f32[1,768,768]{2,1,0:T(8,128)} %get-tuple-element.81) | copy-start | bytes 7077892
  176.9 2.5 %copy-start.1 = (f32[1,768,768]{2,1,0:T(8,128)S(1)}, f32[1,768,768]{2,1,0:T(8,128)}, u32[]{:S(2)}) copy-start(f32[1,768,768]{2,1,0:T(8,128)} %get-tuple-element.82) | copy-start | bytes 7077892

commit v4 on v3

--- a/solution.py
+++ b/solution.py
@@ -19,9 +19,10 @@
 VMEM_CAP = 62 << 20
 CID0 = 0
 CID1 = 1
-AHEAD_W = 4
-AHEAD_X = 2
-BEHIND_W = 2
+AHEAD_W = 5
+AHEAD_X = 3
+BEHIND_W = 3
+SHORT = 3
 
 MESH = pl.DeviceIdType.MESH
 NN_ = (((1,), (0,)), ((), ()))
@@ -174,11 +175,11 @@
 def forward_kernel(c, *refs):
     (v_hbm, dy_hbm, idx_ref, cap_ref, wq_hbm, wo_hbm, cen_ref, g1_ref, g2_ref, up_hbm, down_hbm) = refs[:11]
     (w_out, normt_out, qkv_out, lse_out, att_out, resid_out, meta_out, mrow_out) = refs[11:19]
-    (ret_out, outp_out, ug_out, dg_out, cent_out) = refs[19:24]
+    (ret_out, outp_out, ug_out, dg_out, cent_out, mine_out) = refs[19:25]
     (v, nrm, normed, normt, oh, wbuf, wmat, wtr, misc, mrow, qkv, lse, att, sent, sendx, senddy,
      up, down, xin, dyin, hid, dpre, dexp, outp, part, lc, lx, stage, cent,
      lsem, in_sem, out_sem, w_sem, q_sem, st_sem, s1s, s1r, s2s, s2r, s4s, s4r,
-     ds_, dr, xs_, xr, cs_, cr, fs, fr, gs, gr, ks, kr, rs_, rr, ws_, wr) = refs[24:]
+     ds_, dr, xs_, xr, cs_, cr, fs, fr, gs, gr, ks, kr, rs_, rr, ws_, wr) = refs[25:]
     A, X, NW, NN, T, D, CW, G, J = c.A, c.X, c.NW, c.NN, c.T, c.D, c.CW, c.G, c.J
     w, n, a, b, x, cc = place(c)
     own = (a, b, x, cc)
@@ -207,7 +208,9 @@
         [cen_ref[...].astype(f32), jnp.zeros((GAIN1 - c.E, c.slab), f32), g1_ref[...].astype(f32), g2_ref[...].astype(f32)], 0
     )
     small = jnp.concatenate([small, jnp.zeros((LANES, pad), f32)], 1)
-    misc[own] = jnp.transpose(small)[0 : c.slab].astype(bf16)
+    small = jnp.transpose(small)[0 : c.slab]
+    mine_out[...] = small
+    misc[own] = small.astype(bf16)
 
     hot = (lax.broadcasted_iota(jnp.int32, (c.EP, T), 0) == idx_ref[...]).astype(f32)
     lane = lax.broadcasted_iota(jnp.int32, (c.EP, T), 1)
@@ -236,7 +239,8 @@
 
     plane = [(p, q) for p in range(2) for q in range(X) if p or q]
 
-    def s2(j):
+
+    def s2_short(j):
         arrive(buf(j).at[pl.ds(0, A - 1), b, x, cc], s1r.at[j])
         mine = buf(j).at[:, b, x, cc]
         for i, (p, q) in enumerate(plane):
@@ -245,14 +249,36 @@
                 wide=a * 2 + lax.rem(b + p, 2), narrow=lax.rem(x + q, X) * 2 + cc,
             )
 
-    def plane_bytes(j, sem):
+    def s2_long(j):
+        arrive(buf(j).at[pl.ds(0, A - 1), b, x, cc], s1r.at[j])
+        mine = buf(j).at[:, b, x, cc]
+        for q in range(1, X):
+            push(mine, mine, s2s.at[j, q], s2r.at[j, q], narrow=lax.rem(x + q, X) * 2 + cc)
+
+    def s3_long(j):
+        for q in range(1, X):
+            arrive(buf(j).at[:, b, x, cc], s2r.at[j, q])
+        mine = buf(j).at[:, b, :, cc]
+        push(mine, mine, s2s.at[j, 0], s2r.at[j, 0], wide=a * 2 + 1 - b)
+
+    def plane_short(j, sem):
         for i in range(len(plane)):
             arrive(buf(j).at[:, b, x, cc], sem.at[j, i])
 
-    def s4(j):
-        plane_bytes(j, s2r)
+    def plane_long(j, sem):
+        arrive(buf(j).at[:, b, :, cc], sem.at[j, 0])
+
+    def to_core(j):
         mine = buf(j).at[:, :, :, cc]
         push(mine, mine, s4s.at[j], s4r.at[j], narrow=x * 2 + 1 - cc)
+
+    def s4_short(j):
+        plane_short(j, s2r)
+        to_core(j)
+
+    def s4_long(j):
+        plane_long(j, s2r)
+        to_core(j)
 
     def take(j):
         arrive(buf(j).at[:, :, :, cc], s4r.at[j])
@@ -265,13 +291,16 @@
     s1(0)
     oh[...] = (lax.broadcasted_iota(jnp.int32, (c.S, T), 0).astype(f32) == slot).astype(bf16)
     s1(1)
-    s2(J)
-    s2(0)
+    s2_short(J)
+    s1(3)
+    s2_short(0)
     s1(2)
+    s1(4)
     load_wait(0)
     senddy[...] = mm(oh[...], dy[...]).astype(bf16)
-    s2(1)
-    s1(3)
+    s2_short(1)
+    s2_long(3)
+    s1(5)
 
     def dy_w(k):
         to = lax.rem(w + k, NW)
@@ -296,10 +325,11 @@
         return 0
 
     lax.fori_loop(0, T // 128, norm1, 0)
-    s4(J)
-    s4(0)
-    s2(2)
-    s1(4)
+    s4_short(J)
+    s4_short(0)
+    s2_short(2)
+    s2_long(4)
+    s1(6)
     arrive(misc.at[:, :, :, cc], s4r.at[J])
     mrow[...] = jnp.transpose(misc[...].reshape(D, LANES).astype(f32))
     gain1 = mrow[GAIN1 : GAIN1 + 1, :]
@@ -324,15 +354,26 @@
 
         qkv[slot_] = mm(normed[...], wmat[g]).astype(bf16)
         pltpu.make_async_copy(qkv.at[slot_], qkv_out.at[g], q_sem.at[slot_]).start()
-        s4(g + 1)
-
-        @pl.when(g + 3 < J)
-        def _():
-            s2(g + 3)
-
-        @pl.when(g + 5 < J)
-        def _():
-            s1(g + 5)
+
+        @pl.when(g + 1 < SHORT)
+        def _():
+            s4_short(g + 1)
+
+        @pl.when(g + 1 >= SHORT)
+        def _():
+            s4_long(g + 1)
+
+        @pl.when(g + SHORT < J)
+        def _():
+            s3_long(g + SHORT)
+
+        @pl.when(g + SHORT + 2 < J)
+        def _():
+            s2_long(g + SHORT + 2)
+
+        @pl.when(g + SHORT + 4 < J)
+        def _():
+            s1(g + SHORT + 4)
 
         def put_out(rows, val):
             att[rows, pl.ds(pl.multiple_of(g * PAIR, PAIR), PAIR)] = val
@@ -360,7 +401,7 @@
     pltpu.make_async_copy(lse, lse_out, out_sem.at[1]).start()
     pltpu.make_async_copy(att, att_out, out_sem.at[2]).start()
     for j in range(G + 1, J):
-        s4(j)
+        s4_long(j)
     for j in range(G, J):
         take(j)
 
@@ -539,7 +580,12 @@
         if not (isinstance(j, int) and j == J):
             wait_bytes(wtr.at[j], w_sem.at[j])
         arrive(buf(j).at[pl.ds(0, A - 1), b, x, cc], s1s.at[j])
-        plane_bytes(j, s2s)
+        if j == J or j < SHORT:
+            plane_short(j, s2s)
+        else:
+            plane_long(j, s2s)
+            for q in range(1, X):
+                arrive(buf(j).at[:, b, x, cc], s2s.at[j, q])
         arrive(buf(j).at[:, :, :, cc], s4s.at[j])
     arrive(dyin.at[:, :, cc], cs_)
 
@@ -587,6 +633,7 @@
         (sds((1, D, F), f32), any_),
         (sds((1, D, F), f32), any_),
         (sds((8, D), f32), vm),
+        (sds((L, LANES), f32), vm),
     ]
     dma, V = pltpu.SemaphoreType.DMA, pltpu.VMEM
     rows = NW * c.R
@@ -615,12 +662,12 @@
 
 
 def backward_kernel(c, *refs):
-    (v_hbm, dy_hbm, qkv_hbm, lse_hbm, att_hbm, resid_hbm, wt_hbm, nt_hbm, ret_hbm, outp_hbm, mrow, meta, cent) = refs[:13]
-    (mixed_out, tok_out, qg_out, og_out, small_out) = refs[13:18]
+    (v_hbm, dy_hbm, qkv_hbm, lse_hbm, att_hbm, resid_hbm, wt_hbm, nt_hbm, ret_hbm, outp_hbm, mrow, meta, cent, wq, mine) = refs[:15]
+    (mixed_out, tok_out, qg_out, og_out, small_out) = refs[15:20]
     (v, dy, qkv, lse, att, resid, wt, ret, oh, normt, dbr, datt, dnm, dqkv, dk, dv, prod, rowbuf,
      part, lc, lx, got, mixed,
      gb, la, lb, lz, sgb, sla, slb, slz,
-     in_sem, q_sem, out_sem, os_, orv, ows, owr, rs_, rr, ps_, pr, tokacc) = refs[18:]
+     in_sem, q_sem, out_sem, os_, orv, ows, owr, rs_, rr, ps_, pr, tokacc) = refs[20:]
     A, X, NW, NN, T, D, CW, G, J = c.A, c.X, c.NW, c.NN, c.T, c.D, c.CW, c.G, c.J
     H = J - G
     w, n, a, b, x, cc = place(c)
@@ -722,6 +769,8 @@
         for p in range(3):
             qg_out[:, pl.ds(pl.multiple_of(p * D + g * PAIR, PAIR), PAIR)] = total[:, p * PAIR : (p + 1) * PAIR]
 
+    sgb[0] = jnp.transpose(rowbuf[...]).astype(bf16).reshape(A, 2, X, 2, c.slab, LANES)
+    ra(tiny, 0)
     for h in range(H):
         gb[h] = mm(att[...], dbr[:, h * CW : (h + 1) * CW], TN_).astype(bf16).reshape(A, 2, X, 2, c.slab, CW)
         ra(big, h)
@@ -736,10 +785,12 @@
     lax.fori_loop(0, D // QB, out_back, 0)
     load_wait(4)
     load_wait(6)
+    rb(tiny, 0)
     for h in range(H):
         rb(big, h)
     load_wait(5)
     own_part.wait()
+    rc(tiny, 0)
 
     def o_x(i):
         for k in range(1, X):
@@ -833,22 +884,18 @@
     rc(big, J - 2)
     for i in range(1, D // QB):
         back(i)
-    def norm1_back(i, acc):
+    def norm1_back(i, _):
         rows = pl.ds(i * QB, QB)
         n1, r1 = layer_stats(v[rows, :].astype(f32))
-        dm0 = tokacc[rows, :]
-        dm = dm0 * gain1
+        dm = tokacc[rows, :] * gain1
         step = r1 * (dm - jnp.mean(dm, 1, keepdims=True) - n1 * jnp.mean(dm * n1, 1, keepdims=True))
         dnm[rows, :] = dnm[rows, :] + step
-        return acc + jnp.sum(dm0 * n1, 0, keepdims=True)
-
-    rowbuf[GAIN1 : GAIN1 + 1, :] = lax.fori_loop(0, blocks, norm1_back, jnp.zeros((1, D), f32))
+        return 0
+
+    lax.fori_loop(0, blocks, norm1_back, 0)
     tok_copy = pltpu.make_async_copy(dnm, tok_out, out_sem.at[0])
     tok_copy.start()
-    sgb[0] = jnp.transpose(rowbuf[...]).astype(bf16).reshape(A, 2, X, 2, c.slab, LANES)
-    ra(tiny, 0)
     rc(big, J - 1)
-    rb(tiny, 0)
 
     def o_wait(k, _):
         arrive(got.at[0], owr.at[k])
@@ -865,7 +912,6 @@
     lax.fori_loop(0, blocks, mix, 0)
     mix_copy = pltpu.make_async_copy(mixed, mixed_out, out_sem.at[1])
     mix_copy.start()
-    rc(tiny, 0)
     for h in range(H):
         rf_w(h)
 
@@ -874,7 +920,9 @@
         return 0
 
     lax.fori_loop(0, G, fin, 0)
-    small_out[...] = rf(tiny, 0)
+    sums_ = jnp.sum(qg_out[...] * wq[...].astype(f32), 1, keepdims=True) / mine[:, GAIN1 : GAIN1 + 1]
+    at_gain = lax.broadcasted_iota(jnp.int32, (c.slab, LANES), 1) == GAIN1
+    small_out[...] = jnp.where(at_gain, sums_, rf(tiny, 0))
 
     arrive(lc, os_.at[0])
 
@@ -904,7 +952,7 @@
     mix_copy.wait()
 
 
-def backward_call(c, v, dy, qkv, lse, att, resid, wt, nt, ret, outp, mrow, meta, cent):
+def backward_call(c, v, dy, qkv, lse, att, resid, wt, nt, ret, outp, mrow, meta, cent, wq, mine):
     T, D, CW, G, J, NW, NN, A, X, L = c.T, c.D, c.CW, c.G, c.J, c.NW, c.NN, c.A, c.X, c.slab
     any_ = pl.BlockSpec(memory_space=pl.ANY)
     vm = pl.BlockSpec(memory_space=pltpu.VMEM)
@@ -934,14 +982,58 @@
         out_shape=(
             sds((T, D), bf16), sds((T, D), f32), sds((L, 3 * D), f32), sds((L, D), f32), sds((L, LANES), f32),
         ),
-        in_specs=[any_] * 10 + [vm] * 3,
+        in_specs=[any_] * 10 + [vm] * 5,
         out_specs=(any_, any_, vm, vm, vm),
         scratch_shapes=scratch,
         compiler_params=pltpu.CompilerParams(
             collective_id=CID1, has_side_effects=True, vmem_limit_bytes=VMEM_CAP
         ),
         name="backward",
-    )(v, dy, qkv, lse, att, resid, wt, nt, ret, outp, mrow, meta, cent)
+    )(v, dy, qkv, lse, att, resid, wt, nt, ret, outp, mrow, meta, cent, wq, mine)
+
+
+def finish_kernel(c, *refs):
+    big, small = refs[:6], refs[6]
+    outs, (cen_out, g1_out, g2_out) = refs[7:13], refs[13:16]
+    bufs, (in_sem, out_sem) = refs[16:22], refs[22:]
+    cuts = []
+    for i, ref in enumerate(big):
+        axis = len(ref.shape) - 2
+        size = ref.shape[axis]
+        step = QB if size % QB == 0 else size
+        for at in range(0, size, step):
+            where = (0,) * axis + (pl.ds(at, step),)
+            cuts.append((big[i].at[where], bufs[i].at[where], outs[i].at[where]))
+    for k, (src, mid, _) in enumerate(cuts):
+        pltpu.make_async_copy(src, mid, in_sem.at[k]).start()
+    wide_small = jnp.concatenate([small[...], jnp.zeros((LANES - c.slab, LANES), f32)], 0)
+    rows = jnp.transpose(wide_small)[:, 0 : c.slab]
+    cen_out[...] = rows[0 : c.E]
+    g1_out[...] = rows[GAIN1 : GAIN1 + 1]
+    g2_out[...] = rows[GAIN2 : GAIN2 + 1]
+    for k, (src, mid, dst) in enumerate(cuts):
+        pltpu.make_async_copy(src, mid, in_sem.at[k]).wait()
+        pltpu.make_async_copy(mid, dst, out_sem.at[k]).start()
+    for k, (_, mid, dst) in enumerate(cuts):
+        pltpu.make_async_copy(mid, dst, out_sem.at[k]).wait()
+
+
+def finish_call(c, big, small):
+    any_ = pl.BlockSpec(memory_space=pl.ANY)
+    vm = pl.BlockSpec(memory_space=pltpu.VMEM)
+    sds = jax.ShapeDtypeStruct
+    copies = sum(t.shape[-2] // QB if t.shape[-2] % QB == 0 else 1 for t in big)
+    return pl.pallas_call(
+        functools.partial(finish_kernel, c),
+        out_shape=tuple(sds(t.shape, t.dtype) for t in big)
+        + (sds((c.E, c.slab), f32), sds((1, c.slab), f32), sds((1, c.slab), f32)),
+        in_specs=[any_] * 6 + [vm],
+        out_specs=(any_,) * 6 + (vm,) * 3,
+        scratch_shapes=[pltpu.VMEM(t.shape, t.dtype) for t in big]
+        + [pltpu.SemaphoreType.DMA((copies,)), pltpu.SemaphoreType.DMA((copies,))],
+        compiler_params=pltpu.CompilerParams(vmem_limit_bytes=VMEM_CAP),
+        name="finish",
+    )(*big, small)
 
 
 precise = lax.Precision.HIGHEST
@@ -1212,12 +1304,15 @@
     res = forward_call(
         c, v, dy, idx.reshape(1, T), caps, wq, wo, centers.T, g1.reshape(1, -1), g2.reshape(1, -1), up, down
     )
-    wt, nt, qkv, lse, att, resid, meta, mrow, ret, outp, ug, dg, cent = res
+    wt, nt, qkv, lse, att, resid, meta, mrow, ret, outp, ug, dg, cent, mine = res
     mixed, tokens_grad, qg, og, small = backward_call(
-        c, v, dy, qkv, lse, att, resid, wt, nt, ret, outp, mrow, meta, cent
+        c, v, dy, qkv, lse, att, resid, wt, nt, ret, outp, mrow, meta, cent, wq, mine
+    )
+    mixed, tokens_grad, qg, og, ug, dg, cen, g1_grad, g2_grad = finish_call(
+        c, (mixed, tokens_grad, qg, og, ug, dg), small
     )
     return (
-        mixed, tokens_grad, small[:, GAIN1], qg, og, small[:, GAIN2], small[:, :E], ug, dg,
+        mixed, tokens_grad, g1_grad.reshape(-1), qg, og, g2_grad.reshape(-1), cen.T, ug, dg,
     )
 
 

time: 181 us -> 166 us (0.917)
  local copies, waits for them, and re-layouts: 12.6 us -> 0 us
  Pallas kernels: 168 us -> 165 us
    unnamed x17 -> x0, local copies, waits for them, and re-layouts: 11 us -> none
    pallas_call x0 -> x1, Pallas kernels: none -> 8.83 us  [finish_call(): pl.pallas_call(functools.partial(finish_kernel, c), out_shape=tuple((sds(...]
    pallas_call x1, Pallas kernels: 102 us -> 95.1 us  [forward_call(): pl.pallas_call(functools.partial(forward_kernel, c), out_shape=tuple((o[0...]
    pallas_call x1, Pallas kernels: 65.4 us -> 61.1 us  [backward_call(): pl.pallas_call(functools.partial(backward_kernel, c), out_shape=(sds((T,...]
where the time goes in v4:
time: 166 us
  Pallas kernels  165 us (99%)
    pallas_call x1, Pallas kernels, forward_call(): pl.pallas_call(functools.partial(forward_kernel, c), out_shape=tuple((o[0...  95.1 us
    pallas_call x1, Pallas kernels, backward_call(): pl.pallas_call(functools.partial(backward_kernel, c), out_shape=(sds((T,...  61.1 us
    pallas_call x1, Pallas kernels, finish_call(): pl.pallas_call(functools.partial(finish_kernel, c), out_shape=tuple((sds(...  8.83 us

profile of v4, /device:TPU:0, one launch (start us, length us, event | category | flops | bytes accessed | tf_op | source)
XLA Modules:
  0.0 165.9 jit_solution(13370772880742150081)
XLA Ops:
  0.6 95.1 %forward.1 = (bf16[8,384,768]{2,1,0:T(8,128)(2,1)}, bf16[768,1024]{1,0:T(8,128)(2,1)}, bf16[6,1024,384]{2,1,0:T(8,128)(2,1)}, f32[6,8,1024]{2,1,0:T(8,128)}, bf1...) custom-call(bf16[1024,768]{1,0:T(8,128)(2,1)} %refs_0_.3, ...), custom_call_target="tpu_custom_call" | custom-call | tf_op jit(solution)/shard_map/forward/pallas_call | solution.py:651
  95.7 61.1 %backward.1 = (bf16[1024,768]{1,0:T(8,128)(2,1)}, f32[1024,768]{1,0:T(8,128)}, f32[24,2304]{1,0:T(8,128)}, f32[24,768]{1,0:T(8,128)}, f32[24,128]{1,0:T(8,128)}) custom-call(bf16[1024,768]{1,0:T(8,128)(2,1)} %refs_0_.3, bf16[1024,768]{1,0:T(8,128)(2,1)} %refs_1_.3, bf16[6,1024,384]{2,1,0:T(8,128)(2,1)} %get-tuple-element.37.refs_2_, ...), custom_call_target="tpu_custom_call" | custom-call | tf_op jit(solution)/shard_map/backward/pallas_call | solution.py:980
  156.9 8.8 %finish.1 = (bf16[1024,768]{1,0:T(8,128)(2,1)}, f32[1024,768]{1,0:T(8,128)}, f32[24,2304]{1,0:T(8,128)}, f32[24,768]{1,0:T(8,128)}, f32[1,768,768]{2,1,0:T(8,128...) custom-call(bf16[1024,768]{1,0:T(8,128)(2,1)} %get-tuple-element.49.refs_0_, ...), custom_call_target="tpu_custom_call" | custom-call | tf_op jit(solution)/shard_map/finish/pallas_call | solution.py:1026

commit v5 on v4

--- a/solution.py
+++ b/solution.py
@@ -23,6 +23,7 @@
 AHEAD_X = 3
 BEHIND_W = 3
 SHORT = 3
+LAST = 2
 
 MESH = pl.DeviceIdType.MESH
 NN_ = (((1,), (0,)), ((), ()))
@@ -212,6 +213,85 @@
     mine_out[...] = small
     misc[own] = small.astype(bf16)
 
+    met()
+
+    def buf(j):
+        return misc if isinstance(j, int) and j == J else wbuf.at[j]
+
+    def s1(j):
+        if not (isinstance(j, int) and j == J):
+            wait_bytes(buf(j).at[own], lsem.at[j])
+        for k in range(1, A):
+            push(buf(j).at[own], buf(j).at[own], s1s.at[j], s1r.at[j], wide=lax.rem(a + k, A) * 2 + b)
+
+    plane = [(p, q) for p in range(2) for q in range(X) if p or q]
+
+
+    def s2_short(j):
+        arrive(buf(j).at[pl.ds(0, A - 1), b, x, cc], s1r.at[j])
+        mine = buf(j).at[:, b, x, cc]
+        for i, (p, q) in enumerate(plane):
+            push(
+                mine, mine, s2s.at[j, i], s2r.at[j, i],
+                wide=a * 2 + lax.rem(b + p, 2), narrow=lax.rem(x + q, X) * 2 + cc,
+            )
+
+    def s2_long(j):
+        arrive(buf(j).at[pl.ds(0, A - 1), b, x, cc], s1r.at[j])
+        mine = buf(j).at[:, b, x, cc]
+        for q in range(1, X):
+            push(mine, mine, s2s.at[j, q], s2r.at[j, q], narrow=lax.rem(x + q, X) * 2 + cc)
+
+    def s3_long(j):
+        for q in range(1, X):
+            arrive(buf(j).at[:, b, x, cc], s2r.at[j, q])
+        mine = buf(j).at[:, b, :, cc]
+        push(mine, mine, s2s.at[j, 0], s2r.at[j, 0], wide=a * 2 + 1 - b)
+
+    def plane_short(j, sem):
+        for i in range(len(plane)):
+            arrive(buf(j).at[:, b, x, cc], sem.at[j, i])
+
+    def plane_long(j, sem):
+        arrive(buf(j).at[:, b, :, cc], sem.at[j, 0])
+
+    def to_core(j):
+        mine = buf(j).at[:, :, :, cc]
+        push(mine, mine, s4s.at[j], s4r.at[j], narrow=x * 2 + 1 - cc)
+
+    def s4_short(j):
+        plane_short(j, s2r)
+        to_core(j)
+
+    def s4_long(j):
+        plane_long(j, s2r)
+        to_core(j)
+
+    def take(j, turn=True):
+        arrive(buf(j).at[:, :, :, cc], s4r.at[j])
+        val = wbuf[j].reshape(D, CW)
+        wmat[j] = val
+        if turn:
+            turned(j, val)
+
+    def turned(j, val):
+        wtr[j] = jnp.transpose(val)
+        pltpu.make_async_copy(wtr.at[j], w_out.at[j], w_sem.at[j]).start()
+
+    def due(t):
+        for j in range(J):
+            short = j < SHORT
+            if t == (j + 4):
+                (s4_short if short else s4_long)(j)
+            if not short and t == j + 2:
+                s3_long(j)
+            if t == (j + 2 if short else j):
+                (s2_short if short else s2_long)(j)
+            if t == (j if short else max(j - 2, 1)):
+                s1(j)
+
+    s1(J)
+    due(0)
     hot = (lax.broadcasted_iota(jnp.int32, (c.EP, T), 0) == idx_ref[...]).astype(f32)
     lane = lax.broadcasted_iota(jnp.int32, (c.EP, T), 1)
     count = hot
@@ -226,81 +306,13 @@
     kept = rank < ceiling
     slot = jnp.where(kept, idx_ref[...].astype(f32) * SLOT + rank, -1.0)
 
-    met()
-
-    def buf(j):
-        return misc if isinstance(j, int) and j == J else wbuf.at[j]
-
-    def s1(j):
-        if not (isinstance(j, int) and j == J):
-            wait_bytes(buf(j).at[own], lsem.at[j])
-        for k in range(1, A):
-            push(buf(j).at[own], buf(j).at[own], s1s.at[j], s1r.at[j], wide=lax.rem(a + k, A) * 2 + b)
-
-    plane = [(p, q) for p in range(2) for q in range(X) if p or q]
-
-
-    def s2_short(j):
-        arrive(buf(j).at[pl.ds(0, A - 1), b, x, cc], s1r.at[j])
-        mine = buf(j).at[:, b, x, cc]
-        for i, (p, q) in enumerate(plane):
-            push(
-                mine, mine, s2s.at[j, i], s2r.at[j, i],
-                wide=a * 2 + lax.rem(b + p, 2), narrow=lax.rem(x + q, X) * 2 + cc,
-            )
-
-    def s2_long(j):
-        arrive(buf(j).at[pl.ds(0, A - 1), b, x, cc], s1r.at[j])
-        mine = buf(j).at[:, b, x, cc]
-        for q in range(1, X):
-            push(mine, mine, s2s.at[j, q], s2r.at[j, q], narrow=lax.rem(x + q, X) * 2 + cc)
-
-    def s3_long(j):
-        for q in range(1, X):
-            arrive(buf(j).at[:, b, x, cc], s2r.at[j, q])
-        mine = buf(j).at[:, b, :, cc]
-        push(mine, mine, s2s.at[j, 0], s2r.at[j, 0], wide=a * 2 + 1 - b)
-
-    def plane_short(j, sem):
-        for i in range(len(plane)):
-            arrive(buf(j).at[:, b, x, cc], sem.at[j, i])
-
-    def plane_long(j, sem):
-        arrive(buf(j).at[:, b, :, cc], sem.at[j, 0])
-
-    def to_core(j):
-        mine = buf(j).at[:, :, :, cc]
-        push(mine, mine, s4s.at[j], s4r.at[j], narrow=x * 2 + 1 - cc)
-
-    def s4_short(j):
-        plane_short(j, s2r)
-        to_core(j)
-
-    def s4_long(j):
-        plane_long(j, s2r)
-        to_core(j)
-
-    def take(j):
-        arrive(buf(j).at[:, :, :, cc], s4r.at[j])
-        val = wbuf[j].reshape(D, CW)
-        wmat[j] = val
-        wtr[j] = jnp.transpose(val)
-        pltpu.make_async_copy(wtr.at[j], w_out.at[j], w_sem.at[j]).start()
-
-    s1(J)
-    s1(0)
+    due(1)
+    s2_short(J)
     oh[...] = (lax.broadcasted_iota(jnp.int32, (c.S, T), 0).astype(f32) == slot).astype(bf16)
-    s1(1)
-    s2_short(J)
-    s1(3)
-    s2_short(0)
-    s1(2)
-    s1(4)
+    due(2)
     load_wait(0)
     senddy[...] = mm(oh[...], dy[...]).astype(bf16)
-    s2_short(1)
-    s2_long(3)
-    s1(5)
+    due(3)
 
     def dy_w(k):
         to = lax.rem(w + k, NW)
@@ -326,10 +338,7 @@
 
     lax.fori_loop(0, T // 128, norm1, 0)
     s4_short(J)
-    s4_short(0)
-    s2_short(2)
-    s2_long(4)
-    s1(6)
+    due(4)
     arrive(misc.at[:, :, :, cc], s4r.at[J])
     mrow[...] = jnp.transpose(misc[...].reshape(D, LANES).astype(f32))
     gain1 = mrow[GAIN1 : GAIN1 + 1, :]
@@ -355,25 +364,18 @@
         qkv[slot_] = mm(normed[...], wmat[g]).astype(bf16)
         pltpu.make_async_copy(qkv.at[slot_], qkv_out.at[g], q_sem.at[slot_]).start()
 
-        @pl.when(g + 1 < SHORT)
-        def _():
-            s4_short(g + 1)
-
-        @pl.when(g + 1 >= SHORT)
-        def _():
-            s4_long(g + 1)
-
-        @pl.when(g + SHORT < J)
-        def _():
-            s3_long(g + SHORT)
-
-        @pl.when(g + SHORT + 2 < J)
-        def _():
-            s2_long(g + SHORT + 2)
-
-        @pl.when(g + SHORT + 4 < J)
-        def _():
-            s1(g + SHORT + 4)
+        def at_step(fn, j, wanted):
+            @pl.when(wanted & (j < J))
+            def _():
+                fn(j)
+
+        at_step(s4_short, g + 1, g + 1 < SHORT)
+        at_step(s4_long, g + 1, g + 1 >= SHORT)
+        at_step(s3_long, g + 3, g + 3 >= SHORT)
+        at_step(s2_short, g + 3, g + 3 < SHORT)
+        at_step(s2_long, g + 5, g + 5 >= SHORT)
+        at_step(s1, g + 5, g + 5 < SHORT)
+        at_step(s1, g + 7, g + 7 >= SHORT)
 
         def put_out(rows, val):
             att[rows, pl.ds(pl.multiple_of(g * PAIR, PAIR), PAIR)] = val
@@ -383,6 +385,11 @@
 
         for i in range(T // QB):
             if i == T // QB - 1:
+                @pl.when(g == G - 1)
+                def _():
+                    for j in range(G + 1, J):
+                        (s4_short if j < SHORT else s4_long)(j)
+
                 for q in range(per):
                     k = g * per + q
 
@@ -400,12 +407,9 @@
     lax.fori_loop(0, G, pair, 0)
     pltpu.make_async_copy(lse, lse_out, out_sem.at[1]).start()
     pltpu.make_async_copy(att, att_out, out_sem.at[2]).start()
-    for j in range(G + 1, J):
-        s4_long(j)
+
     for j in range(G, J):
-        take(j)
-
-    for j in range(G, J):
+        take(j, False)
         at = slice((j - G) * CW, (j - G + 1) * CW)
         nrm[:, at] = v[:, at].astype(f32) + mm(att[...], wmat[j])
 
@@ -499,6 +503,8 @@
             pltpu.make_async_copy(part.at[src, x, cc], ret_out.at[w], ws_.at[0]).start()
 
     fwd_x(0)
+    for j in range(G, J):
+        turned(j, wmat[j])
     normt[...] = jnp.transpose(normed[...])
     pltpu.make_async_copy(normt, normt_out, out_sem.at[5]).start()
     for k in range(per * (G - 2), NW):
@@ -562,7 +568,7 @@
             at = pl.ds(pl.multiple_of(i * QB, QB), QB)
             if second:
                 wait_bytes(stage.at[i], st_sem.at[i])
-            stage[i] = mm(lhs(at), rhs[...], TN_)
+            stage[i] = mm(lhs(at), rhs[...], TN_).astype(bf16)
             pltpu.make_async_copy(stage.at[i], out.at[0, at], st_sem.at[i]).start()
             return 0
 
@@ -630,8 +636,8 @@
         (sds((LANES, D), f32), any_),
         (sds((NW, SLOT, D), bf16), any_),
         (sds(rows_, bf16), any_),
-        (sds((1, D, F), f32), any_),
-        (sds((1, D, F), f32), any_),
+        (sds((1, D, F), bf16), any_),
+        (sds((1, D, F), bf16), any_),
         (sds((8, D), f32), vm),
         (sds((L, LANES), f32), vm),
     ]
@@ -643,7 +649,7 @@
         V((2, T, CW), bf16), V((G, 8, T), f32), V((T, D), bf16), V((T, D), bf16), V((c.S, D), bf16), V((c.S, D), bf16),
         V((D, F), bf16), V((D, F), bf16), V(rows_, bf16), V(rows_, bf16),
         V((rows, F), bf16), V((rows, F), bf16), V((rows, D), bf16), V(rows_, bf16), V(rows_, bf16),
-        V((NW, X, SLOT, D), bf16), V((NW, X, SLOT, D), bf16), V((D // QB, QB, F), f32), V((8, D), f32),
+        V((NW, X, SLOT, D), bf16), V((NW, X, SLOT, D), bf16), V((D // QB, QB, F), bf16), V((8, D), f32),
         dma((J,)), dma((4,)), dma((6,)), dma((J,)), dma((2,)), dma((D // QB,)),
     ] + [dma((J + 1,))] * 2 + [dma((J + 1, 2 * X - 1))] * 2 + [dma((J + 1,))] * 2 + [dma((NW,))] * 4 + [dma(()), dma(())] + [dma((NW,))] * 6 + [
         dma((2, NW)), dma((2, NW)), dma((NW,)), dma((NW,)),
@@ -666,7 +672,7 @@
     (mixed_out, tok_out, qg_out, og_out, small_out) = refs[15:20]
     (v, dy, qkv, lse, att, resid, wt, ret, oh, normt, dbr, datt, dnm, dqkv, dk, dv, prod, rowbuf,
      part, lc, lx, got, mixed,
-     gb, la, lb, lz, sgb, sla, slb, slz,
+     gb, la, lb, lz, sgb, sla, slb, slz, lxx,
      in_sem, q_sem, out_sem, os_, orv, ows, owr, rs_, rr, ps_, pr, tokacc) = refs[20:]
     A, X, NW, NN, T, D, CW, G, J = c.A, c.X, c.NW, c.NN, c.T, c.D, c.CW, c.G, c.J
     H = J - G
@@ -719,7 +725,7 @@
     rowbuf[GAIN2 : GAIN2 + 1, :] = lax.fori_loop(0, blocks, norm2_back, jnp.zeros((1, D), f32))
     load_wait(3)
 
-    big = (gb, la, lb, lz, 0)
+    big = (gb, la, lb, lz, 0, lxx)
     tiny = (sgb, sla, slb, slz, J)
 
     def add(p, q):
@@ -730,29 +736,65 @@
 
     plane = [(p, q) for p in range(2) for q in range(X) if p or q]
 
-    def rb(t, j):
+    plane = [(p, q) for p in range(2) for q in range(X) if p or q]
+
+    def join(t, j):
         arrive(t[1].at[j], rr.at[0, t[4] + j])
         t[0][j, :, :, :, cc] = add(t[0][j, :, :, :, cc], t[1][j])
-        for i, (p, q) in enumerate(plane):
-            b2, x2 = lax.rem(b + p, 2), lax.rem(x + q, X)
-            push(
-                t[0].at[j, :, b2, x2, cc], t[2].at[j, b, x], ps_.at[t[4] + j, i], pr.at[t[4] + j, i],
-                wide=a * 2 + b2, narrow=x2 * 2 + cc,
-            )
-
-    def plane_bytes(t, j, sem):
-        for i in range(len(plane)):
-            arrive(t[2].at[j, 0, 0], sem.at[t[4] + j, i])
-
-    def rc(t, j):
-        plane_bytes(t, j, pr)
-        total = t[0][j, :, b, x, cc].astype(f32)
-        for p, q in plane:
-            total = total + t[2][j, lax.rem(b + p, 2), lax.rem(x + q, X)].astype(f32)
+
+    def to_plane(t, j, i, src, dst, p, q):
+        push(
+            src, dst, ps_.at[t[4] + j, i], pr.at[t[4] + j, i],
+            wide=a * 2 + lax.rem(b + p, 2), narrow=lax.rem(x + q, X) * 2 + cc,
+        )
+
+    def to_outer(t, j, total):
         t[0][j, :, b, x, cc] = total.astype(bf16)
         for k in range(1, A):
             a2 = lax.rem(a + k, A)
             push(t[0].at[j, a2, b, x, cc], t[3].at[j, a], rs_.at[1, t[4] + j], rr.at[1, t[4] + j], wide=a2 * 2 + b)
+
+    def rb_short(t, j):
+        join(t, j)
+        for i, (p, q) in enumerate(plane):
+            to_plane(t, j, i, t[0].at[j, :, lax.rem(b + p, 2), lax.rem(x + q, X), cc], t[2].at[j, b, x], p, q)
+
+    def rc_short(t, j):
+        plane_short(t, j, pr)
+        total = t[0][j, :, b, x, cc].astype(f32)
+        for p, q in plane:
+            total = total + t[2][j, lax.rem(b + p, 2), lax.rem(x + q, X)].astype(f32)
+        to_outer(t, j, total)
+
+    def plane_short(t, j, sem):
+        for i in range(len(plane)):
+            arrive(t[2].at[j, 0, 0], sem.at[t[4] + j, i])
+
+    def rb_long(t, j):
+        join(t, j)
+        for q in range(X):
+            t[2][j, b, q] = t[0][j, :, 1 - b, q, cc]
+        to_plane(t, j, 0, t[2].at[j, b], t[2].at[j, b], 1, 0)
+
+    def rc_long(t, j):
+        arrive(t[2].at[j, 0], pr.at[t[4] + j, 0])
+        for q in range(X):
+            t[0][j, :, b, q, cc] = add(t[0][j, :, b, q, cc], t[2][j, 1 - b, q])
+        for q in range(1, X):
+            to_plane(t, j, q, t[0].at[j, :, b, lax.rem(x + q, X), cc], t[5].at[j, x], 0, q)
+
+    def rd_long(t, j):
+        for q in range(1, X):
+            arrive(t[2].at[j, 0, 0], pr.at[t[4] + j, q])
+        total = t[0][j, :, b, x, cc].astype(f32)
+        for q in range(1, X):
+            total = total + t[5][j, lax.rem(x + q, X)].astype(f32)
+        to_outer(t, j, total)
+
+    def plane_long(t, j, sem):
+        arrive(t[2].at[j, 0], sem.at[t[4] + j, 0])
+        for q in range(1, X):
+            arrive(t[2].at[j, 0, 0], sem.at[t[4] + j, q])
 
     def rf(t, j):
         arrive(t[3].at[j, pl.ds(0, A - 1)], rr.at[1, t[4] + j])
@@ -785,12 +827,11 @@
     lax.fori_loop(0, D // QB, out_back, 0)
     load_wait(4)
     load_wait(6)
-    rb(tiny, 0)
+    rb_short(tiny, 0)
     for h in range(H):
-        rb(big, h)
+        rb_long(big, h)
     load_wait(5)
     own_part.wait()
-    rc(tiny, 0)
 
     def o_x(i):
         for k in range(1, X):
@@ -848,12 +889,25 @@
 
         for i in reversed(range(blocks)):
             if i == 0:
-                rc(big, g + H - 2)
+                @pl.when(g == 0)
+                def _():
+                    rc_short(tiny, 0)
+
+                rc_long(big, g)
+
+                @pl.when(g >= 1)
+                def _():
+                    rd_long(big, g - 1)
+
             attend_rows_back(qkv.at[s_], att_g, datt_g, lse.at[g], i, i == blocks - 1, prod, dk, dv, put_dq)
             if i == blocks - 1:
-                @pl.when(g >= 1)
+                @pl.when((g >= 1) & (g + H - 1 < J - LAST))
                 def _():
-                    rb(big, g + H - 1)
+                    rb_long(big, g + H - 1)
+
+                @pl.when((g >= 1) & (g + H - 1 >= J - LAST))
+                def _():
+                    rb_short(big, g + H - 1)
 
                 @pl.when(g < 4)
                 def _():
@@ -880,8 +934,10 @@
         tokacc[:, at] = total
 
     back(0)
-    rb(big, J - 1)
-    rc(big, J - 2)
+    rb_short(big, J - 1)
+    rd_long(big, J - LAST - 1)
+    for j in range(J - LAST, J - 1):
+        rc_short(big, j)
     for i in range(1, D // QB):
         back(i)
     def norm1_back(i, _):
@@ -889,13 +945,13 @@
         n1, r1 = layer_stats(v[rows, :].astype(f32))
         dm = tokacc[rows, :] * gain1
         step = r1 * (dm - jnp.mean(dm, 1, keepdims=True) - n1 * jnp.mean(dm * n1, 1, keepdims=True))
-        dnm[rows, :] = dnm[rows, :] + step
+        dbr[rows, :] = (dnm[rows, :] + step).astype(bf16)
         return 0
 
     lax.fori_loop(0, blocks, norm1_back, 0)
-    tok_copy = pltpu.make_async_copy(dnm, tok_out, out_sem.at[0])
+    tok_copy = pltpu.make_async_copy(dbr, tok_out, out_sem.at[0])
     tok_copy.start()
-    rc(big, J - 1)
+    rc_short(big, J - 1)
 
     def o_wait(k, _):
         arrive(got.at[0], owr.at[k])
@@ -937,17 +993,14 @@
 
     lax.fori_loop(0, NW, drain, 0)
 
-    def drain_sums(t, j):
+    def drain_sums(t, j, route):
         arrive(t[1].at[j], rs_.at[0, t[4] + j])
-        plane_bytes(t, j, ps_)
+        route(t, j, ps_)
         arrive(t[3].at[j, pl.ds(0, A - 1)], rs_.at[1, t[4] + j])
 
-    def drain_big(j, _):
-        drain_sums(big, j)
-        return 0
-
-    lax.fori_loop(0, J, drain_big, 0)
-    drain_sums(tiny, 0)
+    for j in range(J):
+        drain_sums(big, j, plane_long if j < J - LAST else plane_short)
+    drain_sums(tiny, 0, plane_short)
     tok_copy.wait()
     mix_copy.wait()
 
@@ -973,6 +1026,7 @@
         V((NW, X, SLOT, D), bf16), V((NW, X, SLOT, D), bf16), V((NW, X, SLOT, D), bf16), V((NW, SLOT, D), bf16),
         V((T, D), bf16),
     ] + sums(J, CW) + sums(1, LANES) + [
+        V((J, X, A, L, CW), bf16),
         dma((10,)), dma((2, 2)), dma((2,)), dma((NW + 1,)), dma((NW + 1,)), dma((NW,)), dma((NW,)),
         dma((2, J + 1)), dma((2, J + 1)), dma((J + 1, 2 * X - 1)), dma((J + 1, 2 * X - 1)),
         V((T, D), f32),
@@ -980,7 +1034,7 @@
     return pl.pallas_call(
         functools.partial(backward_kernel, c),
         out_shape=(
-            sds((T, D), bf16), sds((T, D), f32), sds((L, 3 * D), f32), sds((L, D), f32), sds((L, LANES), f32),
+            sds((T, D), bf16), sds((T, D), bf16), sds((L, 3 * D), f32), sds((L, D), f32), sds((L, LANES), f32),
         ),
         in_specs=[any_] * 10 + [vm] * 5,
         out_specs=(any_, any_, vm, vm, vm),
@@ -992,44 +1046,49 @@
     )(v, dy, qkv, lse, att, resid, wt, nt, ret, outp, mrow, meta, cent, wq, mine)
 
 
+def cuts_of(shape):
+    axis, size = len(shape) - 2, shape[-2]
+    step = QB if size % QB == 0 else size
+    return [(0,) * axis + (pl.ds(at, step),) for at in range(0, size, step)]
+
+
 def finish_kernel(c, *refs):
     big, small = refs[:6], refs[6]
     outs, (cen_out, g1_out, g2_out) = refs[7:13], refs[13:16]
-    bufs, (in_sem, out_sem) = refs[16:22], refs[22:]
-    cuts = []
-    for i, ref in enumerate(big):
-        axis = len(ref.shape) - 2
-        size = ref.shape[axis]
-        step = QB if size % QB == 0 else size
-        for at in range(0, size, step):
-            where = (0,) * axis + (pl.ds(at, step),)
-            cuts.append((big[i].at[where], bufs[i].at[where], outs[i].at[where]))
-    for k, (src, mid, _) in enumerate(cuts):
-        pltpu.make_async_copy(src, mid, in_sem.at[k]).start()
+    held, wide, (in_sem, out_sem) = refs[16:22], refs[22:28], refs[28:]
+    cuts = [(i, where) for i in range(6) for where in cuts_of(big[i].shape)]
+    for k, (i, where) in enumerate(cuts):
+        pltpu.make_async_copy(big[i].at[where], held[i].at[where], in_sem.at[k]).start()
     wide_small = jnp.concatenate([small[...], jnp.zeros((LANES - c.slab, LANES), f32)], 0)
     rows = jnp.transpose(wide_small)[:, 0 : c.slab]
     cen_out[...] = rows[0 : c.E]
     g1_out[...] = rows[GAIN1 : GAIN1 + 1]
     g2_out[...] = rows[GAIN2 : GAIN2 + 1]
-    for k, (src, mid, dst) in enumerate(cuts):
-        pltpu.make_async_copy(src, mid, in_sem.at[k]).wait()
-        pltpu.make_async_copy(mid, dst, out_sem.at[k]).start()
-    for k, (_, mid, dst) in enumerate(cuts):
-        pltpu.make_async_copy(mid, dst, out_sem.at[k]).wait()
-
-
-def finish_call(c, big, small):
+    for k, (i, where) in enumerate(cuts):
+        pltpu.make_async_copy(big[i].at[where], held[i].at[where], in_sem.at[k]).wait()
+        src = held[i]
+        if held[i].dtype != outs[i].dtype:
+            wide[i][where] = held[i][where].astype(f32)
+            src = wide[i]
+        pltpu.make_async_copy(src.at[where], outs[i].at[where], out_sem.at[k]).start()
+    for k, (i, where) in enumerate(cuts):
+        src = wide[i] if held[i].dtype != outs[i].dtype else held[i]
+        pltpu.make_async_copy(src.at[where], outs[i].at[where], out_sem.at[k]).wait()
+
+
+def finish_call(c, big, kinds, small):
     any_ = pl.BlockSpec(memory_space=pl.ANY)
     vm = pl.BlockSpec(memory_space=pltpu.VMEM)
-    sds = jax.ShapeDtypeStruct
-    copies = sum(t.shape[-2] // QB if t.shape[-2] % QB == 0 else 1 for t in big)
+    sds, V = jax.ShapeDtypeStruct, pltpu.VMEM
+    copies = sum(len(cuts_of(t.shape)) for t in big)
     return pl.pallas_call(
         functools.partial(finish_kernel, c),
-        out_shape=tuple(sds(t.shape, t.dtype) for t in big)
+        out_shape=tuple(sds(t.shape, k) for t, k in zip(big, kinds))
         + (sds((c.E, c.slab), f32), sds((1, c.slab), f32), sds((1, c.slab), f32)),
         in_specs=[any_] * 6 + [vm],
         out_specs=(any_,) * 6 + (vm,) * 3,
-        scratch_shapes=[pltpu.VMEM(t.shape, t.dtype) for t in big]
+        scratch_shapes=[V(t.shape, t.dtype) for t in big]
+        + [V(t.shape if t.dtype != k else (8, LANES), f32) for t, k in zip(big, kinds)]
         + [pltpu.SemaphoreType.DMA((copies,)), pltpu.SemaphoreType.DMA((copies,))],
         compiler_params=pltpu.CompilerParams(vmem_limit_bytes=VMEM_CAP),
         name="finish",
@@ -1308,8 +1367,8 @@
     mixed, tokens_grad, qg, og, small = backward_call(
         c, v, dy, qkv, lse, att, resid, wt, nt, ret, outp, mrow, meta, cent, wq, mine
     )
-    mixed, tokens_grad, qg, og, ug, dg, cen, g1_grad, g2_grad = finish_call(
-        c, (mixed, tokens_grad, qg, og, ug, dg), small
+    ug, dg, tokens_grad, mixed, qg, og, cen, g1_grad, g2_grad = finish_call(
+        c, (ug, dg, tokens_grad, mixed, qg, og), (f32, f32, f32, bf16, f32, f32), small
     )
     return (
         mixed, tokens_grad, g1_grad.reshape(-1), qg, og, g2_grad.reshape(-1), cen.T, ug, dg,

time: 166 us -> 163 us (0.982)
  Pallas kernels: 165 us -> 162 us
    pallas_call x1, Pallas kernels: 8.83 us -> 6.55 us  [finish_call(): pl.pallas_call(functools.partial(finish_kernel, c), out_shape=tuple((sds(...]
where the time goes in v5:
time: 163 us; the launch traced here: 162 us
  Pallas kernels  162 us (99%)
    pallas_call x1, Pallas kernels, forward_call(): pl.pallas_call(functools.partial(forward_kernel, c), out_shape=tuple((o[0...  95.4 us
    pallas_call x1, Pallas kernels, backward_call(): pl.pallas_call(functools.partial(backward_kernel, c), out_shape=(sds((T,...  59.6 us
    pallas_call x1, Pallas kernels, finish_call(): pl.pallas_call(functools.partial(finish_kernel, c), out_shape=tuple((sds(...  6.55 us

profile of v5, /device:TPU:0, one launch (start us, length us, event | category | flops | bytes accessed | tf_op | source)
XLA Modules:
  0.0 162.4 jit_solution(2271635867372932796)
XLA Ops:
  0.6 95.4 %forward.1 = (bf16[8,384,768]{2,1,0:T(8,128)(2,1)}, bf16[768,1024]{1,0:T(8,128)(2,1)}, bf16[6,1024,384]{2,1,0:T(8,128)(2,1)}, f32[6,8,1024]{2,1,0:T(8,128)}, bf1...) custom-call(bf16[1024,768]{1,0:T(8,128)(2,1)} %refs_0_.3, ...), custom_call_target="tpu_custom_call" | custom-call | tf_op jit(solution)/shard_map/forward/pallas_call | solution.py:657
  96.0 59.6 %backward.1 = (bf16[1024,768]{1,0:T(8,128)(2,1)}, bf16[1024,768]{1,0:T(8,128)(2,1)}, f32[24,2304]{1,0:T(8,128)}, f32[24,768]{1,0:T(8,128)}, f32[24,128]{1,0:T(8,128)}) custom-call(bf16[1024,768]{1,0:T(8,128)(2,1)} %refs_0_.3, bf16[1024,768]{1,0:T(8,128)(2,1)} %refs_1_.3, bf16[6,1024,384]{2,1,0:T(8,128)(2,1)} %get-tuple-element.39.refs_2_, ...), custom_call_target="tpu_custom_call" | custom-call | tf_op jit(solution)/shard_map/backward/pallas_call | solution.py:1034
  155.7 6.5 %finish.1 = (f32[1,768,768]{2,1,0:T(8,128)}, f32[1,768,768]{2,1,0:T(8,128)}, f32[1024,768]{1,0:T(8,128)}, bf16[1024,768]{1,0:T(8,128)(2,1)}, f32[24,2304]{1,0:T(...) custom-call(bf16[1,768,768]{2,1,0:T(8,128)(2,1)} %get-tuple-element.37.refs_0_, ...), custom_call_target="tpu_custom_call" | custom-call | tf_op jit(solution)/shard_map/finish/pallas_call | solution.py:1084

commit v6 on v5

--- a/solution.py
+++ b/solution.py
@@ -503,25 +503,26 @@
             pltpu.make_async_copy(part.at[src, x, cc], ret_out.at[w], ws_.at[0]).start()
 
     fwd_x(0)
+    for k in range(per * (G - 2), NW):
+        dy_x(k)
+
+    def dy_all(k, _):
+        arrive(dyin.at[w, x, cc], xr.at[k])
+        return 0
+
+    for q in range(X - 1):
+        lax.fori_loop(0, NW, dy_all, 0)
+    push(dyin.at[:, :, cc], dyin.at[:, :, cc], cs_, cr, narrow=x * 2 + 1 - cc)
     for j in range(G, J):
         turned(j, wmat[j])
     normt[...] = jnp.transpose(normed[...])
     pltpu.make_async_copy(normt, normt_out, out_sem.at[5]).start()
-    for k in range(per * (G - 2), NW):
-        dy_x(k)
 
     logits = mm(mrow[0 : c.EP, :].astype(bf16), sent[...], NT_)
     gate = jax.nn.sigmoid(jnp.sum(logits * hot, 0, keepdims=True)) * kept.astype(f32)
     meta_out[...] = jnp.concatenate([slot, gate, jnp.zeros((6, T), f32)], 0)
     cent[...] = jnp.zeros_like(cent)
 
-    def dy_all(k, _):
-        arrive(dyin.at[w, x, cc], xr.at[k])
-        return 0
-
-    for q in range(X - 1):
-        lax.fori_loop(0, NW, dy_all, 0)
-    push(dyin.at[:, :, cc], dyin.at[:, :, cc], cs_, cr, narrow=x * 2 + 1 - cc)
     fwd_c(0)
     for k in range(1, AHEAD_X):
         fwd_x(k)
@@ -704,8 +705,6 @@
     load_wait(0)
     dnm[...] = mm(oh[...], ret[...].reshape(c.S, D), TN_)
     oh[...] = jnp.where(hits, gate, 0.0).astype(bf16)
-    met()
-    push(outp_hbm.at[:, :, 1 - cc], lc, os_.at[0], orv.at[0], narrow=x * 2 + 1 - cc)
     load_wait(1)
     load_wait(2)
     rowbuf[...] = jnp.zeros_like(rowbuf)
@@ -812,9 +811,12 @@
             qg_out[:, pl.ds(pl.multiple_of(p * D + g * PAIR, PAIR), PAIR)] = total[:, p * PAIR : (p + 1) * PAIR]
 
     sgb[0] = jnp.transpose(rowbuf[...]).astype(bf16).reshape(A, 2, X, 2, c.slab, LANES)
-    ra(tiny, 0)
     for h in range(H):
         gb[h] = mm(att[...], dbr[:, h * CW : (h + 1) * CW], TN_).astype(bf16).reshape(A, 2, X, 2, c.slab, CW)
+        if h == 0:
+            met()
+            push(outp_hbm.at[:, :, 1 - cc], lc, os_.at[0], orv.at[0], narrow=x * 2 + 1 - cc)
+            ra(tiny, 0)
         ra(big, h)
 
     load_wait(7)
@@ -900,7 +902,7 @@
                     rd_long(big, g - 1)
 
             attend_rows_back(qkv.at[s_], att_g, datt_g, lse.at[g], i, i == blocks - 1, prod, dk, dv, put_dq)
-            if i == blocks - 1:
+            if i == blocks - 2:
                 @pl.when((g >= 1) & (g + H - 1 < J - LAST))
                 def _():
                     rb_long(big, g + H - 1)

time: 163 us -> 162 us (level)
  no operation moved by 1% of the time
where the time goes in v6:
time: 162 us; the launch traced here: 161 us
  Pallas kernels  161 us (99%)
    pallas_call x1, Pallas kernels, forward_call(): pl.pallas_call(functools.partial(forward_kernel, c), out_shape=tuple((o[0...  95.4 us
    pallas_call x1, Pallas kernels, backward_call(): pl.pallas_call(functools.partial(backward_kernel, c), out_shape=(sds((T,...  58.6 us
    pallas_call x1, Pallas kernels, finish_call(): pl.pallas_call(functools.partial(finish_kernel, c), out_shape=tuple((sds(...  6.55 us

profile of v6, /device:TPU:0, one launch (start us, length us, event | category | flops | bytes accessed | tf_op | source)
XLA Modules:
  0.0 161.4 jit_solution(6567173962925930648)
XLA Ops:
  0.6 95.4 %forward.1 = (bf16[8,384,768]{2,1,0:T(8,128)(2,1)}, bf16[768,1024]{1,0:T(8,128)(2,1)}, bf16[6,1024,384]{2,1,0:T(8,128)(2,1)}, f32[6,8,1024]{2,1,0:T(8,128)}, bf1...) custom-call(bf16[1024,768]{1,0:T(8,128)(2,1)} %refs_0_.3, ...), custom_call_target="tpu_custom_call" | custom-call | tf_op jit(solution)/shard_map/forward/pallas_call | solution.py:658
  96.0 58.6 %backward.1 = (bf16[1024,768]{1,0:T(8,128)(2,1)}, bf16[1024,768]{1,0:T(8,128)(2,1)}, f32[24,2304]{1,0:T(8,128)}, f32[24,768]{1,0:T(8,128)}, f32[24,128]{1,0:T(8,128)}) custom-call(bf16[1024,768]{1,0:T(8,128)(2,1)} %refs_0_.3, bf16[1024,768]{1,0:T(8,128)(2,1)} %refs_1_.3, bf16[6,1024,384]{2,1,0:T(8,128)(2,1)} %get-tuple-element.39.refs_2_, ...), custom_call_target="tpu_custom_call" | custom-call | tf_op jit(solution)/shard_map/backward/pallas_call | solution.py:1036
  154.7 6.5 %finish.1 = (f32[1,768,768]{2,1,0:T(8,128)}, f32[1,768,768]{2,1,0:T(8,128)}, f32[1024,768]{1,0:T(8,128)}, bf16[1024,768]{1,0:T(8,128)(2,1)}, f32[24,2304]{1,0:T(...) custom-call(bf16[1,768,768]{2,1,0:T(8,128)(2,1)} %get-tuple-element.37.refs_0_, ...), custom_call_target="tpu_custom_call" | custom-call | tf_op jit(solution)/shard_map/finish/pallas_call | solution.py:1086

commit v7 on v6

--- a/solution.py
+++ b/solution.py
@@ -343,7 +343,7 @@
     mrow[...] = jnp.transpose(misc[...].reshape(D, LANES).astype(f32))
     gain1 = mrow[GAIN1 : GAIN1 + 1, :]
     gain2 = mrow[GAIN2 : GAIN2 + 1, :]
-    pltpu.make_async_copy(mrow, mrow_out, out_sem.at[0]).start()
+    mrow_out[...] = mrow[LANES - 8 : LANES, :]
 
     def norm1b(i, _):
         rows = pl.ds(i * 128, 128)
@@ -579,8 +579,8 @@
     ret_w(NW - 1)
     grads(lambda at: xin[:, :, :, :, at].reshape(NW * c.R, QB), dpre, ug_out, True)
 
-    for q, ref in enumerate([mrow, lse, att, nrm, outp, normt]):
-        wait_bytes(ref, out_sem.at[q])
+    for q, ref in enumerate([lse, att, nrm, outp, normt]):
+        wait_bytes(ref, out_sem.at[q + 1])
     for q in range(2):
         wait_bytes(qkv.at[q], q_sem.at[q])
     for j in [J] + list(range(J)):
@@ -634,7 +634,7 @@
         (sds((T, D), bf16), any_),
         (sds((T, D), f32), any_),
         (sds((8, T), f32), vm),
-        (sds((LANES, D), f32), any_),
+        (sds((8, D), f32), vm),
         (sds((NW, SLOT, D), bf16), any_),
         (sds(rows_, bf16), any_),
         (sds((1, D, F), bf16), any_),
@@ -669,12 +669,12 @@
 
 
 def backward_kernel(c, *refs):
-    (v_hbm, dy_hbm, qkv_hbm, lse_hbm, att_hbm, resid_hbm, wt_hbm, nt_hbm, ret_hbm, outp_hbm, mrow, meta, cent, wq, mine) = refs[:15]
+    (v_hbm, dy_hbm, qkv_hbm, lse_hbm, att_hbm, resid_hbm, wt_hbm, nt_hbm, ret_hbm, outp_hbm, mrow, meta, cent, wq_hbm, mine) = refs[:15]
     (mixed_out, tok_out, qg_out, og_out, small_out) = refs[15:20]
     (v, dy, qkv, lse, att, resid, wt, ret, oh, normt, dbr, datt, dnm, dqkv, dk, dv, prod, rowbuf,
      part, lc, lx, got, mixed,
      gb, la, lb, lz, sgb, sla, slb, slz, lxx,
-     in_sem, q_sem, out_sem, os_, orv, ows, owr, rs_, rr, ps_, pr, tokacc) = refs[20:]
+     in_sem, q_sem, out_sem, os_, orv, ows, owr, rs_, rr, ps_, pr, tokacc, wq) = refs[20:]
     A, X, NW, NN, T, D, CW, G, J = c.A, c.X, c.NW, c.NN, c.T, c.D, c.CW, c.G, c.J
     H = J - G
     w, n, a, b, x, cc = place(c)
@@ -682,11 +682,11 @@
 
     loads = [
         (ret_hbm, ret), (resid_hbm, resid), (dy_hbm, dy), (att_hbm, att), (v_hbm, v), (lse_hbm, lse), (nt_hbm, normt),
-        (wt_hbm.at[pl.ds(G, H)], wt.at[pl.ds(G, H)]), (wt_hbm.at[pl.ds(0, G)], wt.at[pl.ds(0, G)]),
+        (wt_hbm.at[pl.ds(G, H)], wt.at[pl.ds(G, H)]), (wt_hbm.at[pl.ds(0, G)], wt.at[pl.ds(0, G)]), (wq_hbm, wq),
     ]
     for i, (s, d) in enumerate(loads):
         pltpu.make_async_copy(s, d, in_sem.at[i]).start()
-    own_part = pltpu.make_async_copy(outp_hbm.at[:, :, cc], part, in_sem.at[9])
+    own_part = pltpu.make_async_copy(outp_hbm.at[:, :, cc], part, in_sem.at[10])
     own_part.start()
 
     def load_wait(i):
@@ -701,7 +701,7 @@
     slot, gate = meta[0:1, :], meta[1:2, :]
     hits = lax.broadcasted_iota(jnp.int32, (c.S, T), 0).astype(f32) == slot
     oh[...] = hits.astype(bf16)
-    gain1, gain2 = mrow[GAIN1 : GAIN1 + 1, :], mrow[GAIN2 : GAIN2 + 1, :]
+    gain1, gain2 = mrow[6:7, :], mrow[7:8, :]
     load_wait(0)
     dnm[...] = mm(oh[...], ret[...].reshape(c.S, D), TN_)
     oh[...] = jnp.where(hits, gate, 0.0).astype(bf16)
@@ -978,6 +978,7 @@
         return 0
 
     lax.fori_loop(0, G, fin, 0)
+    load_wait(9)
     sums_ = jnp.sum(qg_out[...] * wq[...].astype(f32), 1, keepdims=True) / mine[:, GAIN1 : GAIN1 + 1]
     at_gain = lax.broadcasted_iota(jnp.int32, (c.slab, LANES), 1) == GAIN1
     small_out[...] = jnp.where(at_gain, sums_, rf(tiny, 0))
@@ -1029,16 +1030,16 @@
         V((T, D), bf16),
     ] + sums(J, CW) + sums(1, LANES) + [
         V((J, X, A, L, CW), bf16),
-        dma((10,)), dma((2, 2)), dma((2,)), dma((NW + 1,)), dma((NW + 1,)), dma((NW,)), dma((NW,)),
+        dma((11,)), dma((2, 2)), dma((2,)), dma((NW + 1,)), dma((NW + 1,)), dma((NW,)), dma((NW,)),
         dma((2, J + 1)), dma((2, J + 1)), dma((J + 1, 2 * X - 1)), dma((J + 1, 2 * X - 1)),
-        V((T, D), f32),
+        V((T, D), f32), V((L, 3 * D), bf16),
     ]
     return pl.pallas_call(
         functools.partial(backward_kernel, c),
         out_shape=(
             sds((T, D), bf16), sds((T, D), bf16), sds((L, 3 * D), f32), sds((L, D), f32), sds((L, LANES), f32),
         ),
-        in_specs=[any_] * 10 + [vm] * 5,
+        in_specs=[any_] * 10 + [vm] * 3 + [any_, vm],
         out_specs=(any_, any_, vm, vm, vm),
         scratch_shapes=scratch,
         compiler_params=pltpu.CompilerParams(

time: 162 us -> 161 us (level)
  no operation moved by 1% of the time
where the time goes in v7:
time: 161 us
  Pallas kernels  160 us (99%)
    pallas_call x1, Pallas kernels, forward_call(): pl.pallas_call(functools.partial(forward_kernel, c), out_shape=tuple((o[0...  95.4 us
    pallas_call x1, Pallas kernels, backward_call(): pl.pallas_call(functools.partial(backward_kernel, c), out_shape=(sds((T,...  58.3 us
    pallas_call x1, Pallas kernels, finish_call(): pl.pallas_call(functools.partial(finish_kernel, c), out_shape=tuple((sds(...  6.54 us

profile of v7, /device:TPU:0, one launch (start us, length us, event | category | flops | bytes accessed | tf_op | source)
XLA Modules:
  0.0 161.1 jit_solution(11845771056957486189)
XLA Ops:
  0.6 95.4 %forward.1 = (bf16[8,384,768]{2,1,0:T(8,128)(2,1)}, bf16[768,1024]{1,0:T(8,128)(2,1)}, bf16[6,1024,384]{2,1,0:T(8,128)(2,1)}, f32[6,8,1024]{2,1,0:T(8,128)}, bf1...) custom-call(bf16[1024,768]{1,0:T(8,128)(2,1)} %refs_0_.3, ...), custom_call_target="tpu_custom_call" | custom-call | tf_op jit(solution)/shard_map/forward/pallas_call | solution.py:658
  96.1 58.3 %backward.1 = (bf16[1024,768]{1,0:T(8,128)(2,1)}, bf16[1024,768]{1,0:T(8,128)(2,1)}, f32[24,2304]{1,0:T(8,128)}, f32[24,768]{1,0:T(8,128)}, f32[24,128]{1,0:T(8,128)}) custom-call(bf16[1024,768]{1,0:T(8,128)(2,1)} %refs_0_.3, bf16[1024,768]{1,0:T(8,128)(2,1)} %refs_1_.3, bf16[6,1024,384]{2,1,0:T(8,128)(2,1)} %get-tuple-element.39.refs_2_, ...), custom_call_target="tpu_custom_call" | custom-call | tf_op jit(solution)/shard_map/backward/pallas_call | solution.py:1037
  154.4 6.5 %finish.1 = (f32[1,768,768]{2,1,0:T(8,128)}, f32[1,768,768]{2,1,0:T(8,128)}, f32[1024,768]{1,0:T(8,128)}, bf16[1024,768]{1,0:T(8,128)(2,1)}, f32[24,2304]{1,0:T(...) custom-call(bf16[1,768,768]{2,1,0:T(8,128)(2,1)} %get-tuple-element.37.refs_0_, ...), custom_call_target="tpu_custom_call" | custom-call | tf_op jit(solution)/shard_map/finish/pallas_call | solution.py:1087
